TPU v7x, 256 devices: a whole 4x4x8 slice. The times are simulated.
256 devices in a mesh: obs: 4 (over x_lo, core), pan: 64 (over x_hi, y, z).
Axes of the slice: x: 4 (x_hi: 2, x_lo: 2; x = x_hi * 2 + x_lo), y: 4, z: 8, core: 2. Of those that a mesh axis runs over, the one named last changes fastest.
Arguments:
- sources: bfloat16 [64, 4, 2048, 256], P('pan', None, 'obs'), may hold values from -16 to 16
- panel_places: float32 [64, 3, 2048], P('pan', None, 'obs'), may hold values from -8 to 8
- observer_places: float32 [3, 1024], P(None, 'obs'), may hold values from 20 to 60
- fraction: bfloat16 [1024, 64, 2048], P(None, 'pan', 'obs'), may hold values from 0 to 1
- delay_bins: int32 [8, 64, 16], P(None, 'pan', 'obs'), may hold values from 0 to 127
- segment_owner: int32 [64], replicated, may hold values from 0 to 63, each once
Outputs:
- pressure: float32 [384, 1024], P('pan', 'obs')
Inputs may be any that keep to these rules, and one draw needn't show every extreme that they name: segment_owner is a permutation of the time segments' owners.
All inputs are finite; a program needn't handle non-finite values.
Results may differ from a plain program's by a relative error of at most 0.003.
Values may be sent and summed in bfloat16 or wider, within the bound.
A program may use at most 64 MiB of HBM per device.

v0:
```python
import math

import jax
import jax.numpy as jnp
from jax import lax
from jax.sharding import PartitionSpec as P

MAXD = 127
OBLK = 128
PBLK = 128


def block_kernel(place_block, observer_group, frac_group, amplitude):
    separation = observer_group[:, :, None] - place_block[:, None, :]
    dist_sq = jnp.sum(separation * separation, axis=0)
    monopole = amplitude / jnp.sqrt(dist_sq)
    dipole = amplitude * separation / dist_sq
    kernel = jnp.concatenate([monopole[None], dipole], axis=0)
    weight = frac_group.astype(jnp.float32)
    lower_part = (kernel * (1.0 - weight)).astype(jnp.bfloat16)
    upper_part = (kernel * weight).astype(jnp.bfloat16)
    return jnp.stack([lower_part, upper_part], axis=0)


def add_block(totals, src_block, weights, shift_group, first_obs, per_group):
    products = jnp.einsum("cjs,gcoj->sgo", src_block, weights, preferred_element_type=jnp.float32)
    placed = jnp.pad(products[:, 0], ((0, 1), (0, 0))) + jnp.pad(products[:, 1], ((1, 0), (0, 0)))
    span = placed.shape[0]
    for member in range(per_group):
        row_start = shift_group[member]
        column = (first_obs + member * OBLK).astype(jnp.int32)
        current = lax.dynamic_slice(totals, (row_start, column), (span, OBLK))
        fresh = current + placed[:, member * OBLK : (member + 1) * OBLK]
        totals = lax.dynamic_update_slice(totals, fresh, (row_start, column))
    return totals


def sweep(totals, src_block, place_block, observer_all, frac_cols, shifts, amplitude):
    block_total = observer_all.shape[1] // OBLK
    per_group = max([d for d in range(1, 9) if block_total % d == 0])
    group_width = per_group * OBLK

    def group(group_index, totals):
        first_obs = group_index * group_width
        weights = block_kernel(place_block, observer_all, frac_cols, amplitude)
        return add_block(totals, src_block, weights, shifts, first_obs, per_group)

    return lax.fori_loop(0, block_total // per_group, group, totals)


def reorder(totals, segment_owner):
    segment_count = segment_owner.shape[0]
    arranged = totals.reshape(segment_count, totals.shape[0] // segment_count, totals.shape[1])
    inverse = jnp.argsort(segment_owner)
    return arranged[inverse].reshape(totals.shape)


def per_device(sources, panel_places, observer_places, fraction, delay_bins, segment_owner):
    local_panels = sources.shape[2]
    window = sources.shape[3]
    bins_total = window + MAXD + 1
    amplitude = 60.0 / math.sqrt(local_panels * lax.axis_size("obs") * lax.axis_size("pan"))
    local_blocks = local_panels // PBLK
    every_obs = lax.all_gather(observer_places, "obs", axis=1, tiled=True)
    totals = jnp.zeros((bins_total, every_obs.shape[1]), jnp.float32)
    for block_index in range(local_blocks):
        lo_col = block_index * PBLK
        src_block = sources[0, :, lo_col : lo_col + PBLK]
        place_block = panel_places[0, :, lo_col : lo_col + PBLK]
        frac_cols = fraction[:, 0, lo_col : lo_col + PBLK]
        shifts = delay_bins[:, 0, block_index]
        totals = sweep(totals, src_block, place_block, every_obs, frac_cols, shifts, amplitude)
    arranged = reorder(totals, segment_owner)
    reduced = lax.psum_scatter(arranged, "pan", scatter_dimension=0, tiled=True)
    result = lax.psum_scatter(reduced, "obs", scatter_dimension=1, tiled=True)
    return result


def solution(mesh):
    return jax.shard_map(
        per_device,
        mesh=mesh,
        in_specs=(
            P("pan", None, "obs", None),
            P("pan", None, "obs"),
            P(None, "obs"),
            P(None, "pan", "obs"),
            P(None, "pan", "obs"),
            P(),
        ),
        out_specs=P("pan", "obs"),
        check_vma=False,
    )
```

profile of v0, /device:TPU:24, one launch (start us, length us, event | category | flops | bytes accessed | tf_op | source)
XLA Modules:
  0.0 509.6 jit_solution(10461130379982518106)
XLA Ops:
  6.5 2.5 broadcast_subtract_fusion
  41.5 5.2 %all_gather.3 = f32[3,1024]{1,0:T(4,128)S(1)} all-gather(f32[3,256]{1,0:T(4,128)S(1)} %copy-done.10), channel_id=1, replica_groups=mesh['obs'=4,'pan'=64] {'obs'}, dimensions={1}, use_global_device_ids=true | all-gather | bytes 15360 | tf_op jit(solution)/shard_map/all_gather | solution.py:64
  48.8 2.6 fusion.40
  62.6 1.6 multiply_convert_fusion.5
  71.5 1.9 dynamic_update_slice.128
  74.5 3.0 dynamic_update_slice.129
  79.1 3.1 dynamic_update_slice.130
  83.8 3.0 dynamic_update_slice.131
  88.5 3.0 dynamic_update_slice.132
  93.2 3.0 dynamic_update_slice.133
  97.8 3.0 dynamic_update_slice.134
  102.5 2.5 dynamic_update_slice.135
  106.7 3.1 dynamic_update_slice.136
  111.4 3.1 dynamic_update_slice.137
  116.2 3.0 dynamic_update_slice.138
  120.8 3.0 dynamic_update_slice.139
  125.4 3.1 dynamic_update_slice.140
  130.1 3.0 dynamic_update_slice.141
  134.7 3.1 dynamic_update_slice.142
  139.3 2.5 dynamic_update_slice.143
  141.9 1.9 multiply_convert_fusion.3
  143.8 1.7 fusion.20
  147.3 3.2 dynamic_update_slice.144
  152.0 3.1 dynamic_update_slice.145
  156.7 3.2 dynamic_update_slice.146
  161.5 3.2 dynamic_update_slice.147
  166.2 3.0 dynamic_update_slice.148
  170.9 3.0 dynamic_update_slice.149
  175.5 3.2 dynamic_update_slice.150
  180.3 2.3 dynamic_update_slice.151
  182.6 1.9 multiply_convert_fusion.1
  184.4 1.7 fusion.17
  188.0 3.0 dynamic_update_slice.152
  192.6 3.1 dynamic_update_slice.153
  197.4 3.0 dynamic_update_slice.154
  201.9 2.0 dynamic_update_slice.155
  205.6 3.0 dynamic_update_slice.156
  210.1 3.1 dynamic_update_slice.157
  214.8 3.1 dynamic_update_slice.158
  219.5 2.5 dynamic_update_slice.159
  223.6 2.0 sort.17
  225.6 2.0 gather_fusion
  227.7 1.6 reshape.376
  229.3 173.6 %fusion = f32[8,1024]{1,0:T(8,128)S(1)} fusion(f32[384,1024]{1,0:T(8,128)S(1)} %reshape.376), kind=kCustom, calls=%all-reduce-scatter | all-reduce-scatter fusion | flops 524289 | bytes 1606656
  403.0 7.3 %collective-permute-start.15 = (f32[6,1024]{1,0:T(8,128)S(1)}, f32[6,1024]{1,0:T(8,128)S(1)}, u32[]{:S(2)}, u32[]{:S(2)}) collective-permute-start(f32[6,1024]{1,0:T(8,128)S(1)} %slice.542), channel_id=1, source_target_pairs={{0,16},{1,17},{2,18},{3,19},{4,20},{5,21},{6,22},{7,23},{8,24},{9,... | collective-permute-start | bytes 73736
  410.2 1.9 collective-permute-start
  412.2 7.0 %collective-permute-start.1 = (f32[8,1024]{1,0:T(8,128)S(1)}, f32[8,1024]{1,0:T(8,128)S(1)}, u32[]{:S(2)}, u32[]{:S(2)}) collective-permute-start(f32[8,1024]{1,0:T(8,128)S(1)} %fusion), channel_id=1, source_target_pairs={{0,2},{1,3},{2,4},{3,5},{4,6},{5,7},{6,8},{7,9},{8,10},{9,11},{10,... | collective-permute-start | bytes 98312
  419.2 9.8 %collective-permute-start.10 = (f32[8,1024]{1,0:T(8,128)S(1)}, f32[8,1024]{1,0:T(8,128)S(1)}, u32[]{:S(2)}, u32[]{:S(2)}) collective-permute-start(f32[8,1024]{1,0:T(8,128)S(1)} %fusion), channel_id=1, source_target_pairs={{0,11},{1,12},{2,13},{3,14},{4,15},{5,16},{6,17},{7,18},{8,19},{9,... | collective-permute-start | bytes 98312
  429.0 13.9 %collective-permute-start.11 = (f32[8,1024]{1,0:T(8,128)S(1)}, f32[8,1024]{1,0:T(8,128)S(1)}, u32[]{:S(2)}, u32[]{:S(2)}) collective-permute-start(f32[8,1024]{1,0:T(8,128)S(1)} %fusion), channel_id=1, source_target_pairs={{0,12},{1,13},{2,14},{3,15},{4,16},{5,17},{6,18},{7,19},{8,20},{9,... | collective-permute-start | bytes 98312
  443.0 6.9 %collective-permute-start.12 = (f32[8,1024]{1,0:T(8,128)S(1)}, f32[8,1024]{1,0:T(8,128)S(1)}, u32[]{:S(2)}, u32[]{:S(2)}) collective-permute-start(f32[8,1024]{1,0:T(8,128)S(1)} %fusion), channel_id=1, source_target_pairs={{0,13},{1,14},{2,15},{3,16},{4,17},{5,18},{6,19},{7,20},{8,21},{9,... | collective-permute-start | bytes 98312
  449.9 1.9 collective-permute-start.13
  451.8 1.9 collective-permute-start.14
  453.8 1.9 collective-permute-start.2
  455.7 1.9 collective-permute-start.3
  457.6 7.4 %collective-permute-start.4 = (f32[8,1024]{1,0:T(8,128)S(1)}, f32[8,1024]{1,0:T(8,128)S(1)}, u32[]{:S(2)}, u32[]{:S(2)}) collective-permute-start(f32[8,1024]{1,0:T(8,128)S(1)} %fusion), channel_id=1, source_target_pairs={{0,5},{1,6},{2,7},{3,8},{4,9},{5,10},{6,11},{7,12},{8,13},{9,14},{... | collective-permute-start | bytes 98312
  465.1 1.9 collective-permute-start.5
  467.0 1.9 collective-permute-start.6
  468.9 1.9 collective-permute-start.7
  470.9 2.0 collective-permute-start.8
  472.9 2.3 collective-permute-start.9
  476.5 3.8 collective-permute-done.8
  480.3 3.1 collective-permute-done.9
  483.4 1.7 concatenate.100
  485.8 17.0 %reduce-scatter.4.cloned.1.call-done = f32[6,256]{1,0:T(8,128)} async-done(((f32[6,1024]{1,0:T(8,128)}), f32[6,256]{1,0:T(8,128)}) %reduce-scatter.4.cloned.1.call-update) | async-done | bytes 6160 | tf_op jit(solution)/shard_map/reduce_scatter | solution.py:75
  (102 shorter events, 45.2 us)
Async XLA Ops:
  6.5 2.5 copy-start.2
  6.5 496.2 %reduce-scatter.4.cloned.1.call-start = ((), (), s32[]{:S(2)}) async-start(), calls=%async_computation.1 | async-start | bytes 40960 | tf_op jit(solution)/shard_map/reduce_scatter | solution.py:75
  9.0 1.4 copy-start.8
  9.0 32.5 %copy-start.9 = (f32[1,3,512]{2,0,1:T(1,128)S(1)}, f32[1,3,512]{2,0,1:T(1,128)}, u32[]{:S(2)}) copy-start(f32[1,3,512]{2,0,1:T(1,128)} %param.7) | copy-start | bytes 18436
  9.0 32.5 %copy-start.10 = (f32[3,256]{1,0:T(4,128)S(1)}, f32[3,256]{1,0:T(4,128)}, u32[]{:S(2)}) copy-start(f32[3,256]{1,0:T(4,128)} %param.8) | copy-start | bytes 9220
  62.6 1.6 copy-start.12
  65.0 1.4 copy-start.1
  65.0 1.5 copy-start.7
  67.9 1.0 copy-start
  134.7 7.2 %copy-start.4 = (f32[1,1,1024,128]{3,2,1,0:T(8,128)S(1)}, f32[1,1,1024,128]{3,2,1,0:T(8,128)}, u32[]{:S(2)}) copy-start(f32[1,1,1024,128]{3,2,1,0:T(8,128)} %multiply_bitcast_fusion.1) | copy-start | bytes 1572868
  134.7 7.2 %copy-start.6 = (f32[1024,128]{1,0:T(8,128)S(1)}, f32[1024,128]{1,0:T(8,128)}, u32[]{:S(2)}) copy-start(f32[1024,128]{1,0:T(8,128)} %get-tuple-element.114) | copy-start | bytes 1572868
  175.5 7.1 %copy-start.3 = (f32[1,1,1024,128]{3,2,1,0:T(8,128)S(1)}, f32[1,1,1024,128]{3,2,1,0:T(8,128)}, u32[]{:S(2)}) copy-start(f32[1,1,1024,128]{3,2,1,0:T(8,128)} %multiply_bitcast_fusion) | copy-start | bytes 1572868
  175.5 7.1 %copy-start.5 = (f32[1024,128]{1,0:T(8,128)S(1)}, f32[1024,128]{1,0:T(8,128)}, u32[]{:S(2)}) copy-start(f32[1024,128]{1,0:T(8,128)} %get-tuple-element.113) | copy-start | bytes 1572868
  222.1 1.5 copy-start.13
  229.3 245.9 %copy-start.11 = (u32[256]{0:T(256)S(1)}, u32[256]{0:T(256)}, u32[]{:S(2)}) copy-start(u32[256]{0:T(256)} %constant.159) | copy-start | bytes 3076
  403.0 40.0 %collective-permute-start.15 = (f32[6,1024]{1,0:T(8,128)S(1)}, f32[6,1024]{1,0:T(8,128)S(1)}, u32[]{:S(2)}, u32[]{:S(2)}) collective-permute-start(f32[6,1024]{1,0:T(8,128)S(1)} %slice.542), channel_id=1, source_target_pairs={{0,16},{1,17},{2,18},{3,19},{4,20},{5,21},{6,22},{7,23},{8,24},{9,... | collective-permute-start | bytes 73736
  410.2 39.6 %collective-permute-start = (f32[8,1024]{1,0:T(8,128)S(1)}, f32[8,1024]{1,0:T(8,128)S(1)}, u32[]{:S(2)}, u32[]{:S(2)}) collective-permute-start(f32[8,1024]{1,0:T(8,128)S(1)} %fusion), channel_id=1, source_target_pairs={{0,1},{1,2},{2,3},{3,4},{4,5},{5,6},{6,7},{7,8},{8,9},{9,10},{10,1... | collective-permute-start | bytes 98312
  412.2 39.6 %collective-permute-start.1 = (f32[8,1024]{1,0:T(8,128)S(1)}, f32[8,1024]{1,0:T(8,128)S(1)}, u32[]{:S(2)}, u32[]{:S(2)}) collective-permute-start(f32[8,1024]{1,0:T(8,128)S(1)} %fusion), channel_id=1, source_target_pairs={{0,2},{1,3},{2,4},{3,5},{4,6},{5,7},{6,8},{7,9},{8,10},{9,11},{10,... | collective-permute-start | bytes 98312
  419.2 34.5 %collective-permute-start.10 = (f32[8,1024]{1,0:T(8,128)S(1)}, f32[8,1024]{1,0:T(8,128)S(1)}, u32[]{:S(2)}, u32[]{:S(2)}) collective-permute-start(f32[8,1024]{1,0:T(8,128)S(1)} %fusion), channel_id=1, source_target_pairs={{0,11},{1,12},{2,13},{3,14},{4,15},{5,16},{6,17},{7,18},{8,19},{9,... | collective-permute-start | bytes 98312
  429.0 26.7 %collective-permute-start.11 = (f32[8,1024]{1,0:T(8,128)S(1)}, f32[8,1024]{1,0:T(8,128)S(1)}, u32[]{:S(2)}, u32[]{:S(2)}) collective-permute-start(f32[8,1024]{1,0:T(8,128)S(1)} %fusion), channel_id=1, source_target_pairs={{0,12},{1,13},{2,14},{3,15},{4,16},{5,17},{6,18},{7,19},{8,20},{9,... | collective-permute-start | bytes 98312
  443.0 14.7 %collective-permute-start.12 = (f32[8,1024]{1,0:T(8,128)S(1)}, f32[8,1024]{1,0:T(8,128)S(1)}, u32[]{:S(2)}, u32[]{:S(2)}) collective-permute-start(f32[8,1024]{1,0:T(8,128)S(1)} %fusion), channel_id=1, source_target_pairs={{0,13},{1,14},{2,15},{3,16},{4,17},{5,18},{6,19},{7,20},{8,21},{9,... | collective-permute-start | bytes 98312
  449.9 15.2 %collective-permute-start.13 = (f32[8,1024]{1,0:T(8,128)S(1)}, f32[8,1024]{1,0:T(8,128)S(1)}, u32[]{:S(2)}, u32[]{:S(2)}) collective-permute-start(f32[8,1024]{1,0:T(8,128)S(1)} %fusion), channel_id=1, source_target_pairs={{0,14},{1,15},{2,16},{3,17},{4,18},{5,19},{6,20},{7,21},{8,22},{9,... | collective-permute-start | bytes 98312
  451.8 15.2 %collective-permute-start.14 = (f32[8,1024]{1,0:T(8,128)S(1)}, f32[8,1024]{1,0:T(8,128)S(1)}, u32[]{:S(2)}, u32[]{:S(2)}) collective-permute-start(f32[8,1024]{1,0:T(8,128)S(1)} %fusion), channel_id=1, source_target_pairs={{0,15},{1,16},{2,17},{3,18},{4,19},{5,20},{6,21},{7,22},{8,23},{9,... | collective-permute-start | bytes 98312
  453.8 15.2 %collective-permute-start.2 = (f32[8,1024]{1,0:T(8,128)S(1)}, f32[8,1024]{1,0:T(8,128)S(1)}, u32[]{:S(2)}, u32[]{:S(2)}) collective-permute-start(f32[8,1024]{1,0:T(8,128)S(1)} %fusion), channel_id=1, source_target_pairs={{0,3},{1,4},{2,5},{3,6},{4,7},{5,8},{6,9},{7,10},{8,11},{9,12},{10... | collective-permute-start | bytes 98312
  455.7 15.2 %collective-permute-start.3 = (f32[8,1024]{1,0:T(8,128)S(1)}, f32[8,1024]{1,0:T(8,128)S(1)}, u32[]{:S(2)}, u32[]{:S(2)}) collective-permute-start(f32[8,1024]{1,0:T(8,128)S(1)} %fusion), channel_id=1, source_target_pairs={{0,4},{1,5},{2,6},{3,7},{4,8},{5,9},{6,10},{7,11},{8,12},{9,13},{1... | collective-permute-start | bytes 98312
  457.6 15.2 %collective-permute-start.4 = (f32[8,1024]{1,0:T(8,128)S(1)}, f32[8,1024]{1,0:T(8,128)S(1)}, u32[]{:S(2)}, u32[]{:S(2)}) collective-permute-start(f32[8,1024]{1,0:T(8,128)S(1)} %fusion), channel_id=1, source_target_pairs={{0,5},{1,6},{2,7},{3,8},{4,9},{5,10},{6,11},{7,12},{8,13},{9,14},{... | collective-permute-start | bytes 98312
  465.1 11.4 %collective-permute-start.5 = (f32[8,1024]{1,0:T(8,128)S(1)}, f32[8,1024]{1,0:T(8,128)S(1)}, u32[]{:S(2)}, u32[]{:S(2)}) collective-permute-start(f32[8,1024]{1,0:T(8,128)S(1)} %fusion), channel_id=1, source_target_pairs={{0,6},{1,7},{2,8},{3,9},{4,10},{5,11},{6,12},{7,13},{8,14},{9,15},... | collective-permute-start | bytes 98312
  467.0 9.5 %collective-permute-start.6 = (f32[8,1024]{1,0:T(8,128)S(1)}, f32[8,1024]{1,0:T(8,128)S(1)}, u32[]{:S(2)}, u32[]{:S(2)}) collective-permute-start(f32[8,1024]{1,0:T(8,128)S(1)} %fusion), channel_id=1, source_target_pairs={{0,7},{1,8},{2,9},{3,10},{4,11},{5,12},{6,13},{7,14},{8,15},{9,16}... | collective-permute-start | bytes 98312
  468.9 7.6 %collective-permute-start.7 = (f32[8,1024]{1,0:T(8,128)S(1)}, f32[8,1024]{1,0:T(8,128)S(1)}, u32[]{:S(2)}, u32[]{:S(2)}) collective-permute-start(f32[8,1024]{1,0:T(8,128)S(1)} %fusion), channel_id=1, source_target_pairs={{0,8},{1,9},{2,10},{3,11},{4,12},{5,13},{6,14},{7,15},{8,16},{9,17... | collective-permute-start | bytes 98312
  470.9 9.4 %collective-permute-start.8 = (f32[8,1024]{1,0:T(8,128)S(1)}, f32[8,1024]{1,0:T(8,128)S(1)}, u32[]{:S(2)}, u32[]{:S(2)}) collective-permute-start(f32[8,1024]{1,0:T(8,128)S(1)} %fusion), channel_id=1, source_target_pairs={{0,9},{1,10},{2,11},{3,12},{4,13},{5,14},{6,15},{7,16},{8,17},{9,1... | collective-permute-start | bytes 98312
  472.9 10.5 %collective-permute-start.9 = (f32[8,1024]{1,0:T(8,128)S(1)}, f32[8,1024]{1,0:T(8,128)S(1)}, u32[]{:S(2)}, u32[]{:S(2)}) collective-permute-start(f32[8,1024]{1,0:T(8,128)S(1)} %fusion), channel_id=1, source_target_pairs={{0,10},{1,11},{2,12},{3,13},{4,14},{5,15},{6,16},{7,17},{8,18},{9,... | collective-permute-start | bytes 98312
Sparse Core Ops, SparseCore 0:
  485.9 16.8 reduce-scatter.3
where the time goes:
time: 518 us; the launch traced here: 510 us
  blocking collectives  179 us (35%)
  local copies, waits for them, and re-layouts  108 us (21%)
  between operations  74.7 us (14%)
  starting transfers between devices  72 us (14%)
  other arithmetic  47.4 us (9%)
  waiting for transfers between devices  23.9 us (5%)
    unnamed x1, blocking collectives  174 us
    dynamic_update_slice x32, local copies, waits for them, and re-layouts, add_block(): totals = lax.dynamic_update_slice(totals, fresh, (row_start, column))  93.7 us
    unnamed x16, starting transfers between devices  72 us
    add x31, other arithmetic, add_block(): fresh = current + placed[:, member * OBLK:(member + 1) * OBLK]  30.1 us
    reduce_scatter x1, waiting for transfers between devices, per_device(): result = lax.psum_scatter(reduced, 'obs', scatter_dimension=1, tiled=True)  17 us
  transfers between devices with their start and end apart: 17, of which 3 were waited for; matrix products, arithmetic and copies ran while one was open for 0% of the time, Pallas kernels for 0%

commit v1 on v0

v1 whole, which is shorter than its diff:
```python
import math

import jax
import jax.numpy as jnp
from jax import lax
from jax.sharding import PartitionSpec as P

MAXD = 127
OBLK = 128
PBLK = 128


def block_kernel(place_block, observer_group, frac_group, amplitude):
    separation = observer_group[:, :, None] - place_block[:, None, :]
    dist_sq = jnp.sum(separation * separation, axis=0)
    monopole = amplitude / jnp.sqrt(dist_sq)
    dipole = amplitude * separation / dist_sq
    kernel = jnp.concatenate([monopole[None], dipole], axis=0)
    weight = frac_group.astype(jnp.float32)
    lower_part = (kernel * (1.0 - weight)).astype(jnp.bfloat16)
    upper_part = (kernel * weight).astype(jnp.bfloat16)
    return jnp.stack([lower_part, upper_part], axis=0)


def placed_block(src_block, weights):
    products = jnp.einsum("cjs,gcoj->sgo", src_block, weights, preferred_element_type=jnp.float32)
    return jnp.pad(products[:, 0], ((0, 1), (0, 0))) + jnp.pad(products[:, 1], ((1, 0), (0, 0)))


def per_device(sources, panel_places, observer_places, fraction, delay_bins, segment_owner):
    local_panels = sources.shape[2]
    window = sources.shape[3]
    bins_total = window + MAXD + 1
    amplitude = 60.0 / math.sqrt(local_panels * lax.axis_size("obs") * lax.axis_size("pan"))
    local_blocks = local_panels // PBLK
    every_obs = lax.all_gather(observer_places, "obs", axis=1, tiled=True)
    obs_total = every_obs.shape[1]
    obs_blocks = obs_total // OBLK
    span = window + 1
    lead = MAXD
    padded_rows = lead + span + (bins_total - span)
    columns = [None] * obs_blocks
    for block_index in range(local_blocks):
        lo_col = block_index * PBLK
        src_block = sources[0, :, lo_col : lo_col + PBLK]
        place_block = panel_places[0, :, lo_col : lo_col + PBLK]
        frac_cols = fraction[:, 0, lo_col : lo_col + PBLK]
        weights = block_kernel(place_block, every_obs, frac_cols, amplitude)
        placed = placed_block(src_block, weights)
        padded = jnp.pad(placed, ((lead, padded_rows - lead - span), (0, 0)))
        for ob in range(obs_blocks):
            shift = delay_bins[ob, 0, block_index]
            piece = lax.dynamic_slice(padded, (lead - shift, ob * OBLK), (bins_total, OBLK))
            columns[ob] = piece if columns[ob] is None else columns[ob] + piece
    totals = jnp.concatenate(columns, axis=1)
    reduced = lax.psum_scatter(totals, "obs", scatter_dimension=1, tiled=True)
    segment_count = segment_owner.shape[0]
    seg_len = bins_total // segment_count
    arranged = reduced.reshape(segment_count, seg_len, reduced.shape[1])
    inverse = jnp.argsort(segment_owner)
    arranged = arranged[inverse]
    rows = -(-seg_len // 8) * 8
    flat = jnp.pad(arranged, ((0, 0), (0, rows - seg_len), (0, 0)))
    result = lax.psum_scatter(flat, "pan", scatter_dimension=0, tiled=True)
    return result[0, :seg_len]


def solution(mesh):
    return jax.shard_map(
        per_device,
        mesh=mesh,
        in_specs=(
            P("pan", None, "obs", None),
            P("pan", None, "obs"),
            P(None, "obs"),
            P(None, "pan", "obs"),
            P(None, "pan", "obs"),
            P(),
        ),
        out_specs=P("pan", "obs"),
        check_vma=False,
    )
```

time: 518 us -> 491 us (0.948)
  the two profiles are of different devices: /device:TPU:24 before, /device:TPU:6 now
where the time goes in v1:
time: 491 us; the launch traced here: 490 us
  waiting for transfers between devices  394 us (80%)
  between operations  53.6 us (11%)
  other arithmetic  18.4 us (4%)
  local copies, waits for them, and re-layouts  16.2 us (3%)
  blocking collectives  5.2 us (1%)
    reduce_scatter x1, waiting for transfers between devices, per_device(): result = lax.psum_scatter(flat, 'pan', scatter_dimension=0, tiled=True)  368 us
    reduce_scatter x1, waiting for transfers between devices, per_device(): reduced = lax.psum_scatter(totals, 'obs', scatter_dimension=1, tiled=True)  26.2 us
  transfers between devices with their start and end apart: 2, of which 2 were waited for; matrix products, arithmetic and copies ran while one was open for 0% of the time, Pallas kernels for 0%

profile of v1, /device:TPU:6, one launch (start us, length us, event | category | flops | bytes accessed | tf_op | source)
XLA Modules:
  0.0 490.3 jit_solution(12725346106405002344)
XLA Ops:
  6.5 0.0 copy-start.1
  6.5 0.0 reduce-scatter.3.cloned.1.call-start
  6.5 1.4 broadcast_subtract_fusion
  8.0 0.1 copy-done.1
  8.1 0.0 copy-start.9
  8.1 0.0 copy-start.10
  8.1 0.1 bitcast_convert_fusion
  8.3 0.5 copy-done.9
  8.8 0.0 copy-done.10
  8.8 5.2 %all_gather.3 = f32[3,1024]{1,0:T(4,128)S(1)} all-gather(f32[3,256]{1,0:T(4,128)S(1)} %copy-done.10), channel_id=1, replica_groups=mesh['obs'=4,'pan'=64] {'obs'}, dimensions={1}, use_global_device_ids=true | all-gather | bytes 15360 | tf_op jit(solution)/shard_map/all_gather | solution.py:36
  14.0 0.9 fusion.37
  15.0 0.1 multiply_bitcast_fusion
  15.1 0.1 multiply_bitcast_fusion.1
  15.1 0.1 multiply_bitcast_fusion.2
  15.2 0.0 copy-start.8
  15.2 1.0 fusion.39
  16.3 0.1 multiply_bitcast_fusion.3
  16.3 0.0 copy-done.8
  16.4 0.7 fusion.86
  31.9 0.7 fusion.85
  57.8 0.0 copy-start.11
  57.8 0.3 multiply_convert_fusion.1
  58.2 0.9 copy-done.11
  59.0 0.8 fusion.16
  59.8 0.2 slice_bitcast_fusion.1
  60.0 0.4 multiply_convert_fusion.3
  60.4 0.8 fusion.19
  61.2 1.6 slice_bitcast_fusion.3
  62.7 0.3 multiply_convert_fusion.5
  63.1 0.8 fusion.22
  63.8 1.6 slice_bitcast_fusion.5
  65.4 0.3 multiply_convert_fusion.7
  65.8 0.8 fusion.25
  66.5 1.5 slice_bitcast_fusion.7
  68.0 0.2 pad_add_fusion
  68.3 1.0 copy-done.2
  69.2 0.3 copy-done.3
  69.5 0.2 pad_add_fusion.1
  69.7 1.0 copy-done.4
  70.8 0.3 copy-done.5
  71.1 0.2 pad_add_fusion.2
  71.3 1.0 copy-done.6
  72.3 0.3 copy-done.7
  72.6 1.2 pad_add_fusion.3
  73.8 2.0 fusion.51
  75.9 0.0 copy-done
  75.9 1.0 fusion.55
  76.9 1.0 fusion.59
  77.9 1.0 fusion.63
  78.9 1.0 fusion.67
  80.0 1.0 fusion.71
  81.0 1.1 fusion.75
  82.1 1.0 fusion.79
  83.1 0.0 reduce-scatter.3.cloned.1.call-update
  83.1 0.0 reduce-scatter.5.cloned.1.call-start
  83.2 0.6 copy-done.12
  83.8 2.0 sort.17
  85.8 26.2 %reduce-scatter.3.cloned.1.call-done = f32[384,256]{1,0:T(8,128)} async-done(((f32[384,1024]{1,0:T(8,128)}), f32[384,256]{1,0:T(8,128)}) %reduce-scatter.3.cloned.1.call-update) | async-done | bytes 393232 | tf_op jit(solution)/shard_map/reduce_scatter | solution.py:56
  112.0 1.0 reshape.436
  113.0 0.6 gather_fusion
  113.7 0.8 pad.55
  114.5 0.0 reduce-scatter.5.cloned.1.call-update
  114.5 367.6 %reduce-scatter.5.cloned.1.call-done = f32[1,8,256]{2,1,0:T(8,128)} async-done(((f32[64,8,256]{2,1,0:T(8,128)}), f32[1,8,256]{2,1,0:T(8,128)}) %reduce-scatter.5.cloned.1.call-update) | async-done | bytes 8208 | tf_op jit(solution)/shard_map/reduce_scatter | solution.py:64
  482.1 1.3 slice_bitcast_fusion.8
  (14 shorter events, 0.0 us)
Async XLA Ops:
  6.5 1.6 copy-start.1
  6.5 105.4 %reduce-scatter.3.cloned.1.call-start = ((), (), s32[]{:S(2)}) async-start(), calls=%async_computation.2 | async-start | bytes 1966080 | tf_op jit(solution)/shard_map/reduce_scatter | solution.py:56
  8.1 0.7 copy-start.9
  8.1 0.7 copy-start.10
  15.2 1.1 copy-start.8
  57.8 1.2 copy-start.11
  68.0 1.2 copy-start.2
  68.0 1.5 copy-start.3
  69.5 1.2 copy-start.4
  69.5 1.5 copy-start.5
  71.1 1.2 copy-start.6
  71.1 1.5 copy-start.7
  73.8 2.0 copy-start
  83.1 0.7 copy-start.12
  83.1 399.0 %reduce-scatter.5.cloned.1.call-start = ((), (), s32[]{:S(2)}) async-start(), calls=%async_computation.3 | async-start | bytes 532480 | tf_op jit(solution)/shard_map/reduce_scatter | solution.py:64
Sparse Core Ops, SparseCore 0:
  83.3 28.6 reduce-scatter.2
  114.7 367.4 reduce-scatter.4

commit v2 on v1

--- a/solution.py
+++ b/solution.py
@@ -59,10 +59,26 @@
     arranged = reduced.reshape(segment_count, seg_len, reduced.shape[1])
     inverse = jnp.argsort(segment_owner)
     arranged = arranged[inverse]
-    rows = -(-seg_len // 8) * 8
-    flat = jnp.pad(arranged, ((0, 0), (0, rows - seg_len), (0, 0)))
-    result = lax.psum_scatter(flat, "pan", scatter_dimension=0, tiled=True)
-    return result[0, :seg_len]
+    return halving_sum(arranged, "pan", (0, 3, 1, 4, 2, 5))
+
+
+def halving_sum(data, axis, bit_order):
+    count = data.shape[0]
+    levels = count.bit_length() - 1
+    me = lax.axis_index(axis)
+    data = data.reshape((2,) * levels + data.shape[1:])
+    remaining = list(range(levels - 1, -1, -1))
+    for bit in bit_order:
+        dim = remaining.index(bit)
+        mine = (me >> bit) & 1
+        low = lax.index_in_dim(data, 0, dim, keepdims=False)
+        high = lax.index_in_dim(data, 1, dim, keepdims=False)
+        keep = jnp.where(mine == 1, high, low)
+        send = jnp.where(mine == 1, low, high)
+        pairs = [(p, p ^ (1 << bit)) for p in range(count)]
+        data = keep + lax.ppermute(send, axis, pairs)
+        remaining.pop(dim)
+    return data
 
 
 def solution(mesh):

time: 491 us -> 160 us (0.33)
  the two profiles are of different devices: /device:TPU:6 before, /device:TPU:24 now
where the time goes in v2:
time: 160 us; the launch traced here: 159 us
  between operations  54 us (34%)
  waiting for transfers between devices  46.3 us (29%)
  other arithmetic  19.8 us (12%)
  starting transfers between devices  16 us (10%)
  local copies, waits for them, and re-layouts  14.4 us (9%)
  blocking collectives  5.2 us (3%)
  matrix products  3.01 us (2%)
    reduce_scatter x1, waiting for transfers between devices, per_device(): reduced = lax.psum_scatter(totals, 'obs', scatter_dimension=1, tiled=True)  26.6 us
    ppermute x6, waiting for transfers between devices, halving_sum(): data = keep + lax.ppermute(send, axis, pairs)  19.7 us
    ppermute x6, starting transfers between devices, halving_sum(): data = keep + lax.ppermute(send, axis, pairs)  16 us
    unnamed x7, other arithmetic  8.21 us
    unnamed x32, local copies, waits for them, and re-layouts  6.32 us
    all_gather x1, blocking collectives, per_device(): every_obs = lax.all_gather(observer_places, 'obs', axis=1, tiled=True)  5.2 us
    squeeze x4, local copies, waits for them, and re-layouts, placed_block(): products[:, 0]  4.88 us
  transfers between devices with their start and end apart: 7, of which 7 were waited for; matrix products, arithmetic and copies ran while one was open for 1% of the time, Pallas kernels for 0%

profile of v2, /device:TPU:24, one launch (start us, length us, event | category | flops | bytes accessed | tf_op | source)
XLA Modules:
  0.0 158.6 jit_solution(11911982236685478341)
XLA Ops:
  6.5 1.4 broadcast_subtract_fusion
  8.0 0.1 copy-done.1
  8.1 0.1 bitcast_convert_fusion
  8.3 0.5 copy-done.9
  8.8 5.2 %all_gather.3 = f32[3,1024]{1,0:T(4,128)S(1)} all-gather(f32[3,256]{1,0:T(4,128)S(1)} %copy-done.10), channel_id=1, replica_groups=mesh['obs'=4,'pan'=64] {'obs'}, dimensions={1}, use_global_device_ids=true | all-gather | bytes 15360 | tf_op jit(solution)/shard_map/all_gather | solution.py:36
  14.0 0.9 fusion.37
  15.0 0.1 multiply_bitcast_fusion
  15.1 0.1 multiply_bitcast_fusion.1
  15.2 1.0 fusion.39
  16.4 0.7 fusion.104
  32.3 0.7 fusion.103
  58.1 0.3 multiply_convert_fusion.1
  58.4 0.9 copy-done.11
  59.3 0.8 fusion.16
  60.1 0.2 slice_bitcast_fusion.1
  60.3 0.4 multiply_convert_fusion.3
  60.7 0.8 fusion.19
  61.4 1.6 %slice_bitcast_fusion.3 = (f32[256,1024]{1,0:T(8,128)}, f32[256,1024]{1,0:T(8,128)}) fusion(f32[256,2,1024]{2,0,1:T(8,128)S(1)} %fusion.19), kind=kLoop, calls=%fused_computation.92 | loop fusion | bytes 4194304 | tf_op jit(solution)/shard_map/squeeze | solution.py:27
  63.0 0.3 multiply_convert_fusion.5
  63.4 0.8 fusion.22
  64.1 1.6 slice_bitcast_fusion.5
  65.7 0.3 multiply_convert_fusion.7
  66.0 0.8 fusion.25
  66.8 1.5 slice_bitcast_fusion.7
  68.3 0.2 pad_add_fusion
  68.5 1.0 copy-done.2
  69.5 0.3 copy-done.3
  69.8 0.2 pad_add_fusion.1
  70.0 1.0 copy-done.4
  71.0 0.3 copy-done.5
  71.4 0.2 pad_add_fusion.2
  71.6 1.0 copy-done.6
  72.6 0.3 copy-done.7
  72.9 1.2 pad_add_fusion.3
  74.1 2.0 %fusion.51 = f32[384,1024]{1,0:T(8,128)} fusion(s32[]{:T(128)S(6)} %select_n.213, f32[257,1024]{1,0:T(8,128)} %pad_add_fusion.3, s32[]{:T(128)S(6)} %select_n.214, f32[257,1024]{1,0:T(8,128)S(1)} %pad_add_fusion.2, s32[]{:T(128)S(6)} %select_n.215, f32[257,1024]{1,0:T(8,128)S(1)} %pad_add_fusion.1, s32[]{:T(128)S(6)} %select_n.216, ...), kind=kLoop, calls=%fused_computation.121 | loop fusion | flops 147455 | bytes 4407312
  76.1 1.0 fusion.55
  77.2 1.0 fusion.59
  78.2 1.0 fusion.63
  79.2 1.0 fusion.67
  80.3 1.0 fusion.71
  81.3 1.0 fusion.75
  82.3 1.0 fusion.79
  83.4 0.6 copy-done.12
  84.0 2.0 %sort.17 = (s32[64]{0:T(128)}, s32[64]{0:T(128)S(1)}) sort(s32[64]{0:T(128)S(1)} %copy-done.12, s32[64]{0:T(128)S(1)} %iota.4), dimensions={0}, to_apply=%region_5.6 | sort | flops 384 | bytes 1024 | tf_op jit(solution)/shard_map/jit(argsort)/sort | solution.py:60
  86.1 26.6 %reduce-scatter.2.cloned.1.call-done = f32[384,256]{1,0:T(8,128)} async-done(((f32[384,1024]{1,0:T(8,128)}), f32[384,256]{1,0:T(8,128)}) %reduce-scatter.2.cloned.1.call-update) | async-done | bytes 393232 | tf_op jit(solution)/shard_map/reduce_scatter | solution.py:56
  112.6 1.0 reshape.463
  113.7 0.6 gather_fusion
  114.4 0.3 broadcast_select_fusion
  114.7 0.1 copy.101
  114.8 1.8 %collective-permute-start = (f32[2,2,2,2,2,6,256]{6,4,3,2,1,0,5:T(2,128)S(1)}, f32[2,2,2,2,2,6,256]{6,4,3,2,1,0,5:T(2,128)S(1)}, u32[]{:S(2)}, u32[]{:S(2)}) collective-permute-start(f32[2,2,2,2,2,6,256]{6,4,3,2,1,0,5:T(2,128)S(1)} %bitcast.234), channel_id=1, source_target_pairs={{0,1},{1,0},{2,3},{3,2},{4,5},{5,4},{6,7},{7,6},{8,9},{9,8},{10,11... | collective-permute-start | bytes 589832 | tf_op jit(solution)/shard_map/ppermute | solution.py:79
  116.6 5.4 %collective-permute-done = f32[2,2,2,2,2,6,256]{6,4,3,2,1,0,5:T(2,128)S(1)} collective-permute-done((f32[2,2,2,2,2,6,256]{6,4,3,2,1,0,5:T(2,128)S(1)}, f32[2,2,2,2,2,6,256]{6,4,3,2,1,0,5:T(2,128)S(1)}, u32[]{:S(2)}, u32[]{:S(2)}) %collective-permute-start) | collective-permute-done | bytes 196640 | tf_op jit(solution)/shard_map/ppermute | solution.py:79
  122.0 0.2 fusion.81
  122.3 0.9 collective-permute-start.1
  123.2 3.8 %collective-permute-done.1 = f32[2,2,2,2,6,256]{5,3,2,1,0,4:T(2,128)S(1)} collective-permute-done((f32[2,2,2,2,6,256]{5,3,2,1,0,4:T(2,128)S(1)}, f32[2,2,2,2,6,256]{5,3,2,1,0,4:T(2,128)S(1)}, u32[]{:S(2)}, u32[]{:S(2)}) %collective-permute-start.1) | collective-permute-done | bytes 98336 | tf_op jit(solution)/shard_map/ppermute | solution.py:79
  127.1 0.1 fusion.99
  127.2 2.6 %collective-permute-start.2 = (f32[2,2,2,6,256]{4,2,1,0,3:T(2,128)S(1)}, f32[2,2,2,6,256]{4,2,1,0,3:T(2,128)S(1)}, u32[]{:S(2)}, u32[]{:S(2)}) collective-permute-start(f32[2,2,2,6,256]{4,2,1,0,3:T(2,128)S(1)} %bitcast.235), channel_id=1, source_target_pairs={{0,2},{1,3},{2,0},{3,1},{4,6},{5,7},{6,4},{7,5},{8,10},{9,11},{10,... | collective-permute-start | bytes 147464 | tf_op jit(solution)/shard_map/ppermute | solution.py:79
  129.8 2.4 %collective-permute-done.2 = f32[2,2,2,6,256]{4,2,1,0,3:T(2,128)S(1)} collective-permute-done((f32[2,2,2,6,256]{4,2,1,0,3:T(2,128)S(1)}, f32[2,2,2,6,256]{4,2,1,0,3:T(2,128)S(1)}, u32[]{:S(2)}, u32[]{:S(2)}) %collective-permute-start.2) | collective-permute-done | bytes 49184 | tf_op jit(solution)/shard_map/ppermute | solution.py:79
  132.4 1.5 collective-permute-start.3
  133.9 3.9 %collective-permute-done.3 = f32[2,2,6,256]{3,1,0,2:T(2,128)S(1)} collective-permute-done((f32[2,2,6,256]{3,1,0,2:T(2,128)S(1)}, f32[2,2,6,256]{3,1,0,2:T(2,128)S(1)}, u32[]{:S(2)}, u32[]{:S(2)}) %collective-permute-start.3) | collective-permute-done | bytes 24608 | tf_op jit(solution)/shard_map/ppermute | solution.py:79
  137.9 6.3 %collective-permute-start.4 = (f32[2,6,256]{2,0,1:T(2,128)S(1)}, f32[2,6,256]{2,0,1:T(2,128)S(1)}, u32[]{:S(2)}, u32[]{:S(2)}) collective-permute-start(f32[2,6,256]{2,0,1:T(2,128)S(1)} %bitcast.236), channel_id=1, source_target_pairs={{0,4},{1,5},{2,6},{3,7},{4,0},{5,1},{6,2},{7,3},{8,12},{9,13},{10,... | collective-permute-start | bytes 36872 | tf_op jit(solution)/shard_map/ppermute | solution.py:79
  144.2 1.7 %collective-permute-done.4 = f32[2,6,256]{2,0,1:T(2,128)S(1)} collective-permute-done((f32[2,6,256]{2,0,1:T(2,128)S(1)}, f32[2,6,256]{2,0,1:T(2,128)S(1)}, u32[]{:S(2)}, u32[]{:S(2)}) %collective-permute-start.4) | collective-permute-done | bytes 12320 | tf_op jit(solution)/shard_map/ppermute | solution.py:79
  146.0 2.8 %collective-permute-start.5 = (f32[6,256]{1,0:T(8,128)S(1)}, f32[6,256]{1,0:T(8,128)S(1)}, u32[]{:S(2)}, u32[]{:S(2)}) collective-permute-start(f32[6,256]{1,0:T(8,128)S(1)} %bitcast.237), channel_id=1, source_target_pairs={{0,32},{1,33},{2,34},{3,35},{4,36},{5,37},{6,38},{7,39},{8,40},{9,... | collective-permute-start | bytes 18440 | tf_op jit(solution)/shard_map/ppermute | solution.py:79
  148.7 2.5 %collective-permute-done.5 = f32[6,256]{1,0:T(8,128)S(1)} collective-permute-done((f32[6,256]{1,0:T(8,128)S(1)}, f32[6,256]{1,0:T(8,128)S(1)}, u32[]{:S(2)}, u32[]{:S(2)}) %collective-permute-start.5) | collective-permute-done | bytes 6176 | tf_op jit(solution)/shard_map/ppermute | solution.py:79
  151.2 0.6 fusion.93
  (38 shorter events, 0.6 us)
Async XLA Ops:
  6.5 1.6 copy-start.1
  6.5 106.1 %reduce-scatter.2.cloned.1.call-start = ((), (), s32[]{:S(2)}) async-start(), calls=%async_computation.1 | async-start | bytes 1966080 | tf_op jit(solution)/shard_map/reduce_scatter | solution.py:56
  8.1 0.7 copy-start.9
  8.1 0.7 copy-start.10
  15.2 1.1 copy-start.8
  58.1 1.2 copy-start.11
  68.3 1.2 copy-start.2
  68.3 1.5 copy-start.3
  69.8 1.2 copy-start.4
  69.8 1.5 copy-start.5
  71.4 1.2 copy-start.6
  71.4 1.5 copy-start.7
  74.1 2.0 %copy-start = (f32[257,1024]{1,0:T(8,128)S(1)}, f32[257,1024]{1,0:T(8,128)}, u32[]{:S(2)}) copy-start(f32[257,1024]{1,0:T(8,128)} %pad_add_fusion.3) | copy-start | bytes 3158020
  83.4 0.7 copy-start.12
  114.8 7.2 %collective-permute-start = (f32[2,2,2,2,2,6,256]{6,4,3,2,1,0,5:T(2,128)S(1)}, f32[2,2,2,2,2,6,256]{6,4,3,2,1,0,5:T(2,128)S(1)}, u32[]{:S(2)}, u32[]{:S(2)}) collective-permute-start(f32[2,2,2,2,2,6,256]{6,4,3,2,1,0,5:T(2,128)S(1)} %bitcast.234), channel_id=1, source_target_pairs={{0,1},{1,0},{2,3},{3,2},{4,5},{5,4},{6,7},{7,6},{8,9},{9,8},{10,11... | collective-permute-start | bytes 589832 | tf_op jit(solution)/shard_map/ppermute | solution.py:79
  122.3 4.7 %collective-permute-start.1 = (f32[2,2,2,2,6,256]{5,3,2,1,0,4:T(2,128)S(1)}, f32[2,2,2,2,6,256]{5,3,2,1,0,4:T(2,128)S(1)}, u32[]{:S(2)}, u32[]{:S(2)}) collective-permute-start(f32[2,2,2,2,6,256]{5,3,2,1,0,4:T(2,128)S(1)} %fusion.82), channel_id=1, source_target_pairs={{0,8},{1,9},{2,10},{3,11},{4,12},{5,13},{6,14},{7,15},{8,0},{9,1},... | collective-permute-start | bytes 294920 | tf_op jit(solution)/shard_map/ppermute | solution.py:79
  127.2 5.1 %collective-permute-start.2 = (f32[2,2,2,6,256]{4,2,1,0,3:T(2,128)S(1)}, f32[2,2,2,6,256]{4,2,1,0,3:T(2,128)S(1)}, u32[]{:S(2)}, u32[]{:S(2)}) collective-permute-start(f32[2,2,2,6,256]{4,2,1,0,3:T(2,128)S(1)} %bitcast.235), channel_id=1, source_target_pairs={{0,2},{1,3},{2,0},{3,1},{4,6},{5,7},{6,4},{7,5},{8,10},{9,11},{10,... | collective-permute-start | bytes 147464 | tf_op jit(solution)/shard_map/ppermute | solution.py:79
  132.4 5.4 %collective-permute-start.3 = (f32[2,2,6,256]{3,1,0,2:T(2,128)S(1)}, f32[2,2,6,256]{3,1,0,2:T(2,128)S(1)}, u32[]{:S(2)}, u32[]{:S(2)}) collective-permute-start(f32[2,2,6,256]{3,1,0,2:T(2,128)S(1)} %fusion.87), channel_id=1, source_target_pairs={{0,16},{1,17},{2,18},{3,19},{4,20},{5,21},{6,22},{7,23},{8,24},{9,... | collective-permute-start | bytes 73736 | tf_op jit(solution)/shard_map/ppermute | solution.py:79
  137.9 8.0 %collective-permute-start.4 = (f32[2,6,256]{2,0,1:T(2,128)S(1)}, f32[2,6,256]{2,0,1:T(2,128)S(1)}, u32[]{:S(2)}, u32[]{:S(2)}) collective-permute-start(f32[2,6,256]{2,0,1:T(2,128)S(1)} %bitcast.236), channel_id=1, source_target_pairs={{0,4},{1,5},{2,6},{3,7},{4,0},{5,1},{6,2},{7,3},{8,12},{9,13},{10,... | collective-permute-start | bytes 36872 | tf_op jit(solution)/shard_map/ppermute | solution.py:79
  146.0 5.2 %collective-permute-start.5 = (f32[6,256]{1,0:T(8,128)S(1)}, f32[6,256]{1,0:T(8,128)S(1)}, u32[]{:S(2)}, u32[]{:S(2)}) collective-permute-start(f32[6,256]{1,0:T(8,128)S(1)} %bitcast.237), channel_id=1, source_target_pairs={{0,32},{1,33},{2,34},{3,35},{4,36},{5,37},{6,38},{7,39},{8,40},{9,... | collective-permute-start | bytes 18440 | tf_op jit(solution)/shard_map/ppermute | solution.py:79
Sparse Core Ops, SparseCore 0:
  83.5 29.0 reduce-scatter.1

commit v3 on v2

v3 whole, which is shorter than its diff:
```python
import functools
import math

import jax
import jax.numpy as jnp
from jax import lax
from jax.experimental import pallas as pl
from jax.experimental.pallas import tpu as pltpu
from jax.sharding import PartitionSpec as P

MAXD = 127
OBLK = 128
PBLK = 128


def fwh_kernel(bins_ref, obs_ref, place_ref, frac_ref, src_ref, out_ref, *, amplitude, panel_blocks, window, bins_total):
    ob = pl.program_id(0)
    acc = jnp.zeros((OBLK, bins_total), jnp.float32)
    pad = jnp.zeros((OBLK, bins_total - window), jnp.float32)
    for pb in range(panel_blocks):
        cols = slice(pb * PBLK, (pb + 1) * PBLK)
        seps = [obs_ref[:, c : c + 1] - place_ref[c : c + 1, cols] for c in range(3)]
        dist_sq = seps[0] * seps[0] + seps[1] * seps[1] + seps[2] * seps[2]
        parts = [amplitude / jnp.sqrt(dist_sq)] + [amplitude * sep / dist_sq for sep in seps]
        weight = frac_ref[:, cols].astype(jnp.float32)
        low = None
        high = None
        for c in range(4):
            src = src_ref[c, cols, :]
            lo_w = (parts[c] * (1.0 - weight)).astype(jnp.bfloat16)
            hi_w = (parts[c] * weight).astype(jnp.bfloat16)
            lo_p = jnp.dot(lo_w, src, preferred_element_type=jnp.float32)
            hi_p = jnp.dot(hi_w, src, preferred_element_type=jnp.float32)
            low = lo_p if low is None else low + lo_p
            high = hi_p if high is None else high + hi_p
        shift = bins_ref[ob, pb]
        acc = acc + pltpu.roll(jnp.concatenate([low, pad], axis=1), shift, 1)
        acc = acc + pltpu.roll(jnp.concatenate([high, pad], axis=1), shift + 1, 1)
    out_ref[...] = acc.T


def per_device(sources, panel_places, observer_places, fraction, delay_bins, segment_owner):
    local_panels = sources.shape[2]
    window = sources.shape[3]
    bins_total = window + MAXD + 1
    amplitude = 60.0 / math.sqrt(local_panels * lax.axis_size("obs") * lax.axis_size("pan"))
    panel_blocks = local_panels // PBLK
    every_obs = lax.all_gather(observer_places, "obs", axis=1, tiled=True)
    obs_total = every_obs.shape[1]
    obs_blocks = obs_total // OBLK
    kernel = functools.partial(fwh_kernel, amplitude=amplitude, panel_blocks=panel_blocks, window=window, bins_total=bins_total)
    grid_spec = pltpu.PrefetchScalarGridSpec(
        num_scalar_prefetch=1,
        grid=(obs_blocks,),
        in_specs=[
            pl.BlockSpec((OBLK, 3), lambda i, b: (i, 0)),
            pl.BlockSpec((3, local_panels), lambda i, b: (0, 0)),
            pl.BlockSpec((OBLK, local_panels), lambda i, b: (i, 0)),
            pl.BlockSpec((4, local_panels, window), lambda i, b: (0, 0, 0)),
        ],
        out_specs=pl.BlockSpec((bins_total, OBLK), lambda i, b: (0, i)),
    )
    totals = pl.pallas_call(
        kernel,
        grid_spec=grid_spec,
        out_shape=jax.ShapeDtypeStruct((bins_total, obs_total), jnp.float32),
    )(delay_bins[:, 0, :], every_obs.T, panel_places[0], fraction[:, 0, :], sources[0])
    reduced = lax.psum_scatter(totals, "obs", scatter_dimension=1, tiled=True)
    segment_count = segment_owner.shape[0]
    seg_len = bins_total // segment_count
    arranged = reduced.reshape(segment_count, seg_len, reduced.shape[1])
    inverse = jnp.argsort(segment_owner)
    arranged = arranged[inverse]
    return halving_sum(arranged, "pan", (0, 3, 1, 4, 2, 5))


def halving_sum(data, axis, bit_order):
    count = data.shape[0]
    levels = count.bit_length() - 1
    me = lax.axis_index(axis)
    data = data.reshape((2,) * levels + data.shape[1:])
    remaining = list(range(levels - 1, -1, -1))
    for bit in bit_order:
        dim = remaining.index(bit)
        mine = (me >> bit) & 1
        low = lax.index_in_dim(data, 0, dim, keepdims=False)
        high = lax.index_in_dim(data, 1, dim, keepdims=False)
        keep = jnp.where(mine == 1, high, low)
        send = jnp.where(mine == 1, low, high)
        pairs = [(p, p ^ (1 << bit)) for p in range(count)]
        data = keep + lax.ppermute(send, axis, pairs)
        remaining.pop(dim)
    return data


def solution(mesh):
    return jax.shard_map(
        per_device,
        mesh=mesh,
        in_specs=(
            P("pan", None, "obs", None),
            P("pan", None, "obs"),
            P(None, "obs"),
            P(None, "pan", "obs"),
            P(None, "pan", "obs"),
            P(),
        ),
        out_specs=P("pan", "obs"),
        check_vma=False,
    )
```

time: 160 us -> 104 us (0.65)
  between operations: 54 us -> 13.5 us
  other arithmetic: 19.8 us -> 3.51 us
  Pallas kernels: 0 us -> 11.2 us
  local copies, waits for them, and re-layouts: 14.4 us -> 5.95 us
  matrix products: 3.01 us -> 0 us
  blocking collectives: 5.2 us -> 7.62 us
    pallas_call x0 -> x1, Pallas kernels: none -> 11.2 us  [per_device(): pl.pallas_call(kernel, grid_spec=grid_spec, out_shape=jax.ShapeDtypeStruc...]
    unnamed x7 -> x0, other arithmetic: 8.21 us -> none
    squeeze x4 -> x1, local copies, waits for them, and re-layouts: 4.88 us -> 1.35 us  [per_device(): delay_bins[:, 0, :]]
    unnamed x32 -> x8, local copies, waits for them, and re-layouts: 6.32 us -> 2.86 us
    dot_general x4 -> x0, matrix products: 3.01 us -> none  [placed_block(): jnp.einsum('cjs,gcoj->sgo', src_block, weights, preferred_element_type=jn...]
    all_gather x1, blocking collectives: 5.2 us -> 7.62 us  [per_device(): every_obs = lax.all_gather(observer_places, 'obs', axis=1, tiled=True)]
    concatenate x6 -> x0, other arithmetic: 2.34 us -> none  [the longest x5 1.32 us: block_kernel(): kernel = jnp.concatenate([monopole[None], dipole], axis=0)]
    add x4 -> x0, other arithmetic: 1.81 us -> none  [placed_block(): jnp.pad(products[:, 0], ((0, 1), (0, 0)))]
  transfers between devices with their start and end apart: 7 -> 7, of which waited for: 7 -> 7; matrix products, arithmetic and copies ran while one was open for 1% -> 2% of each run, Pallas kernels for 0% -> 0%
where the time goes in v3:
time: 104 us
  waiting for transfers between devices  46.1 us (44%)
  starting transfers between devices  15.8 us (15%)
  between operations  13.5 us (13%)
  Pallas kernels  11.2 us (11%)
  blocking collectives  7.62 us (7%)
  local copies, waits for them, and re-layouts  5.95 us (6%)
  other arithmetic  3.51 us (3%)
    reduce_scatter x1, waiting for transfers between devices, per_device(): reduced = lax.psum_scatter(totals, 'obs', scatter_dimension=1, tiled=True)  26.3 us
    ppermute x6, waiting for transfers between devices, halving_sum(): data = keep + lax.ppermute(send, axis, pairs)  19.8 us
    ppermute x6, starting transfers between devices, halving_sum(): data = keep + lax.ppermute(send, axis, pairs)  15.8 us
    pallas_call x1, Pallas kernels, per_device(): pl.pallas_call(kernel, grid_spec=grid_spec, out_shape=jax.ShapeDtypeStruc...  11.2 us
    all_gather x1, blocking collectives, per_device(): every_obs = lax.all_gather(observer_places, 'obs', axis=1, tiled=True)  7.62 us
    unnamed x8, local copies, waits for them, and re-layouts  2.86 us
  transfers between devices with their start and end apart: 7, of which 7 were waited for; matrix products, arithmetic and copies ran while one was open for 2% of the time, Pallas kernels for 0%

profile of v3, /device:TPU:24, one launch (start us, length us, event | category | flops | bytes accessed | tf_op | source)
XLA Modules:
  0.0 103.7 jit_solution(1707826389403118481)
XLA Ops:
  6.5 0.0 reduce-scatter.2.cloned.1.call-start
  6.5 0.8 copy.9
  7.4 7.6 %all_gather.3 = f32[3,1024]{0,1:T(8,128)} all-gather(f32[3,256]{0,1:T(8,128)S(1)} %copy.9), channel_id=1, replica_groups=mesh['obs'=4,'pan'=64] {'obs'}, dimensions={1}, use_global_device_ids=true | all-gather | bytes 15360 | tf_op jit(solution)/shard_map/all_gather | solution.py:48
  15.0 1.3 %copy.87 = f32[1,3,512]{2,1,0:T(4,128)} copy(f32[1,3,512]{2,0,1:T(1,128)} %param.7) | data formatting | bytes 12288
  16.3 1.3 %copy.10.bins_ref = s32[8,4]{1,0:T(8,128)} copy(s32[8,4]{0,1:T(4,128)} %bitcast.85) | data formatting | bytes 256 | tf_op jit(solution)/shard_map/squeeze | solution.py:67
  17.6 11.2 %shard_map.64 = f32[384,1024]{1,0:T(8,128)} custom-call(s32[8,4]{1,0:T(8,128)} %copy.10.bins_ref, f32[1024,3]{1,0:T(8,128)} %bitcast.76, f32[3,512]{1,0:T(4,128)} %bitcast.82, bf16[1024,512]{1,0:T(8,128)(2,1)} %bitcast.78, bf16[4,512,256]{2,1,0:T(8,128)(2,1)} %bitcast.79), custom_call_target="tpu_custom_call" | custom-call | tf_op jit(solution)/shard_map/pallas_call | solution.py:63
  28.9 0.0 copy-start
  28.9 0.0 reduce-scatter.2.cloned.1.call-update
  28.9 0.6 copy-done
  29.5 2.0 %sort.17 = (s32[64]{0:T(128)}, s32[64]{0:T(128)S(1)}) sort(s32[64]{0:T(128)S(1)} %copy-done, s32[64]{0:T(128)S(1)} %iota.4), dimensions={0}, to_apply=%region_1.0 | sort | flops 384 | bytes 1024 | tf_op jit(solution)/shard_map/jit(argsort)/sort | solution.py:72
  31.6 26.3 %reduce-scatter.2.cloned.1.call-done = f32[384,256]{1,0:T(8,128)} async-done(((f32[384,1024]{1,0:T(8,128)}), f32[384,256]{1,0:T(8,128)}) %reduce-scatter.2.cloned.1.call-update) | async-done | bytes 393232 | tf_op jit(solution)/shard_map/reduce_scatter | solution.py:68
  57.8 1.0 %reshape.30 = f32[64,6,256]{2,1,0:T(8,128)S(1)} reshape(f32[384,256]{1,0:T(8,128)} %reduce-scatter.2.cloned.1.call-done) | data formatting | bytes 786432 | tf_op jit(solution)/shard_map/reshape | solution.py:71
  58.9 0.6 gather_fusion
  59.5 0.1 fusion.14
  59.6 0.3 broadcast_select_fusion
  59.9 0.1 copy.83
  60.0 1.6 %collective-permute-start = (f32[2,2,2,2,2,6,256]{6,4,3,2,1,0,5:T(2,128)S(1)}, f32[2,2,2,2,2,6,256]{6,4,3,2,1,0,5:T(2,128)S(1)}, u32[]{:S(2)}, u32[]{:S(2)}) collective-permute-start(f32[2,2,2,2,2,6,256]{6,4,3,2,1,0,5:T(2,128)S(1)} %bitcast.80), channel_id=1, source_target_pairs={{0,1},{1,0},{2,3},{3,2},{4,5},{5,4},{6,7},{7,6},{8,9},{9,8},{10,11... | collective-permute-start | bytes 589832 | tf_op jit(solution)/shard_map/ppermute | solution.py:91
  61.7 5.4 %collective-permute-done = f32[2,2,2,2,2,6,256]{6,4,3,2,1,0,5:T(2,128)S(1)} collective-permute-done((f32[2,2,2,2,2,6,256]{6,4,3,2,1,0,5:T(2,128)S(1)}, f32[2,2,2,2,2,6,256]{6,4,3,2,1,0,5:T(2,128)S(1)}, u32[]{:S(2)}, u32[]{:S(2)}) %collective-permute-start) | collective-permute-done | bytes 196640 | tf_op jit(solution)/shard_map/ppermute | solution.py:91
  67.1 0.2 fusion.1
  67.3 0.1 fusion.2
  67.4 0.9 collective-permute-start.1
  68.3 3.8 %collective-permute-done.1 = f32[2,2,2,2,6,256]{5,3,2,1,0,4:T(2,128)S(1)} collective-permute-done((f32[2,2,2,2,6,256]{5,3,2,1,0,4:T(2,128)S(1)}, f32[2,2,2,2,6,256]{5,3,2,1,0,4:T(2,128)S(1)}, u32[]{:S(2)}, u32[]{:S(2)}) %collective-permute-start.1) | collective-permute-done | bytes 98336 | tf_op jit(solution)/shard_map/ppermute | solution.py:91
  72.1 0.1 fusion.4
  72.1 0.1 fusion.15
  72.3 2.6 %collective-permute-start.2 = (f32[2,2,2,6,256]{4,2,1,0,3:T(2,128)S(1)}, f32[2,2,2,6,256]{4,2,1,0,3:T(2,128)S(1)}, u32[]{:S(2)}, u32[]{:S(2)}) collective-permute-start(f32[2,2,2,6,256]{4,2,1,0,3:T(2,128)S(1)} %bitcast.81), channel_id=1, source_target_pairs={{0,2},{1,3},{2,0},{3,1},{4,6},{5,7},{6,4},{7,5},{8,10},{9,11},{10,... | collective-permute-start | bytes 147464 | tf_op jit(solution)/shard_map/ppermute | solution.py:91
  74.9 2.5 %collective-permute-done.2 = f32[2,2,2,6,256]{4,2,1,0,3:T(2,128)S(1)} collective-permute-done((f32[2,2,2,6,256]{4,2,1,0,3:T(2,128)S(1)}, f32[2,2,2,6,256]{4,2,1,0,3:T(2,128)S(1)}, u32[]{:S(2)}, u32[]{:S(2)}) %collective-permute-start.2) | collective-permute-done | bytes 49184 | tf_op jit(solution)/shard_map/ppermute | solution.py:91
  77.4 1.5 %collective-permute-start.3 = (f32[2,2,6,256]{3,1,0,2:T(2,128)S(1)}, f32[2,2,6,256]{3,1,0,2:T(2,128)S(1)}, u32[]{:S(2)}, u32[]{:S(2)}) collective-permute-start(f32[2,2,6,256]{3,1,0,2:T(2,128)S(1)} %fusion.7), channel_id=1, source_target_pairs={{0,16},{1,17},{2,18},{3,19},{4,20},{5,21},{6,22},{7,23},{8,24},{9,... | collective-permute-start | bytes 73736 | tf_op jit(solution)/shard_map/ppermute | solution.py:91
  78.9 3.9 %collective-permute-done.3 = f32[2,2,6,256]{3,1,0,2:T(2,128)S(1)} collective-permute-done((f32[2,2,6,256]{3,1,0,2:T(2,128)S(1)}, f32[2,2,6,256]{3,1,0,2:T(2,128)S(1)}, u32[]{:S(2)}, u32[]{:S(2)}) %collective-permute-start.3) | collective-permute-done | bytes 24608 | tf_op jit(solution)/shard_map/ppermute | solution.py:91
  82.9 6.3 %collective-permute-start.4 = (f32[2,6,256]{2,0,1:T(2,128)S(1)}, f32[2,6,256]{2,0,1:T(2,128)S(1)}, u32[]{:S(2)}, u32[]{:S(2)}) collective-permute-start(f32[2,6,256]{2,0,1:T(2,128)S(1)} %bitcast.83), channel_id=1, source_target_pairs={{0,4},{1,5},{2,6},{3,7},{4,0},{5,1},{6,2},{7,3},{8,12},{9,13},{10,... | collective-permute-start | bytes 36872 | tf_op jit(solution)/shard_map/ppermute | solution.py:91
  89.3 1.7 %collective-permute-done.4 = f32[2,6,256]{2,0,1:T(2,128)S(1)} collective-permute-done((f32[2,6,256]{2,0,1:T(2,128)S(1)}, f32[2,6,256]{2,0,1:T(2,128)S(1)}, u32[]{:S(2)}, u32[]{:S(2)}) %collective-permute-start.4) | collective-permute-done | bytes 12320 | tf_op jit(solution)/shard_map/ppermute | solution.py:91
  91.0 2.8 %collective-permute-start.5 = (f32[6,256]{1,0:T(8,128)S(1)}, f32[6,256]{1,0:T(8,128)S(1)}, u32[]{:S(2)}, u32[]{:S(2)}) collective-permute-start(f32[6,256]{1,0:T(8,128)S(1)} %bitcast.84), channel_id=1, source_target_pairs={{0,32},{1,33},{2,34},{3,35},{4,36},{5,37},{6,38},{7,39},{8,40},{9,... | collective-permute-start | bytes 18440 | tf_op jit(solution)/shard_map/ppermute | solution.py:91
  93.8 2.5 %collective-permute-done.5 = f32[6,256]{1,0:T(8,128)S(1)} collective-permute-done((f32[6,256]{1,0:T(8,128)S(1)}, f32[6,256]{1,0:T(8,128)S(1)}, u32[]{:S(2)}, u32[]{:S(2)}) %collective-permute-start.5) | collective-permute-done | bytes 6176 | tf_op jit(solution)/shard_map/ppermute | solution.py:91
  96.2 0.6 fusion.13
  (12 shorter events, 0.2 us)
Async XLA Ops:
  6.5 51.3 %reduce-scatter.2.cloned.1.call-start = ((), (), s32[]{:S(2)}) async-start(), calls=%async_computation.1 | async-start | bytes 1966080 | tf_op jit(solution)/shard_map/reduce_scatter | solution.py:68
  28.9 0.7 copy-start
  60.0 7.1 %collective-permute-start = (f32[2,2,2,2,2,6,256]{6,4,3,2,1,0,5:T(2,128)S(1)}, f32[2,2,2,2,2,6,256]{6,4,3,2,1,0,5:T(2,128)S(1)}, u32[]{:S(2)}, u32[]{:S(2)}) collective-permute-start(f32[2,2,2,2,2,6,256]{6,4,3,2,1,0,5:T(2,128)S(1)} %bitcast.80), channel_id=1, source_target_pairs={{0,1},{1,0},{2,3},{3,2},{4,5},{5,4},{6,7},{7,6},{8,9},{9,8},{10,11... | collective-permute-start | bytes 589832 | tf_op jit(solution)/shard_map/ppermute | solution.py:91
  67.4 4.7 %collective-permute-start.1 = (f32[2,2,2,2,6,256]{5,3,2,1,0,4:T(2,128)S(1)}, f32[2,2,2,2,6,256]{5,3,2,1,0,4:T(2,128)S(1)}, u32[]{:S(2)}, u32[]{:S(2)}) collective-permute-start(f32[2,2,2,2,6,256]{5,3,2,1,0,4:T(2,128)S(1)} %fusion.2), channel_id=1, source_target_pairs={{0,8},{1,9},{2,10},{3,11},{4,12},{5,13},{6,14},{7,15},{8,0},{9,1},... | collective-permute-start | bytes 294920 | tf_op jit(solution)/shard_map/ppermute | solution.py:91
  72.3 5.1 %collective-permute-start.2 = (f32[2,2,2,6,256]{4,2,1,0,3:T(2,128)S(1)}, f32[2,2,2,6,256]{4,2,1,0,3:T(2,128)S(1)}, u32[]{:S(2)}, u32[]{:S(2)}) collective-permute-start(f32[2,2,2,6,256]{4,2,1,0,3:T(2,128)S(1)} %bitcast.81), channel_id=1, source_target_pairs={{0,2},{1,3},{2,0},{3,1},{4,6},{5,7},{6,4},{7,5},{8,10},{9,11},{10,... | collective-permute-start | bytes 147464 | tf_op jit(solution)/shard_map/ppermute | solution.py:91
  77.4 5.4 %collective-permute-start.3 = (f32[2,2,6,256]{3,1,0,2:T(2,128)S(1)}, f32[2,2,6,256]{3,1,0,2:T(2,128)S(1)}, u32[]{:S(2)}, u32[]{:S(2)}) collective-permute-start(f32[2,2,6,256]{3,1,0,2:T(2,128)S(1)} %fusion.7), channel_id=1, source_target_pairs={{0,16},{1,17},{2,18},{3,19},{4,20},{5,21},{6,22},{7,23},{8,24},{9,... | collective-permute-start | bytes 73736 | tf_op jit(solution)/shard_map/ppermute | solution.py:91
  82.9 8.0 %collective-permute-start.4 = (f32[2,6,256]{2,0,1:T(2,128)S(1)}, f32[2,6,256]{2,0,1:T(2,128)S(1)}, u32[]{:S(2)}, u32[]{:S(2)}) collective-permute-start(f32[2,6,256]{2,0,1:T(2,128)S(1)} %bitcast.83), channel_id=1, source_target_pairs={{0,4},{1,5},{2,6},{3,7},{4,0},{5,1},{6,2},{7,3},{8,12},{9,13},{10,... | collective-permute-start | bytes 36872 | tf_op jit(solution)/shard_map/ppermute | solution.py:91
  91.0 5.2 %collective-permute-start.5 = (f32[6,256]{1,0:T(8,128)S(1)}, f32[6,256]{1,0:T(8,128)S(1)}, u32[]{:S(2)}, u32[]{:S(2)}) collective-permute-start(f32[6,256]{1,0:T(8,128)S(1)} %bitcast.84), channel_id=1, source_target_pairs={{0,32},{1,33},{2,34},{3,35},{4,36},{5,37},{6,38},{7,39},{8,40},{9,... | collective-permute-start | bytes 18440 | tf_op jit(solution)/shard_map/ppermute | solution.py:91
Sparse Core Ops, SparseCore 0:
  29.0 28.7 reduce-scatter.1

commit v4 on v3

--- a/solution.py
+++ b/solution.py
@@ -65,7 +65,18 @@
         grid_spec=grid_spec,
         out_shape=jax.ShapeDtypeStruct((bins_total, obs_total), jnp.float32),
     )(delay_bins[:, 0, :], every_obs.T, panel_places[0], fraction[:, 0, :], sources[0])
-    reduced = lax.psum_scatter(totals, "obs", scatter_dimension=1, tiled=True)
+    quarter = obs_total // 4
+    halves = totals.reshape(bins_total, 2, 2, quarter)
+    me = lax.axis_index("obs")
+    for bit, dim in ((0, 2), (1, 1)):
+        mine = (me >> bit) & 1
+        low = lax.index_in_dim(halves, 0, dim, keepdims=False)
+        high = lax.index_in_dim(halves, 1, dim, keepdims=False)
+        keep = jnp.where(mine == 1, high, low)
+        send = jnp.where(mine == 1, low, high)
+        pairs = [(p, p ^ (1 << bit)) for p in range(4)]
+        halves = keep + lax.ppermute(send, "obs", pairs)
+    reduced = halves
     segment_count = segment_owner.shape[0]
     seg_len = bins_total // segment_count
     arranged = reduced.reshape(segment_count, seg_len, reduced.shape[1])

time: 104 us -> 81.8 us (0.79)
  waiting for transfers between devices: 46.1 us -> 28.9 us
  between operations: 13.5 us -> 0.17 us
  local copies, waits for them, and re-layouts: 5.95 us -> 11 us
  starting transfers between devices: 15.8 us -> 18.7 us
    reduce_scatter x1 -> x0, waiting for transfers between devices: 26.3 us -> none  [per_device(): reduced = lax.psum_scatter(totals, 'obs', scatter_dimension=1, tiled=True)]
    ppermute x0 -> x2, waiting for transfers between devices: none -> 10.2 us  [per_device(): halves = keep + lax.ppermute(send, 'obs', pairs)]
    reshape x0 -> x1, local copies, waits for them, and re-layouts: none -> 3.43 us  [per_device(): halves = totals.reshape(bins_total, 2, 2, quarter)]
    slice x0 -> x1, local copies, waits for them, and re-layouts: none -> 3.23 us  [per_device(): high = lax.index_in_dim(halves, 1, dim, keepdims=False)]
    ppermute x0 -> x2, starting transfers between devices: none -> 1.58 us  [per_device(): halves = keep + lax.ppermute(send, 'obs', pairs)]
    ppermute x6, starting transfers between devices: 15.8 us -> 17.1 us  [halving_sum(): data = keep + lax.ppermute(send, axis, pairs)]
    ppermute x6, waiting for transfers between devices: 19.8 us -> 18.7 us  [halving_sum(): data = keep + lax.ppermute(send, axis, pairs)]
  transfers between devices with their start and end apart: 7 -> 8, of which waited for: 7 -> 8; matrix products, arithmetic and copies ran while one was open for 2% -> 3% of each run, Pallas kernels for 0% -> 0%
where the time goes in v4:
time: 81.8 us; the launch traced here: 81.5 us
  waiting for transfers between devices  28.9 us (35%)
  starting transfers between devices  18.7 us (23%)
  Pallas kernels  11.3 us (14%)
  local copies, waits for them, and re-layouts  11 us (13%)
  blocking collectives  7.62 us (9%)
  other arithmetic  3.89 us (5%)
    ppermute x6, waiting for transfers between devices, halving_sum(): data = keep + lax.ppermute(send, axis, pairs)  18.7 us
    ppermute x6, starting transfers between devices, halving_sum(): data = keep + lax.ppermute(send, axis, pairs)  17.1 us
    pallas_call x1, Pallas kernels, per_device(): pl.pallas_call(kernel, grid_spec=grid_spec, out_shape=jax.ShapeDtypeStruc...  11.3 us
    ppermute x2, waiting for transfers between devices, per_device(): halves = keep + lax.ppermute(send, 'obs', pairs)  10.2 us
    all_gather x1, blocking collectives, per_device(): every_obs = lax.all_gather(observer_places, 'obs', axis=1, tiled=True)  7.62 us
    reshape x1, local copies, waits for them, and re-layouts, per_device(): halves = totals.reshape(bins_total, 2, 2, quarter)  3.43 us
    slice x1, local copies, waits for them, and re-layouts, per_device(): high = lax.index_in_dim(halves, 1, dim, keepdims=False)  3.23 us
    unnamed x8, local copies, waits for them, and re-layouts  2.25 us
  transfers between devices with their start and end apart: 8, of which 8 were waited for; matrix products, arithmetic and copies ran while one was open for 3% of the time, Pallas kernels for 0%

profile of v4, /device:TPU:24, one launch (start us, length us, event | category | flops | bytes accessed | tf_op | source)
XLA Modules:
  0.0 81.5 jit_solution(3590171129854614502)
XLA Ops:
  0.0 0.8 copy.17
  0.8 7.6 %all_gather.3 = f32[3,1024]{0,1:T(8,128)} all-gather(f32[3,256]{0,1:T(8,128)S(1)} %copy.17), channel_id=1, replica_groups=mesh['obs'=4,'pan'=64] {'obs'}, dimensions={1}, use_global_device_ids=true | all-gather | bytes 15360 | tf_op jit(solution)/shard_map/all_gather | solution.py:48
  8.4 1.3 %copy.103 = f32[1,3,512]{2,1,0:T(4,128)} copy(f32[1,3,512]{2,0,1:T(1,128)} %param.7) | data formatting | bytes 12288
  9.7 1.3 %copy.18.bins_ref = s32[8,4]{1,0:T(8,128)} copy(s32[8,4]{0,1:T(4,128)} %bitcast.93) | data formatting | bytes 256 | tf_op jit(solution)/shard_map/squeeze | solution.py:67
  11.1 11.3 %shard_map.64 = f32[384,1024]{1,0:T(8,128)} custom-call(s32[8,4]{1,0:T(8,128)} %copy.18.bins_ref, f32[1024,3]{1,0:T(8,128)} %bitcast.84, f32[3,512]{1,0:T(4,128)} %bitcast.90, bf16[1024,512]{1,0:T(8,128)(2,1)} %bitcast.86, bf16[4,512,256]{2,1,0:T(8,128)(2,1)} %bitcast.87), custom_call_target="tpu_custom_call" | custom-call | tf_op jit(solution)/shard_map/pallas_call | solution.py:63
  22.3 3.4 %reshape.41 = f32[384,2,2,256]{3,2,1,0:T(2,128)} reshape(f32[384,1024]{1,0:T(8,128)} %shard_map.64) | data formatting | bytes 3145728 | tf_op jit(solution)/shard_map/reshape | solution.py:69
  25.8 3.2 %fusion.14 = (f32[384,2,1,256]{3,2,1,0:T(1,128)S(1)}, f32[384,2,1,256]{3,2,1,0:T(1,128)S(1)}) fusion(f32[384,2,2,256]{3,2,1,0:T(2,128)} %reshape.41), kind=kLoop, calls=%fused_computation.38 | loop fusion | bytes 3145728 | tf_op jit(solution)/shard_map/slice | solution.py:74
  29.0 0.1 select_bitcast_fusion
  29.1 0.4 collective-permute-start
  29.5 0.0 copy-start
  29.5 1.9 %collective-permute-done = f32[384,2,256]{2,0,1:T(8,128)S(1)} collective-permute-done((f32[384,2,256]{2,0,1:T(8,128)S(1)}, f32[384,2,256]{2,0,1:T(8,128)S(1)}, u32[]{:S(2)}, u32[]{:S(2)}) %collective-permute-start) | collective-permute-done | bytes 786464 | tf_op jit(solution)/shard_map/ppermute | solution.py:78
  31.5 0.2 bitcast_add_fusion
  31.6 0.1 select_bitcast_fusion.1
  31.7 1.2 %collective-permute-start.1 = (f32[384,256]{1,0:T(8,128)S(1)}, f32[384,256]{1,0:T(8,128)S(1)}, u32[]{:S(2)}, u32[]{:S(2)}) collective-permute-start(f32[384,256]{1,0:T(8,128)S(1)} %select_bitcast_fusion.1), channel_id=1, source_target_pairs={{0,128},{64,192},{128,0},{192,64},{1,129},{65,193},{129,1},{193,65... | collective-permute-start | bytes 1179656 | tf_op jit(solution)/shard_map/ppermute | solution.py:78
  32.9 0.0 copy-done
  32.9 2.0 %sort.17 = (s32[64]{0:T(128)}, s32[64]{0:T(128)S(1)}) sort(s32[64]{0:T(128)S(1)} %copy-done, s32[64]{0:T(128)S(1)} %iota.4), dimensions={0}, to_apply=%region_0.1 | sort | flops 384 | bytes 1024 | tf_op jit(solution)/shard_map/jit(argsort)/sort | solution.py:83
  34.9 8.2 %collective-permute-done.1 = f32[384,256]{1,0:T(8,128)S(1)} collective-permute-done((f32[384,256]{1,0:T(8,128)S(1)}, f32[384,256]{1,0:T(8,128)S(1)}, u32[]{:S(2)}, u32[]{:S(2)}) %collective-permute-start.1) | collective-permute-done | bytes 393248 | tf_op jit(solution)/shard_map/ppermute | solution.py:78
  43.1 0.1 bitcast_add_fusion.1
  43.2 0.1 reshape.42
  43.3 0.6 gather_fusion
  43.9 0.1 fusion.15
  44.0 0.3 broadcast_select_fusion
  44.3 0.1 copy.99
  44.4 2.0 %collective-permute-start.2 = (f32[2,2,2,2,2,6,256]{6,4,3,2,1,0,5:T(2,128)S(1)}, f32[2,2,2,2,2,6,256]{6,4,3,2,1,0,5:T(2,128)S(1)}, u32[]{:S(2)}, u32[]{:S(2)}) collective-permute-start(f32[2,2,2,2,2,6,256]{6,4,3,2,1,0,5:T(2,128)S(1)} %bitcast.88), channel_id=1, source_target_pairs={{0,1},{1,0},{2,3},{3,2},{4,5},{5,4},{6,7},{7,6},{8,9},{9,8},{10,11... | collective-permute-start | bytes 589832 | tf_op jit(solution)/shard_map/ppermute | solution.py:102
  46.4 4.5 %collective-permute-done.2 = f32[2,2,2,2,2,6,256]{6,4,3,2,1,0,5:T(2,128)S(1)} collective-permute-done((f32[2,2,2,2,2,6,256]{6,4,3,2,1,0,5:T(2,128)S(1)}, f32[2,2,2,2,2,6,256]{6,4,3,2,1,0,5:T(2,128)S(1)}, u32[]{:S(2)}, u32[]{:S(2)}) %collective-permute-start.2) | collective-permute-done | bytes 196640 | tf_op jit(solution)/shard_map/ppermute | solution.py:102
  51.0 0.2 fusion.1
  51.2 0.1 fusion.2
  51.2 0.8 %collective-permute-start.3 = (f32[2,2,2,2,6,256]{5,3,2,1,0,4:T(2,128)S(1)}, f32[2,2,2,2,6,256]{5,3,2,1,0,4:T(2,128)S(1)}, u32[]{:S(2)}, u32[]{:S(2)}) collective-permute-start(f32[2,2,2,2,6,256]{5,3,2,1,0,4:T(2,128)S(1)} %fusion.2), channel_id=1, source_target_pairs={{0,8},{1,9},{2,10},{3,11},{4,12},{5,13},{6,14},{7,15},{8,0},{9,1},... | collective-permute-start | bytes 294920 | tf_op jit(solution)/shard_map/ppermute | solution.py:102
  52.0 3.9 %collective-permute-done.3 = f32[2,2,2,2,6,256]{5,3,2,1,0,4:T(2,128)S(1)} collective-permute-done((f32[2,2,2,2,6,256]{5,3,2,1,0,4:T(2,128)S(1)}, f32[2,2,2,2,6,256]{5,3,2,1,0,4:T(2,128)S(1)}, u32[]{:S(2)}, u32[]{:S(2)}) %collective-permute-start.3) | collective-permute-done | bytes 98336 | tf_op jit(solution)/shard_map/ppermute | solution.py:102
  55.9 0.1 fusion.4
  56.0 0.1 fusion.16
  56.1 3.4 %collective-permute-start.4 = (f32[2,2,2,6,256]{4,2,1,0,3:T(2,128)S(1)}, f32[2,2,2,6,256]{4,2,1,0,3:T(2,128)S(1)}, u32[]{:S(2)}, u32[]{:S(2)}) collective-permute-start(f32[2,2,2,6,256]{4,2,1,0,3:T(2,128)S(1)} %bitcast.89), channel_id=1, source_target_pairs={{0,2},{1,3},{2,0},{3,1},{4,6},{5,7},{6,4},{7,5},{8,10},{9,11},{10,... | collective-permute-start | bytes 147464 | tf_op jit(solution)/shard_map/ppermute | solution.py:102
  59.5 2.1 %collective-permute-done.4 = f32[2,2,2,6,256]{4,2,1,0,3:T(2,128)S(1)} collective-permute-done((f32[2,2,2,6,256]{4,2,1,0,3:T(2,128)S(1)}, f32[2,2,2,6,256]{4,2,1,0,3:T(2,128)S(1)}, u32[]{:S(2)}, u32[]{:S(2)}) %collective-permute-start.4) | collective-permute-done | bytes 49184 | tf_op jit(solution)/shard_map/ppermute | solution.py:102
  61.7 1.3 %collective-permute-start.5 = (f32[2,2,6,256]{3,1,0,2:T(2,128)S(1)}, f32[2,2,6,256]{3,1,0,2:T(2,128)S(1)}, u32[]{:S(2)}, u32[]{:S(2)}) collective-permute-start(f32[2,2,6,256]{3,1,0,2:T(2,128)S(1)} %fusion.7), channel_id=1, source_target_pairs={{0,16},{1,17},{2,18},{3,19},{4,20},{5,21},{6,22},{7,23},{8,24},{9,... | collective-permute-start | bytes 73736 | tf_op jit(solution)/shard_map/ppermute | solution.py:102
  63.0 4.1 %collective-permute-done.5 = f32[2,2,6,256]{3,1,0,2:T(2,128)S(1)} collective-permute-done((f32[2,2,6,256]{3,1,0,2:T(2,128)S(1)}, f32[2,2,6,256]{3,1,0,2:T(2,128)S(1)}, u32[]{:S(2)}, u32[]{:S(2)}) %collective-permute-start.5) | collective-permute-done | bytes 24608 | tf_op jit(solution)/shard_map/ppermute | solution.py:102
  67.2 6.7 %collective-permute-start.6 = (f32[2,6,256]{2,0,1:T(2,128)S(1)}, f32[2,6,256]{2,0,1:T(2,128)S(1)}, u32[]{:S(2)}, u32[]{:S(2)}) collective-permute-start(f32[2,6,256]{2,0,1:T(2,128)S(1)} %bitcast.91), channel_id=1, source_target_pairs={{0,4},{1,5},{2,6},{3,7},{4,0},{5,1},{6,2},{7,3},{8,12},{9,13},{10,... | collective-permute-start | bytes 36872 | tf_op jit(solution)/shard_map/ppermute | solution.py:102
  73.9 1.7 %collective-permute-done.6 = f32[2,6,256]{2,0,1:T(2,128)S(1)} collective-permute-done((f32[2,6,256]{2,0,1:T(2,128)S(1)}, f32[2,6,256]{2,0,1:T(2,128)S(1)}, u32[]{:S(2)}, u32[]{:S(2)}) %collective-permute-start.6) | collective-permute-done | bytes 12320 | tf_op jit(solution)/shard_map/ppermute | solution.py:102
  75.6 2.8 %collective-permute-start.7 = (f32[6,256]{1,0:T(8,128)S(1)}, f32[6,256]{1,0:T(8,128)S(1)}, u32[]{:S(2)}, u32[]{:S(2)}) collective-permute-start(f32[6,256]{1,0:T(8,128)S(1)} %bitcast.92), channel_id=1, source_target_pairs={{0,32},{1,33},{2,34},{3,35},{4,36},{5,37},{6,38},{7,39},{8,40},{9,... | collective-permute-start | bytes 18440 | tf_op jit(solution)/shard_map/ppermute | solution.py:102
  78.4 2.4 %collective-permute-done.7 = f32[6,256]{1,0:T(8,128)S(1)} collective-permute-done((f32[6,256]{1,0:T(8,128)S(1)}, f32[6,256]{1,0:T(8,128)S(1)}, u32[]{:S(2)}, u32[]{:S(2)}) %collective-permute-start.7) | collective-permute-done | bytes 6176 | tf_op jit(solution)/shard_map/ppermute | solution.py:102
  80.8 0.6 fusion.13
  (12 shorter events, 0.2 us)
Async XLA Ops:
  29.1 2.4 %collective-permute-start = (f32[384,2,256]{2,0,1:T(8,128)S(1)}, f32[384,2,256]{2,0,1:T(8,128)S(1)}, u32[]{:S(2)}, u32[]{:S(2)}) collective-permute-start(f32[384,2,256]{2,0,1:T(8,128)S(1)} %select_bitcast_fusion), channel_id=1, source_target_pairs={{0,64},{64,0},{128,192},{192,128},{1,65},{65,1},{129,193},{193,129... | collective-permute-start | bytes 2359304 | tf_op jit(solution)/shard_map/ppermute | solution.py:78
  29.5 3.3 %copy-start = (s32[64]{0:T(128)S(1)}, s32[64]{0:T(128)}, u32[]{:S(2)}) copy-start(s32[64]{0:T(128)} %param.11) | copy-start | bytes 772
  31.7 11.4 %collective-permute-start.1 = (f32[384,256]{1,0:T(8,128)S(1)}, f32[384,256]{1,0:T(8,128)S(1)}, u32[]{:S(2)}, u32[]{:S(2)}) collective-permute-start(f32[384,256]{1,0:T(8,128)S(1)} %select_bitcast_fusion.1), channel_id=1, source_target_pairs={{0,128},{64,192},{128,0},{192,64},{1,129},{65,193},{129,1},{193,65... | collective-permute-start | bytes 1179656 | tf_op jit(solution)/shard_map/ppermute | solution.py:78
  44.4 6.5 %collective-permute-start.2 = (f32[2,2,2,2,2,6,256]{6,4,3,2,1,0,5:T(2,128)S(1)}, f32[2,2,2,2,2,6,256]{6,4,3,2,1,0,5:T(2,128)S(1)}, u32[]{:S(2)}, u32[]{:S(2)}) collective-permute-start(f32[2,2,2,2,2,6,256]{6,4,3,2,1,0,5:T(2,128)S(1)} %bitcast.88), channel_id=1, source_target_pairs={{0,1},{1,0},{2,3},{3,2},{4,5},{5,4},{6,7},{7,6},{8,9},{9,8},{10,11... | collective-permute-start | bytes 589832 | tf_op jit(solution)/shard_map/ppermute | solution.py:102
  51.2 4.7 %collective-permute-start.3 = (f32[2,2,2,2,6,256]{5,3,2,1,0,4:T(2,128)S(1)}, f32[2,2,2,2,6,256]{5,3,2,1,0,4:T(2,128)S(1)}, u32[]{:S(2)}, u32[]{:S(2)}) collective-permute-start(f32[2,2,2,2,6,256]{5,3,2,1,0,4:T(2,128)S(1)} %fusion.2), channel_id=1, source_target_pairs={{0,8},{1,9},{2,10},{3,11},{4,12},{5,13},{6,14},{7,15},{8,0},{9,1},... | collective-permute-start | bytes 294920 | tf_op jit(solution)/shard_map/ppermute | solution.py:102
  56.1 5.5 %collective-permute-start.4 = (f32[2,2,2,6,256]{4,2,1,0,3:T(2,128)S(1)}, f32[2,2,2,6,256]{4,2,1,0,3:T(2,128)S(1)}, u32[]{:S(2)}, u32[]{:S(2)}) collective-permute-start(f32[2,2,2,6,256]{4,2,1,0,3:T(2,128)S(1)} %bitcast.89), channel_id=1, source_target_pairs={{0,2},{1,3},{2,0},{3,1},{4,6},{5,7},{6,4},{7,5},{8,10},{9,11},{10,... | collective-permute-start | bytes 147464 | tf_op jit(solution)/shard_map/ppermute | solution.py:102
  61.7 5.4 %collective-permute-start.5 = (f32[2,2,6,256]{3,1,0,2:T(2,128)S(1)}, f32[2,2,6,256]{3,1,0,2:T(2,128)S(1)}, u32[]{:S(2)}, u32[]{:S(2)}) collective-permute-start(f32[2,2,6,256]{3,1,0,2:T(2,128)S(1)} %fusion.7), channel_id=1, source_target_pairs={{0,16},{1,17},{2,18},{3,19},{4,20},{5,21},{6,22},{7,23},{8,24},{9,... | collective-permute-start | bytes 73736 | tf_op jit(solution)/shard_map/ppermute | solution.py:102
  67.2 8.4 %collective-permute-start.6 = (f32[2,6,256]{2,0,1:T(2,128)S(1)}, f32[2,6,256]{2,0,1:T(2,128)S(1)}, u32[]{:S(2)}, u32[]{:S(2)}) collective-permute-start(f32[2,6,256]{2,0,1:T(2,128)S(1)} %bitcast.91), channel_id=1, source_target_pairs={{0,4},{1,5},{2,6},{3,7},{4,0},{5,1},{6,2},{7,3},{8,12},{9,13},{10,... | collective-permute-start | bytes 36872 | tf_op jit(solution)/shard_map/ppermute | solution.py:102
  75.6 5.2 %collective-permute-start.7 = (f32[6,256]{1,0:T(8,128)S(1)}, f32[6,256]{1,0:T(8,128)S(1)}, u32[]{:S(2)}, u32[]{:S(2)}) collective-permute-start(f32[6,256]{1,0:T(8,128)S(1)} %bitcast.92), channel_id=1, source_target_pairs={{0,32},{1,33},{2,34},{3,35},{4,36},{5,37},{6,38},{7,39},{8,40},{9,... | collective-permute-start | bytes 18440 | tf_op jit(solution)/shard_map/ppermute | solution.py:102

commit v5 on v4

--- a/solution.py
+++ b/solution.py
@@ -58,17 +58,16 @@
             pl.BlockSpec((OBLK, local_panels), lambda i, b: (i, 0)),
             pl.BlockSpec((4, local_panels, window), lambda i, b: (0, 0, 0)),
         ],
-        out_specs=pl.BlockSpec((bins_total, OBLK), lambda i, b: (0, i)),
+        out_specs=pl.BlockSpec((None, bins_total, OBLK), lambda i, b: (i // 2, 0, i % 2)),
     )
     totals = pl.pallas_call(
         kernel,
         grid_spec=grid_spec,
-        out_shape=jax.ShapeDtypeStruct((bins_total, obs_total), jnp.float32),
+        out_shape=jax.ShapeDtypeStruct((obs_blocks // 2, bins_total, 2 * OBLK), jnp.float32),
     )(delay_bins[:, 0, :], every_obs.T, panel_places[0], fraction[:, 0, :], sources[0])
-    quarter = obs_total // 4
-    halves = totals.reshape(bins_total, 2, 2, quarter)
+    halves = totals.reshape((2, 2) + totals.shape[1:])
     me = lax.axis_index("obs")
-    for bit, dim in ((0, 2), (1, 1)):
+    for bit, dim in ((0, 1), (1, 0)):
         mine = (me >> bit) & 1
         low = lax.index_in_dim(halves, 0, dim, keepdims=False)
         high = lax.index_in_dim(halves, 1, dim, keepdims=False)

time: 81.8 us -> 76.6 us (0.936)
  local copies, waits for them, and re-layouts: 11 us -> 4.33 us
  other arithmetic: 3.89 us -> 5.38 us
    reshape x1 -> x0, local copies, waits for them, and re-layouts: 3.43 us -> none  [per_device(): halves = totals.reshape(bins_total, 2, 2, quarter)]
    slice x1 -> x0, local copies, waits for them, and re-layouts: 3.23 us -> none  [per_device(): high = lax.index_in_dim(halves, 1, dim, keepdims=False)]
    select_n x2, other arithmetic: 0.16 us -> 1.64 us  [per_device(): send = jnp.where(mine == 1, low, high)]
    unnamed x8 -> x10, local copies, waits for them, and re-layouts: 2.25 us -> 2.25 us
where the time goes in v5:
time: 76.6 us; the launch traced here: 76.4 us
  waiting for transfers between devices  28.9 us (38%)
  starting transfers between devices  18.7 us (24%)
  Pallas kernels  11.3 us (15%)
  blocking collectives  7.62 us (10%)
  other arithmetic  5.38 us (7%)
  local copies, waits for them, and re-layouts  4.33 us (6%)
    ppermute x6, waiting for transfers between devices, halving_sum(): data = keep + lax.ppermute(send, axis, pairs)  18.7 us
    ppermute x6, starting transfers between devices, halving_sum(): data = keep + lax.ppermute(send, axis, pairs)  17.1 us
    pallas_call x1, Pallas kernels, per_device(): pl.pallas_call(kernel, grid_spec=grid_spec, out_shape=jax.ShapeDtypeStruc...  11.3 us
    ppermute x2, waiting for transfers between devices, per_device(): halves = keep + lax.ppermute(send, 'obs', pairs)  10.2 us
    all_gather x1, blocking collectives, per_device(): every_obs = lax.all_gather(observer_places, 'obs', axis=1, tiled=True)  7.62 us
    unnamed x10, local copies, waits for them, and re-layouts  2.25 us
    sort x1, other arithmetic, per_device(): inverse = jnp.argsort(segment_owner)  2.03 us
    select_n x2, other arithmetic, per_device(): send = jnp.where(mine == 1, low, high)  1.64 us
  transfers between devices with their start and end apart: 8, of which 8 were waited for; matrix products, arithmetic and copies ran while one was open for 3% of the time, Pallas kernels for 0%

profile of v5, /device:TPU:24, one launch (start us, length us, event | category | flops | bytes accessed | tf_op | source)
XLA Modules:
  0.0 76.4 jit_solution(9954794004434515958)
XLA Ops:
  0.0 0.8 %copy.13 = f32[3,256]{0,1:T(8,128)S(1)} copy(f32[3,256]{1,0:T(4,128)} %param.8) | data formatting | bytes 6144 | tf_op args[2]
  0.8 7.6 %all_gather.3 = f32[3,1024]{0,1:T(8,128)} all-gather(f32[3,256]{0,1:T(8,128)S(1)} %copy.13), channel_id=1, replica_groups=mesh['obs'=4,'pan'=64] {'obs'}, dimensions={1}, use_global_device_ids=true | all-gather | bytes 15360 | tf_op jit(solution)/shard_map/all_gather | solution.py:48
  8.4 1.3 %copy.95 = f32[1,3,512]{2,1,0:T(4,128)} copy(f32[1,3,512]{2,0,1:T(1,128)} %param.7) | data formatting | bytes 12288
  9.7 1.3 %copy.14.bins_ref = s32[8,4]{1,0:T(8,128)} copy(s32[8,4]{0,1:T(4,128)} %bitcast.108) | data formatting | bytes 256 | tf_op jit(solution)/shard_map/squeeze | solution.py:67
  11.1 11.3 %shard_map.64 = f32[4,384,256]{2,1,0:T(8,128)} custom-call(s32[8,4]{1,0:T(8,128)} %copy.14.bins_ref, f32[1024,3]{1,0:T(8,128)} %bitcast.99, f32[3,512]{1,0:T(4,128)} %bitcast.105, bf16[1024,512]{1,0:T(8,128)(2,1)} %bitcast.101, bf16[4,512,256]{2,1,0:T(8,128)(2,1)} %bitcast.102), custom_call_target="tpu_custom_call" | custom-call | tf_op jit(solution)/shard_map/pallas_call | solution.py:63
  22.4 0.0 copy-start
  22.4 1.6 %select_bitcast_fusion = f32[2,384,256]{2,1,0:T(8,128)S(1)} fusion(f32[2,2,384,256]{3,2,1,0:T(8,128)} %bitcast.97, pred[]{:T(512)S(6)} %eq.39), kind=kLoop, calls=%fused_computation.4 | loop fusion | flops 196608 | bytes 2359297 | tf_op jit(solution)/shard_map/jit(_where)/select_n | solution.py:75
  24.0 0.4 collective-permute-start
  24.4 0.0 copy-start.1
  24.4 1.9 %collective-permute-done = f32[2,384,256]{2,1,0:T(8,128)S(1)} collective-permute-done((f32[2,384,256]{2,1,0:T(8,128)S(1)}, f32[2,384,256]{2,1,0:T(8,128)S(1)}, u32[]{:S(2)}, u32[]{:S(2)}) %collective-permute-start) | collective-permute-done | bytes 786464 | tf_op jit(solution)/shard_map/ppermute | solution.py:77
  26.4 0.0 copy-done
  26.4 0.2 bitcast_add_fusion
  26.5 0.1 select_bitcast_fusion.1
  26.6 1.2 %collective-permute-start.1 = (f32[384,256]{1,0:T(8,128)S(1)}, f32[384,256]{1,0:T(8,128)S(1)}, u32[]{:S(2)}, u32[]{:S(2)}) collective-permute-start(f32[384,256]{1,0:T(8,128)S(1)} %select_bitcast_fusion.1), channel_id=1, source_target_pairs={{0,128},{64,192},{128,0},{192,64},{1,129},{65,193},{129,1},{193,65... | collective-permute-start | bytes 1179656 | tf_op jit(solution)/shard_map/ppermute | solution.py:77
  27.7 0.0 copy-done.1
  27.7 2.0 %sort.17 = (s32[64]{0:T(128)}, s32[64]{0:T(128)S(1)}) sort(s32[64]{0:T(128)S(1)} %copy-done.1, s32[64]{0:T(128)S(1)} %iota.4), dimensions={0}, to_apply=%region_0.1 | sort | flops 384 | bytes 1024 | tf_op jit(solution)/shard_map/jit(argsort)/sort | solution.py:82
  29.8 8.2 %collective-permute-done.1 = f32[384,256]{1,0:T(8,128)S(1)} collective-permute-done((f32[384,256]{1,0:T(8,128)S(1)}, f32[384,256]{1,0:T(8,128)S(1)}, u32[]{:S(2)}, u32[]{:S(2)}) %collective-permute-start.1) | collective-permute-done | bytes 393248 | tf_op jit(solution)/shard_map/ppermute | solution.py:77
  38.0 0.1 bitcast_add_fusion.1
  38.1 0.1 reshape.42
  38.2 0.6 gather_fusion
  38.8 0.1 fusion.14
  38.9 0.3 broadcast_select_fusion
  39.2 0.1 copy.91
  39.3 2.0 %collective-permute-start.2 = (f32[2,2,2,2,2,6,256]{6,4,3,2,1,0,5:T(2,128)S(1)}, f32[2,2,2,2,2,6,256]{6,4,3,2,1,0,5:T(2,128)S(1)}, u32[]{:S(2)}, u32[]{:S(2)}) collective-permute-start(f32[2,2,2,2,2,6,256]{6,4,3,2,1,0,5:T(2,128)S(1)} %bitcast.103), channel_id=1, source_target_pairs={{0,1},{1,0},{2,3},{3,2},{4,5},{5,4},{6,7},{7,6},{8,9},{9,8},{10,11... | collective-permute-start | bytes 589832 | tf_op jit(solution)/shard_map/ppermute | solution.py:101
  41.3 4.6 %collective-permute-done.2 = f32[2,2,2,2,2,6,256]{6,4,3,2,1,0,5:T(2,128)S(1)} collective-permute-done((f32[2,2,2,2,2,6,256]{6,4,3,2,1,0,5:T(2,128)S(1)}, f32[2,2,2,2,2,6,256]{6,4,3,2,1,0,5:T(2,128)S(1)}, u32[]{:S(2)}, u32[]{:S(2)}) %collective-permute-start.2) | collective-permute-done | bytes 196640 | tf_op jit(solution)/shard_map/ppermute | solution.py:101
  45.9 0.2 fusion.1
  46.1 0.1 fusion.2
  46.1 0.8 %collective-permute-start.3 = (f32[2,2,2,2,6,256]{5,3,2,1,0,4:T(2,128)S(1)}, f32[2,2,2,2,6,256]{5,3,2,1,0,4:T(2,128)S(1)}, u32[]{:S(2)}, u32[]{:S(2)}) collective-permute-start(f32[2,2,2,2,6,256]{5,3,2,1,0,4:T(2,128)S(1)} %fusion.2), channel_id=1, source_target_pairs={{0,8},{1,9},{2,10},{3,11},{4,12},{5,13},{6,14},{7,15},{8,0},{9,1},... | collective-permute-start | bytes 294920 | tf_op jit(solution)/shard_map/ppermute | solution.py:101
  47.0 3.9 %collective-permute-done.3 = f32[2,2,2,2,6,256]{5,3,2,1,0,4:T(2,128)S(1)} collective-permute-done((f32[2,2,2,2,6,256]{5,3,2,1,0,4:T(2,128)S(1)}, f32[2,2,2,2,6,256]{5,3,2,1,0,4:T(2,128)S(1)}, u32[]{:S(2)}, u32[]{:S(2)}) %collective-permute-start.3) | collective-permute-done | bytes 98336 | tf_op jit(solution)/shard_map/ppermute | solution.py:101
  50.8 0.1 fusion.4
  50.9 0.1 fusion.15
  51.0 3.4 %collective-permute-start.4 = (f32[2,2,2,6,256]{4,2,1,0,3:T(2,128)S(1)}, f32[2,2,2,6,256]{4,2,1,0,3:T(2,128)S(1)}, u32[]{:S(2)}, u32[]{:S(2)}) collective-permute-start(f32[2,2,2,6,256]{4,2,1,0,3:T(2,128)S(1)} %bitcast.104), channel_id=1, source_target_pairs={{0,2},{1,3},{2,0},{3,1},{4,6},{5,7},{6,4},{7,5},{8,10},{9,11},{10,... | collective-permute-start | bytes 147464 | tf_op jit(solution)/shard_map/ppermute | solution.py:101
  54.4 2.1 %collective-permute-done.4 = f32[2,2,2,6,256]{4,2,1,0,3:T(2,128)S(1)} collective-permute-done((f32[2,2,2,6,256]{4,2,1,0,3:T(2,128)S(1)}, f32[2,2,2,6,256]{4,2,1,0,3:T(2,128)S(1)}, u32[]{:S(2)}, u32[]{:S(2)}) %collective-permute-start.4) | collective-permute-done | bytes 49184 | tf_op jit(solution)/shard_map/ppermute | solution.py:101
  56.5 1.3 %collective-permute-start.5 = (f32[2,2,6,256]{3,1,0,2:T(2,128)S(1)}, f32[2,2,6,256]{3,1,0,2:T(2,128)S(1)}, u32[]{:S(2)}, u32[]{:S(2)}) collective-permute-start(f32[2,2,6,256]{3,1,0,2:T(2,128)S(1)} %fusion.7), channel_id=1, source_target_pairs={{0,16},{1,17},{2,18},{3,19},{4,20},{5,21},{6,22},{7,23},{8,24},{9,... | collective-permute-start | bytes 73736 | tf_op jit(solution)/shard_map/ppermute | solution.py:101
  57.9 4.1 %collective-permute-done.5 = f32[2,2,6,256]{3,1,0,2:T(2,128)S(1)} collective-permute-done((f32[2,2,6,256]{3,1,0,2:T(2,128)S(1)}, f32[2,2,6,256]{3,1,0,2:T(2,128)S(1)}, u32[]{:S(2)}, u32[]{:S(2)}) %collective-permute-start.5) | collective-permute-done | bytes 24608 | tf_op jit(solution)/shard_map/ppermute | solution.py:101
  62.0 6.8 %collective-permute-start.6 = (f32[2,6,256]{2,0,1:T(2,128)S(1)}, f32[2,6,256]{2,0,1:T(2,128)S(1)}, u32[]{:S(2)}, u32[]{:S(2)}) collective-permute-start(f32[2,6,256]{2,0,1:T(2,128)S(1)} %bitcast.106), channel_id=1, source_target_pairs={{0,4},{1,5},{2,6},{3,7},{4,0},{5,1},{6,2},{7,3},{8,12},{9,13},{10,... | collective-permute-start | bytes 36872 | tf_op jit(solution)/shard_map/ppermute | solution.py:101
  68.8 1.7 %collective-permute-done.6 = f32[2,6,256]{2,0,1:T(2,128)S(1)} collective-permute-done((f32[2,6,256]{2,0,1:T(2,128)S(1)}, f32[2,6,256]{2,0,1:T(2,128)S(1)}, u32[]{:S(2)}, u32[]{:S(2)}) %collective-permute-start.6) | collective-permute-done | bytes 12320 | tf_op jit(solution)/shard_map/ppermute | solution.py:101
  70.5 2.8 %collective-permute-start.7 = (f32[6,256]{1,0:T(8,128)S(1)}, f32[6,256]{1,0:T(8,128)S(1)}, u32[]{:S(2)}, u32[]{:S(2)}) collective-permute-start(f32[6,256]{1,0:T(8,128)S(1)} %bitcast.107), channel_id=1, source_target_pairs={{0,32},{1,33},{2,34},{3,35},{4,36},{5,37},{6,38},{7,39},{8,40},{9,... | collective-permute-start | bytes 18440 | tf_op jit(solution)/shard_map/ppermute | solution.py:101
  73.3 2.4 %collective-permute-done.7 = f32[6,256]{1,0:T(8,128)S(1)} collective-permute-done((f32[6,256]{1,0:T(8,128)S(1)}, f32[6,256]{1,0:T(8,128)S(1)}, u32[]{:S(2)}, u32[]{:S(2)}) %collective-permute-start.7) | collective-permute-done | bytes 6176 | tf_op jit(solution)/shard_map/ppermute | solution.py:101
  75.8 0.6 fusion.13
  (12 shorter events, 0.2 us)
Async XLA Ops:
  22.4 4.0 %copy-start = (f32[4,384,256]{2,1,0:T(8,128)S(1)}, f32[4,384,256]{2,1,0:T(8,128)}, u32[]{:S(2)}) copy-start(f32[4,384,256]{2,1,0:T(8,128)} %shard_map.64) | copy-start | bytes 4718596
  24.0 2.4 %collective-permute-start = (f32[2,384,256]{2,1,0:T(8,128)S(1)}, f32[2,384,256]{2,1,0:T(8,128)S(1)}, u32[]{:S(2)}, u32[]{:S(2)}) collective-permute-start(f32[2,384,256]{2,1,0:T(8,128)S(1)} %select_bitcast_fusion), channel_id=1, source_target_pairs={{0,64},{64,0},{128,192},{192,128},{1,65},{65,1},{129,193},{193,129... | collective-permute-start | bytes 2359304 | tf_op jit(solution)/shard_map/ppermute | solution.py:77
  24.4 3.3 %copy-start.1 = (s32[64]{0:T(128)S(1)}, s32[64]{0:T(128)}, u32[]{:S(2)}) copy-start(s32[64]{0:T(128)} %param.11) | copy-start | bytes 772
  26.6 11.5 %collective-permute-start.1 = (f32[384,256]{1,0:T(8,128)S(1)}, f32[384,256]{1,0:T(8,128)S(1)}, u32[]{:S(2)}, u32[]{:S(2)}) collective-permute-start(f32[384,256]{1,0:T(8,128)S(1)} %select_bitcast_fusion.1), channel_id=1, source_target_pairs={{0,128},{64,192},{128,0},{192,64},{1,129},{65,193},{129,1},{193,65... | collective-permute-start | bytes 1179656 | tf_op jit(solution)/shard_map/ppermute | solution.py:77
  39.3 6.6 %collective-permute-start.2 = (f32[2,2,2,2,2,6,256]{6,4,3,2,1,0,5:T(2,128)S(1)}, f32[2,2,2,2,2,6,256]{6,4,3,2,1,0,5:T(2,128)S(1)}, u32[]{:S(2)}, u32[]{:S(2)}) collective-permute-start(f32[2,2,2,2,2,6,256]{6,4,3,2,1,0,5:T(2,128)S(1)} %bitcast.103), channel_id=1, source_target_pairs={{0,1},{1,0},{2,3},{3,2},{4,5},{5,4},{6,7},{7,6},{8,9},{9,8},{10,11... | collective-permute-start | bytes 589832 | tf_op jit(solution)/shard_map/ppermute | solution.py:101
  46.1 4.7 %collective-permute-start.3 = (f32[2,2,2,2,6,256]{5,3,2,1,0,4:T(2,128)S(1)}, f32[2,2,2,2,6,256]{5,3,2,1,0,4:T(2,128)S(1)}, u32[]{:S(2)}, u32[]{:S(2)}) collective-permute-start(f32[2,2,2,2,6,256]{5,3,2,1,0,4:T(2,128)S(1)} %fusion.2), channel_id=1, source_target_pairs={{0,8},{1,9},{2,10},{3,11},{4,12},{5,13},{6,14},{7,15},{8,0},{9,1},... | collective-permute-start | bytes 294920 | tf_op jit(solution)/shard_map/ppermute | solution.py:101
  51.0 5.4 %collective-permute-start.4 = (f32[2,2,2,6,256]{4,2,1,0,3:T(2,128)S(1)}, f32[2,2,2,6,256]{4,2,1,0,3:T(2,128)S(1)}, u32[]{:S(2)}, u32[]{:S(2)}) collective-permute-start(f32[2,2,2,6,256]{4,2,1,0,3:T(2,128)S(1)} %bitcast.104), channel_id=1, source_target_pairs={{0,2},{1,3},{2,0},{3,1},{4,6},{5,7},{6,4},{7,5},{8,10},{9,11},{10,... | collective-permute-start | bytes 147464 | tf_op jit(solution)/shard_map/ppermute | solution.py:101
  56.5 5.4 %collective-permute-start.5 = (f32[2,2,6,256]{3,1,0,2:T(2,128)S(1)}, f32[2,2,6,256]{3,1,0,2:T(2,128)S(1)}, u32[]{:S(2)}, u32[]{:S(2)}) collective-permute-start(f32[2,2,6,256]{3,1,0,2:T(2,128)S(1)} %fusion.7), channel_id=1, source_target_pairs={{0,16},{1,17},{2,18},{3,19},{4,20},{5,21},{6,22},{7,23},{8,24},{9,... | collective-permute-start | bytes 73736 | tf_op jit(solution)/shard_map/ppermute | solution.py:101
  62.0 8.4 %collective-permute-start.6 = (f32[2,6,256]{2,0,1:T(2,128)S(1)}, f32[2,6,256]{2,0,1:T(2,128)S(1)}, u32[]{:S(2)}, u32[]{:S(2)}) collective-permute-start(f32[2,6,256]{2,0,1:T(2,128)S(1)} %bitcast.106), channel_id=1, source_target_pairs={{0,4},{1,5},{2,6},{3,7},{4,0},{5,1},{6,2},{7,3},{8,12},{9,13},{10,... | collective-permute-start | bytes 36872 | tf_op jit(solution)/shard_map/ppermute | solution.py:101
  70.5 5.2 %collective-permute-start.7 = (f32[6,256]{1,0:T(8,128)S(1)}, f32[6,256]{1,0:T(8,128)S(1)}, u32[]{:S(2)}, u32[]{:S(2)}) collective-permute-start(f32[6,256]{1,0:T(8,128)S(1)} %bitcast.107), channel_id=1, source_target_pairs={{0,32},{1,33},{2,34},{3,35},{4,36},{5,37},{6,38},{7,39},{8,40},{9,... | collective-permute-start | bytes 18440 | tf_op jit(solution)/shard_map/ppermute | solution.py:101

commit v6 on v5

--- a/solution.py
+++ b/solution.py
@@ -81,7 +81,8 @@
     arranged = reduced.reshape(segment_count, seg_len, reduced.shape[1])
     inverse = jnp.argsort(segment_owner)
     arranged = arranged[inverse]
-    return halving_sum(arranged, "pan", (0, 3, 1, 4, 2, 5))
+    gathered = lax.all_to_all(arranged, "pan", 0, 0, tiled=True)
+    return jnp.sum(gathered, axis=0)
 
 
 def halving_sum(data, axis, bit_order):

time: 76.6 us -> 73.1 us (0.954)
  blocking collectives: 7.62 us -> 40.8 us
  waiting for transfers between devices: 28.9 us -> 10.2 us
  starting transfers between devices: 18.7 us -> 1.61 us
  other arithmetic: 5.38 us -> 4.6 us
    all_to_all x0 -> x1, blocking collectives: none -> 33.2 us  [per_device(): gathered = lax.all_to_all(arranged, 'pan', 0, 0, tiled=True)]
    ppermute x6 -> x0, waiting for transfers between devices: 18.7 us -> none  [halving_sum(): data = keep + lax.ppermute(send, axis, pairs)]
    ppermute x6 -> x0, starting transfers between devices: 17.1 us -> none  [halving_sum(): data = keep + lax.ppermute(send, axis, pairs)]
    add x6 -> x0, other arithmetic: 0.96 us -> none  [halving_sum(): data = keep + lax.ppermute(send, axis, pairs)]
    unnamed x10 -> x6, local copies, waits for them, and re-layouts: 2.25 us -> 2.11 us
  transfers between devices with their start and end apart: 8 -> 2, of which waited for: 8 -> 2; matrix products, arithmetic and copies ran while one was open for 3% -> 3% of each run, Pallas kernels for 0% -> 0%
where the time goes in v6:
time: 73.1 us; the launch traced here: 72.7 us
  blocking collectives  40.8 us (56%)
  Pallas kernels  11.3 us (15%)
  waiting for transfers between devices  10.2 us (14%)
  other arithmetic  4.6 us (6%)
  local copies, waits for them, and re-layouts  4.15 us (6%)
  starting transfers between devices  1.61 us (2%)
    all_to_all x1, blocking collectives, per_device(): gathered = lax.all_to_all(arranged, 'pan', 0, 0, tiled=True)  33.2 us
    pallas_call x1, Pallas kernels, per_device(): pl.pallas_call(kernel, grid_spec=grid_spec, out_shape=jax.ShapeDtypeStruc...  11.3 us
    ppermute x2, waiting for transfers between devices, per_device(): halves = keep + lax.ppermute(send, 'obs', pairs)  10.2 us
    all_gather x1, blocking collectives, per_device(): every_obs = lax.all_gather(observer_places, 'obs', axis=1, tiled=True)  7.62 us
    unnamed x6, local copies, waits for them, and re-layouts  2.11 us
    sort x1, other arithmetic, per_device(): inverse = jnp.argsort(segment_owner)  2.03 us
    select_n x2, other arithmetic, per_device(): send = jnp.where(mine == 1, low, high)  1.65 us
    ppermute x2, starting transfers between devices, per_device(): halves = keep + lax.ppermute(send, 'obs', pairs)  1.61 us
  transfers between devices with their start and end apart: 2, of which 2 were waited for; matrix products, arithmetic and copies ran while one was open for 3% of the time, Pallas kernels for 0%

profile of v6, /device:TPU:24, one launch (start us, length us, event | category | flops | bytes accessed | tf_op | source)
XLA Modules:
  0.0 72.7 jit_solution(7444169712640246338)
XLA Ops:
  0.0 0.8 %copy.13 = f32[3,256]{0,1:T(8,128)S(1)} copy(f32[3,256]{1,0:T(4,128)} %param.8) | data formatting | bytes 6144 | tf_op args[2]
  0.8 7.6 %all_gather.3 = f32[3,1024]{0,1:T(8,128)} all-gather(f32[3,256]{0,1:T(8,128)S(1)} %copy.13), channel_id=1, replica_groups=mesh['obs'=4,'pan'=64] {'obs'}, dimensions={1}, use_global_device_ids=true | all-gather | bytes 15360 | tf_op jit(solution)/shard_map/all_gather | solution.py:48
  8.4 1.3 %copy.21 = f32[1,3,512]{2,1,0:T(4,128)} copy(f32[1,3,512]{2,0,1:T(1,128)} %param.7) | data formatting | bytes 12288
  9.7 1.3 %copy.14.bins_ref = s32[8,4]{1,0:T(8,128)} copy(s32[8,4]{0,1:T(4,128)} %bitcast.34) | data formatting | bytes 256 | tf_op jit(solution)/shard_map/squeeze | solution.py:67
  11.1 11.3 %shard_map.64 = f32[4,384,256]{2,1,0:T(8,128)} custom-call(s32[8,4]{1,0:T(8,128)} %copy.14.bins_ref, f32[1024,3]{1,0:T(8,128)} %bitcast.30, f32[3,512]{1,0:T(4,128)} %bitcast.33, bf16[1024,512]{1,0:T(8,128)(2,1)} %bitcast.31, bf16[4,512,256]{2,1,0:T(8,128)(2,1)} %bitcast.32), custom_call_target="tpu_custom_call" | custom-call | tf_op jit(solution)/shard_map/pallas_call | solution.py:63
  22.4 0.0 copy-start
  22.4 1.6 %select_bitcast_fusion = f32[2,384,256]{2,1,0:T(8,128)S(1)} fusion(f32[2,2,384,256]{3,2,1,0:T(8,128)} %bitcast.28, pred[]{:T(512)S(6)} %eq.9), kind=kLoop, calls=%fused_computation.4 | loop fusion | flops 196608 | bytes 2359297 | tf_op jit(solution)/shard_map/jit(_where)/select_n | solution.py:75
  24.0 0.4 collective-permute-start
  24.4 0.0 copy-start.1
  24.4 1.9 %collective-permute-done = f32[2,384,256]{2,1,0:T(8,128)S(1)} collective-permute-done((f32[2,384,256]{2,1,0:T(8,128)S(1)}, f32[2,384,256]{2,1,0:T(8,128)S(1)}, u32[]{:S(2)}, u32[]{:S(2)}) %collective-permute-start) | collective-permute-done | bytes 786464 | tf_op jit(solution)/shard_map/ppermute | solution.py:77
  26.4 0.0 copy-done
  26.4 0.2 bitcast_add_fusion
  26.5 0.1 select_bitcast_fusion.1
  26.6 1.2 %collective-permute-start.1 = (f32[384,256]{1,0:T(8,128)S(1)}, f32[384,256]{1,0:T(8,128)S(1)}, u32[]{:S(2)}, u32[]{:S(2)}) collective-permute-start(f32[384,256]{1,0:T(8,128)S(1)} %select_bitcast_fusion.1), channel_id=1, source_target_pairs={{0,128},{64,192},{128,0},{192,64},{1,129},{65,193},{129,1},{193,65... | collective-permute-start | bytes 1179656 | tf_op jit(solution)/shard_map/ppermute | solution.py:77
  27.8 0.0 copy-done.1
  27.8 2.0 %sort.17 = (s32[64]{0:T(128)}, s32[64]{0:T(128)S(1)}) sort(s32[64]{0:T(128)S(1)} %copy-done.1, s32[64]{0:T(128)S(1)} %iota.4), dimensions={0}, to_apply=%region_0.1 | sort | flops 384 | bytes 1024 | tf_op jit(solution)/shard_map/jit(argsort)/sort | solution.py:82
  29.8 8.2 %collective-permute-done.1 = f32[384,256]{1,0:T(8,128)S(1)} collective-permute-done((f32[384,256]{1,0:T(8,128)S(1)}, f32[384,256]{1,0:T(8,128)S(1)}, u32[]{:S(2)}, u32[]{:S(2)}) %collective-permute-start.1) | collective-permute-done | bytes 393248 | tf_op jit(solution)/shard_map/ppermute | solution.py:77
  38.0 0.1 bitcast_add_fusion.1
  38.1 0.1 reshape.15
  38.2 0.6 gather_fusion
  38.8 33.2 %all_to_all.5 = f32[64,6,256]{2,1,0:T(8,128)S(1)} all-to-all(f32[64,6,256]{2,1,0:T(8,128)S(1)} %gather_fusion), channel_id=1, replica_groups=mesh['obs'=4,'pan'=64] {'pan'}, dimensions={0} | all-to-all | bytes 786432 | tf_op jit(solution)/shard_map/all_to_all | solution.py:84
  72.0 0.7 reduce_sum.9
  (3 shorter events, 0.0 us)
Async XLA Ops:
  22.4 4.0 %copy-start = (f32[4,384,256]{2,1,0:T(8,128)S(1)}, f32[4,384,256]{2,1,0:T(8,128)}, u32[]{:S(2)}) copy-start(f32[4,384,256]{2,1,0:T(8,128)} %shard_map.64) | copy-start | bytes 4718596
  24.0 2.4 %collective-permute-start = (f32[2,384,256]{2,1,0:T(8,128)S(1)}, f32[2,384,256]{2,1,0:T(8,128)S(1)}, u32[]{:S(2)}, u32[]{:S(2)}) collective-permute-start(f32[2,384,256]{2,1,0:T(8,128)S(1)} %select_bitcast_fusion), channel_id=1, source_target_pairs={{0,64},{64,0},{128,192},{192,128},{1,65},{65,1},{129,193},{193,129... | collective-permute-start | bytes 2359304 | tf_op jit(solution)/shard_map/ppermute | solution.py:77
  24.4 3.3 %copy-start.1 = (s32[64]{0:T(128)S(1)}, s32[64]{0:T(128)}, u32[]{:S(2)}) copy-start(s32[64]{0:T(128)} %param.11) | copy-start | bytes 772
  26.6 11.5 %collective-permute-start.1 = (f32[384,256]{1,0:T(8,128)S(1)}, f32[384,256]{1,0:T(8,128)S(1)}, u32[]{:S(2)}, u32[]{:S(2)}) collective-permute-start(f32[384,256]{1,0:T(8,128)S(1)} %select_bitcast_fusion.1), channel_id=1, source_target_pairs={{0,128},{64,192},{128,0},{192,64},{1,129},{65,193},{129,1},{193,65... | collective-permute-start | bytes 1179656 | tf_op jit(solution)/shard_map/ppermute | solution.py:77

commit v7 on v5

--- a/solution.py
+++ b/solution.py
@@ -81,7 +81,74 @@
     arranged = reduced.reshape(segment_count, seg_len, reduced.shape[1])
     inverse = jnp.argsort(segment_owner)
     arranged = arranged[inverse]
-    return halving_sum(arranged, "pan", (0, 3, 1, 4, 2, 5))
+    rows = -(-seg_len // 8) * 8
+    padded = jnp.pad(arranged, ((0, 0), (0, rows - seg_len), (0, 0)))
+    return exchange_sum(padded)[:seg_len]
+
+
+def exchange_kernel(x_ref, out_ref, slots, send_sem, recv_sem):
+    count = x_ref.shape[0]
+    me = lax.axis_index("pan")
+
+    def send(d, carry):
+        target = lax.rem(me + d, count)
+        pltpu.make_async_remote_copy(
+            src_ref=x_ref.at[target],
+            dst_ref=slots.at[me],
+            send_sem=send_sem.at[target],
+            recv_sem=recv_sem.at[me],
+            device_id={"pan": target},
+            device_id_type=pl.DeviceIdType.MESH,
+        ).start()
+        return carry
+
+    lax.fori_loop(1, count, send, 0)
+    total = x_ref[me]
+
+    def gather(d, total):
+        source = lax.rem(me + count - d, count)
+        pltpu.make_async_remote_copy(
+            src_ref=x_ref.at[source],
+            dst_ref=slots.at[source],
+            send_sem=send_sem.at[source],
+            recv_sem=recv_sem.at[source],
+            device_id={"pan": source},
+            device_id_type=pl.DeviceIdType.MESH,
+        ).wait_recv()
+        return total + slots[source]
+
+    total = lax.fori_loop(1, count, gather, total)
+
+    def drain(d, carry):
+        target = lax.rem(me + d, count)
+        pltpu.make_async_remote_copy(
+            src_ref=x_ref.at[target],
+            dst_ref=slots.at[me],
+            send_sem=send_sem.at[target],
+            recv_sem=recv_sem.at[me],
+            device_id={"pan": target},
+            device_id_type=pl.DeviceIdType.MESH,
+        ).wait_send()
+        return carry
+
+    lax.fori_loop(1, count, drain, 0)
+    out_ref[...] = total
+
+
+def exchange_sum(data):
+    count = data.shape[0]
+    return pl.pallas_call(
+        exchange_kernel,
+        out_shape=jax.ShapeDtypeStruct(data.shape[1:], data.dtype),
+        in_specs=[pl.BlockSpec(memory_space=pltpu.VMEM)],
+        out_specs=pl.BlockSpec(memory_space=pltpu.VMEM),
+        scratch_shapes=[
+            pltpu.VMEM(data.shape, data.dtype),
+            pltpu.SemaphoreType.DMA((count,)),
+            pltpu.SemaphoreType.DMA((count,)),
+        ],
+        compiler_params=pltpu.CompilerParams(has_side_effects=True),
+    )(data)
 
 
 def halving_sum(data, axis, bit_order):

time: 76.6 us -> 77.3 us (level)
  Pallas kernels: 11.3 us -> 47.3 us
  waiting for transfers between devices: 28.9 us -> 10.2 us
  starting transfers between devices: 18.7 us -> 1.61 us
  local copies, waits for them, and re-layouts: 4.33 us -> 6.27 us
  other arithmetic: 5.38 us -> 3.92 us
    pallas_call x0 -> x1, Pallas kernels: none -> 36 us  [exchange_sum(): pl.pallas_call(exchange_kernel, out_shape=jax.ShapeDtypeStruct(data.shape...]
    ppermute x6 -> x0, waiting for transfers between devices: 18.7 us -> none  [halving_sum(): data = keep + lax.ppermute(send, axis, pairs)]
    ppermute x6 -> x0, starting transfers between devices: 17.1 us -> none  [halving_sum(): data = keep + lax.ppermute(send, axis, pairs)]
    unnamed x10 -> x7, local copies, waits for them, and re-layouts: 2.25 us -> 3.41 us
    add x6 -> x0, other arithmetic: 0.96 us -> none  [halving_sum(): data = keep + lax.ppermute(send, axis, pairs)]
    pad x0 -> x1, local copies, waits for them, and re-layouts: none -> 0.83 us  [per_device(): padded = jnp.pad(arranged, ((0, 0), (0, rows - seg_len), (0, 0)))]
  transfers between devices with their start and end apart: 8 -> 2, of which waited for: 8 -> 2; matrix products, arithmetic and copies ran while one was open for 3% -> 3% of each run, Pallas kernels for 0% -> 0%
where the time goes in v7:
time: 77.3 us; the launch traced here: 76.9 us
  Pallas kernels  47.3 us (61%)
  waiting for transfers between devices  10.2 us (13%)
  blocking collectives  7.62 us (10%)
  local copies, waits for them, and re-layouts  6.27 us (8%)
  other arithmetic  3.92 us (5%)
  starting transfers between devices  1.61 us (2%)
    pallas_call x1, Pallas kernels, exchange_sum(): pl.pallas_call(exchange_kernel, out_shape=jax.ShapeDtypeStruct(data.shape...  36 us
    pallas_call x1, Pallas kernels, per_device(): pl.pallas_call(kernel, grid_spec=grid_spec, out_shape=jax.ShapeDtypeStruc...  11.3 us
    ppermute x2, waiting for transfers between devices, per_device(): halves = keep + lax.ppermute(send, 'obs', pairs)  10.2 us
    all_gather x1, blocking collectives, per_device(): every_obs = lax.all_gather(observer_places, 'obs', axis=1, tiled=True)  7.62 us
    unnamed x7, local copies, waits for them, and re-layouts  3.41 us
    sort x1, other arithmetic, per_device(): inverse = jnp.argsort(segment_owner)  2.03 us
    select_n x2, other arithmetic, per_device(): send = jnp.where(mine == 1, low, high)  1.65 us
    ppermute x2, starting transfers between devices, per_device(): halves = keep + lax.ppermute(send, 'obs', pairs)  1.61 us
  transfers between devices with their start and end apart: 2, of which 2 were waited for; matrix products, arithmetic and copies ran while one was open for 3% of the time, Pallas kernels for 0%

profile of v7, /device:TPU:24, one launch (start us, length us, event | category | flops | bytes accessed | tf_op | source)
XLA Modules:
  0.0 76.9 jit_solution(2579353899317260949)
XLA Ops:
  0.0 0.8 %copy.13 = f32[3,256]{0,1:T(8,128)S(1)} copy(f32[3,256]{1,0:T(4,128)} %param.8) | data formatting | bytes 6144 | tf_op args[2]
  0.8 7.6 %all_gather.3 = f32[3,1024]{0,1:T(8,128)} all-gather(f32[3,256]{0,1:T(8,128)S(1)} %copy.13), channel_id=1, replica_groups=mesh['obs'=4,'pan'=64] {'obs'}, dimensions={1}, use_global_device_ids=true | all-gather | bytes 15360 | tf_op jit(solution)/shard_map/all_gather | solution.py:48
  8.4 1.3 %copy.21 = f32[1,3,512]{2,1,0:T(4,128)} copy(f32[1,3,512]{2,0,1:T(1,128)} %param.7) | data formatting | bytes 12288
  9.7 1.3 %copy.14.bins_ref = s32[8,4]{1,0:T(8,128)} copy(s32[8,4]{0,1:T(4,128)} %bitcast.36) | data formatting | bytes 256 | tf_op jit(solution)/shard_map/squeeze | solution.py:67
  11.1 11.3 %shard_map.64 = f32[4,384,256]{2,1,0:T(8,128)} custom-call(s32[8,4]{1,0:T(8,128)} %copy.14.bins_ref, f32[1024,3]{1,0:T(8,128)} %bitcast.31, f32[3,512]{1,0:T(4,128)} %bitcast.34, bf16[1024,512]{1,0:T(8,128)(2,1)} %bitcast.32, bf16[4,512,256]{2,1,0:T(8,128)(2,1)} %bitcast.33), custom_call_target="tpu_custom_call" | custom-call | tf_op jit(solution)/shard_map/pallas_call | solution.py:63
  22.4 0.0 copy-start
  22.4 1.6 %select_bitcast_fusion = f32[2,384,256]{2,1,0:T(8,128)S(1)} fusion(f32[2,2,384,256]{3,2,1,0:T(8,128)} %bitcast.29, pred[]{:T(512)S(6)} %eq.9), kind=kLoop, calls=%fused_computation.4 | loop fusion | flops 196608 | bytes 2359297 | tf_op jit(solution)/shard_map/jit(_where)/select_n | solution.py:75
  24.0 0.4 collective-permute-start
  24.4 0.0 copy-start.1
  24.4 1.9 %collective-permute-done = f32[2,384,256]{2,1,0:T(8,128)S(1)} collective-permute-done((f32[2,384,256]{2,1,0:T(8,128)S(1)}, f32[2,384,256]{2,1,0:T(8,128)S(1)}, u32[]{:S(2)}, u32[]{:S(2)}) %collective-permute-start) | collective-permute-done | bytes 786464 | tf_op jit(solution)/shard_map/ppermute | solution.py:77
  26.4 0.0 copy-done
  26.4 0.2 bitcast_add_fusion
  26.5 0.1 select_bitcast_fusion.1
  26.6 1.2 %collective-permute-start.1 = (f32[384,256]{1,0:T(8,128)S(1)}, f32[384,256]{1,0:T(8,128)S(1)}, u32[]{:S(2)}, u32[]{:S(2)}) collective-permute-start(f32[384,256]{1,0:T(8,128)S(1)} %select_bitcast_fusion.1), channel_id=1, source_target_pairs={{0,128},{64,192},{128,0},{192,64},{1,129},{65,193},{129,1},{193,65... | collective-permute-start | bytes 1179656 | tf_op jit(solution)/shard_map/ppermute | solution.py:77
  27.8 0.0 copy-done.1
  27.8 2.0 %sort.17 = (s32[64]{0:T(128)}, s32[64]{0:T(128)S(1)}) sort(s32[64]{0:T(128)S(1)} %copy-done.1, s32[64]{0:T(128)S(1)} %iota.4), dimensions={0}, to_apply=%region_0.1 | sort | flops 384 | bytes 1024 | tf_op jit(solution)/shard_map/jit(argsort)/sort | solution.py:82
  29.8 8.2 %collective-permute-done.1 = f32[384,256]{1,0:T(8,128)S(1)} collective-permute-done((f32[384,256]{1,0:T(8,128)S(1)}, f32[384,256]{1,0:T(8,128)S(1)}, u32[]{:S(2)}, u32[]{:S(2)}) %collective-permute-start.1) | collective-permute-done | bytes 393248 | tf_op jit(solution)/shard_map/ppermute | solution.py:77
  38.0 0.1 bitcast_add_fusion.1
  38.1 0.1 reshape.15
  38.2 0.6 gather_fusion
  38.8 0.8 %pad.4.x_ref = f32[64,8,256]{2,1,0:T(8,128)} pad(f32[64,6,256]{2,1,0:T(8,128)S(1)} %gather_fusion, f32[]{:T(128)} %constant.14.clone.1), padding=0_0x0_2x0_0 | pad | bytes 917508 | tf_op jit(solution)/shard_map/jit(_pad)/pad | solution.py:85
  39.6 36.0 %shard_map.65 = f32[8,256]{1,0:T(8,128)} custom-call(f32[64,8,256]{2,1,0:T(8,128)} %pad.4.x_ref), custom_call_target="tpu_custom_call" | custom-call | tf_op jit(solution)/shard_map/pallas_call | solution.py:140
  75.6 1.3 %copy.23 = f32[6,256]{1,0:T(8,128)} copy(f32[6,256]{1,0:T(8,128)} %bitcast.35) | data formatting | bytes 12288
  (3 shorter events, 0.0 us)
Async XLA Ops:
  22.4 4.0 %copy-start = (f32[4,384,256]{2,1,0:T(8,128)S(1)}, f32[4,384,256]{2,1,0:T(8,128)}, u32[]{:S(2)}) copy-start(f32[4,384,256]{2,1,0:T(8,128)} %shard_map.64) | copy-start | bytes 4718596
  24.0 2.4 %collective-permute-start = (f32[2,384,256]{2,1,0:T(8,128)S(1)}, f32[2,384,256]{2,1,0:T(8,128)S(1)}, u32[]{:S(2)}, u32[]{:S(2)}) collective-permute-start(f32[2,384,256]{2,1,0:T(8,128)S(1)} %select_bitcast_fusion), channel_id=1, source_target_pairs={{0,64},{64,0},{128,192},{192,128},{1,65},{65,1},{129,193},{193,129... | collective-permute-start | bytes 2359304 | tf_op jit(solution)/shard_map/ppermute | solution.py:77
  24.4 3.3 %copy-start.1 = (s32[64]{0:T(128)S(1)}, s32[64]{0:T(128)}, u32[]{:S(2)}) copy-start(s32[64]{0:T(128)} %param.11) | copy-start | bytes 772
  26.6 11.5 %collective-permute-start.1 = (f32[384,256]{1,0:T(8,128)S(1)}, f32[384,256]{1,0:T(8,128)S(1)}, u32[]{:S(2)}, u32[]{:S(2)}) collective-permute-start(f32[384,256]{1,0:T(8,128)S(1)} %select_bitcast_fusion.1), channel_id=1, source_target_pairs={{0,128},{64,192},{128,0},{192,64},{1,129},{65,193},{129,1},{193,65... | collective-permute-start | bytes 1179656 | tf_op jit(solution)/shard_map/ppermute | solution.py:77

commit v8 on v5

--- a/solution.py
+++ b/solution.py
@@ -81,7 +81,93 @@
     arranged = reduced.reshape(segment_count, seg_len, reduced.shape[1])
     inverse = jnp.argsort(segment_owner)
     arranged = arranged[inverse]
-    return halving_sum(arranged, "pan", (0, 3, 1, 4, 2, 5))
+    rows = -(-seg_len // 8) * 8
+    padded = jnp.pad(arranged, ((0, 0), (0, rows - seg_len), (0, 0)))
+    return exchange_sum(padded, 8)[:seg_len]
+
+
+def exchange_kernel(x_ref, out_ref, first, mid, second, sems):
+    inner, outer = x_ref.shape[0], x_ref.shape[1]
+    me = lax.axis_index("pan")
+    my_g = me // inner
+    my_z = lax.rem(me, inner)
+
+    def first_copy(zt, zs):
+        return pltpu.make_async_remote_copy(
+            src_ref=x_ref.at[zt],
+            dst_ref=first.at[zs],
+            send_sem=sems.at[0, zt],
+            recv_sem=sems.at[1, zs],
+            device_id={"pan": my_g * inner + zt},
+            device_id_type=pl.DeviceIdType.MESH,
+        )
+
+    def second_copy(gt, gs):
+        return pltpu.make_async_remote_copy(
+            src_ref=mid.at[gt],
+            dst_ref=second.at[gs],
+            send_sem=sems.at[2, gt],
+            recv_sem=sems.at[3, gs],
+            device_id={"pan": gt * inner + my_z},
+            device_id_type=pl.DeviceIdType.MESH,
+        )
+
+    def send_first(d, carry):
+        first_copy(lax.rem(my_z + d, inner), my_z).start()
+        return carry
+
+    lax.fori_loop(1, inner, send_first, 0)
+
+    def take_first(d, total):
+        source = lax.rem(my_z + inner - d, inner)
+        first_copy(source, source).wait_recv()
+        return total + first[source]
+
+    mid[...] = lax.fori_loop(1, inner, take_first, x_ref[my_z])
+
+    def send_second(d, carry):
+        second_copy(lax.rem(my_g + d, outer), my_g).start()
+        return carry
+
+    lax.fori_loop(1, outer, send_second, 0)
+
+    def take_second(d, total):
+        source = lax.rem(my_g + outer - d, outer)
+        second_copy(source, source).wait_recv()
+        return total + second[source]
+
+    total = lax.fori_loop(1, outer, take_second, mid[my_g])
+
+    def drain_first(d, carry):
+        first_copy(lax.rem(my_z + d, inner), my_z).wait_send()
+        return carry
+
+    def drain_second(d, carry):
+        second_copy(lax.rem(my_g + d, outer), my_g).wait_send()
+        return carry
+
+    lax.fori_loop(1, inner, drain_first, 0)
+    lax.fori_loop(1, outer, drain_second, 0)
+    out_ref[...] = total
+
+
+def exchange_sum(data, inner):
+    count = data.shape[0]
+    outer = count // inner
+    grouped = data.reshape((outer, inner) + data.shape[1:]).swapaxes(0, 1)
+    return pl.pallas_call(
+        exchange_kernel,
+        out_shape=jax.ShapeDtypeStruct(data.shape[1:], data.dtype),
+        in_specs=[pl.BlockSpec(memory_space=pltpu.VMEM)],
+        out_specs=pl.BlockSpec(memory_space=pltpu.VMEM),
+        scratch_shapes=[
+            pltpu.VMEM(grouped.shape, data.dtype),
+            pltpu.VMEM((outer,) + data.shape[1:], data.dtype),
+            pltpu.VMEM((outer,) + data.shape[1:], data.dtype),
+            pltpu.SemaphoreType.DMA((4, max(inner, outer))),
+        ],
+        compiler_params=pltpu.CompilerParams(has_side_effects=True),
+    )(grouped)
 
 
 def halving_sum(data, axis, bit_order):

time: 76.6 us -> 80.9 us (1.056); the launches traced: 76.4 us -> 79.6 us
  Pallas kernels: 11.3 us -> 50 us
  waiting for transfers between devices: 28.9 us -> 10.2 us
  starting transfers between devices: 18.7 us -> 1.61 us
  local copies, waits for them, and re-layouts: 4.33 us -> 6.31 us
  other arithmetic: 5.38 us -> 3.92 us
    pallas_call x0 -> x1, Pallas kernels: none -> 38.6 us  [exchange_sum(): pl.pallas_call(exchange_kernel, out_shape=jax.ShapeDtypeStruct(data.shape...]
    ppermute x6 -> x0, waiting for transfers between devices: 18.7 us -> none  [halving_sum(): data = keep + lax.ppermute(send, axis, pairs)]
    ppermute x6 -> x0, starting transfers between devices: 17.1 us -> none  [halving_sum(): data = keep + lax.ppermute(send, axis, pairs)]
    unnamed x10 -> x7, local copies, waits for them, and re-layouts: 2.25 us -> 3.41 us
    add x6 -> x0, other arithmetic: 0.96 us -> none  [halving_sum(): data = keep + lax.ppermute(send, axis, pairs)]
    reshape x0 -> x1, local copies, waits for them, and re-layouts: none -> 0.83 us  [exchange_sum(): grouped = data.reshape((outer, inner) + data.shape[1:]).swapaxes(0, 1)]
  transfers between devices with their start and end apart: 8 -> 2, of which waited for: 8 -> 2; matrix products, arithmetic and copies ran while one was open for 3% -> 3% of each run, Pallas kernels for 0% -> 0%
where the time goes in v8:
time: 80.9 us; the launch traced here: 79.6 us
  Pallas kernels  50 us (62%)
  waiting for transfers between devices  10.2 us (13%)
  blocking collectives  7.62 us (9%)
  local copies, waits for them, and re-layouts  6.31 us (8%)
  other arithmetic  3.92 us (5%)
  starting transfers between devices  1.61 us (2%)
    pallas_call x1, Pallas kernels, exchange_sum(): pl.pallas_call(exchange_kernel, out_shape=jax.ShapeDtypeStruct(data.shape...  38.6 us
    pallas_call x1, Pallas kernels, per_device(): pl.pallas_call(kernel, grid_spec=grid_spec, out_shape=jax.ShapeDtypeStruc...  11.3 us
    ppermute x2, waiting for transfers between devices, per_device(): halves = keep + lax.ppermute(send, 'obs', pairs)  10.2 us
    all_gather x1, blocking collectives, per_device(): every_obs = lax.all_gather(observer_places, 'obs', axis=1, tiled=True)  7.62 us
    unnamed x7, local copies, waits for them, and re-layouts  3.41 us
    sort x1, other arithmetic, per_device(): inverse = jnp.argsort(segment_owner)  2.03 us
    select_n x2, other arithmetic, per_device(): send = jnp.where(mine == 1, low, high)  1.65 us
  transfers between devices with their start and end apart: 2, of which 2 were waited for; matrix products, arithmetic and copies ran while one was open for 3% of the time, Pallas kernels for 0%

profile of v8, /device:TPU:24, one launch (start us, length us, event | category | flops | bytes accessed | tf_op | source)
XLA Modules:
  0.0 79.6 jit_solution(11762326566084591370)
XLA Ops:
  0.0 0.8 %copy.13 = f32[3,256]{0,1:T(8,128)S(1)} copy(f32[3,256]{1,0:T(4,128)} %param.8) | data formatting | bytes 6144 | tf_op args[2]
  0.8 7.6 %all_gather.3 = f32[3,1024]{0,1:T(8,128)} all-gather(f32[3,256]{0,1:T(8,128)S(1)} %copy.13), channel_id=1, replica_groups=mesh['obs'=4,'pan'=64] {'obs'}, dimensions={1}, use_global_device_ids=true | all-gather | bytes 15360 | tf_op jit(solution)/shard_map/all_gather | solution.py:48
  8.4 1.3 %copy.24 = f32[1,3,512]{2,1,0:T(4,128)} copy(f32[1,3,512]{2,0,1:T(1,128)} %param.7) | data formatting | bytes 12288
  9.7 1.3 %copy.14.bins_ref = s32[8,4]{1,0:T(8,128)} copy(s32[8,4]{0,1:T(4,128)} %bitcast.42) | data formatting | bytes 256 | tf_op jit(solution)/shard_map/squeeze | solution.py:67
  11.1 11.3 %shard_map.64 = f32[4,384,256]{2,1,0:T(8,128)} custom-call(s32[8,4]{1,0:T(8,128)} %copy.14.bins_ref, f32[1024,3]{1,0:T(8,128)} %bitcast.35, f32[3,512]{1,0:T(4,128)} %bitcast.40, bf16[1024,512]{1,0:T(8,128)(2,1)} %bitcast.38, bf16[4,512,256]{2,1,0:T(8,128)(2,1)} %bitcast.39), custom_call_target="tpu_custom_call" | custom-call | tf_op jit(solution)/shard_map/pallas_call | solution.py:63
  22.4 0.0 copy-start
  22.4 1.6 %select_bitcast_fusion = f32[2,384,256]{2,1,0:T(8,128)S(1)} fusion(f32[2,2,384,256]{3,2,1,0:T(8,128)} %bitcast.33, pred[]{:T(512)S(6)} %eq.9), kind=kLoop, calls=%fused_computation.4 | loop fusion | flops 196608 | bytes 2359297 | tf_op jit(solution)/shard_map/jit(_where)/select_n | solution.py:75
  24.0 0.4 collective-permute-start
  24.4 0.0 copy-start.1
  24.4 1.9 %collective-permute-done = f32[2,384,256]{2,1,0:T(8,128)S(1)} collective-permute-done((f32[2,384,256]{2,1,0:T(8,128)S(1)}, f32[2,384,256]{2,1,0:T(8,128)S(1)}, u32[]{:S(2)}, u32[]{:S(2)}) %collective-permute-start) | collective-permute-done | bytes 786464 | tf_op jit(solution)/shard_map/ppermute | solution.py:77
  26.4 0.0 copy-done
  26.4 0.2 bitcast_add_fusion
  26.5 0.1 select_bitcast_fusion.1
  26.6 1.2 %collective-permute-start.1 = (f32[384,256]{1,0:T(8,128)S(1)}, f32[384,256]{1,0:T(8,128)S(1)}, u32[]{:S(2)}, u32[]{:S(2)}) collective-permute-start(f32[384,256]{1,0:T(8,128)S(1)} %select_bitcast_fusion.1), channel_id=1, source_target_pairs={{0,128},{64,192},{128,0},{192,64},{1,129},{65,193},{129,1},{193,65... | collective-permute-start | bytes 1179656 | tf_op jit(solution)/shard_map/ppermute | solution.py:77
  27.8 0.0 copy-done.1
  27.8 2.0 %sort.17 = (s32[64]{0:T(128)}, s32[64]{0:T(128)S(1)}) sort(s32[64]{0:T(128)S(1)} %copy-done.1, s32[64]{0:T(128)S(1)} %iota.4), dimensions={0}, to_apply=%region_0.1 | sort | flops 384 | bytes 1024 | tf_op jit(solution)/shard_map/jit(argsort)/sort | solution.py:82
  29.8 8.2 %collective-permute-done.1 = f32[384,256]{1,0:T(8,128)S(1)} collective-permute-done((f32[384,256]{1,0:T(8,128)S(1)}, f32[384,256]{1,0:T(8,128)S(1)}, u32[]{:S(2)}, u32[]{:S(2)}) %collective-permute-start.1) | collective-permute-done | bytes 393248 | tf_op jit(solution)/shard_map/ppermute | solution.py:77
  38.0 0.1 bitcast_add_fusion.1
  38.1 0.1 reshape.18
  38.2 0.6 gather_fusion
  38.9 0.8 %copy.23 = f32[8,8,8,256]{3,2,0,1:T(8,128)} copy(f32[8,8,8,256]{3,2,1,0:T(8,128)S(1)} %bitcast.36) | data formatting | bytes 1048576 | tf_op jit(solution)/shard_map/reshape | solution.py:157
  39.7 38.6 %shard_map.65 = f32[8,256]{1,0:T(8,128)} custom-call(f32[8,8,8,256]{3,2,1,0:T(8,128)} %bitcast.37), custom_call_target="tpu_custom_call" | custom-call | tf_op jit(solution)/shard_map/pallas_call | solution.py:158
  78.4 1.3 %copy.26 = f32[6,256]{1,0:T(8,128)} copy(f32[6,256]{1,0:T(8,128)} %bitcast.41) | data formatting | bytes 12288
  (4 shorter events, 0.1 us)
Async XLA Ops:
  22.4 4.0 %copy-start = (f32[4,384,256]{2,1,0:T(8,128)S(1)}, f32[4,384,256]{2,1,0:T(8,128)}, u32[]{:S(2)}) copy-start(f32[4,384,256]{2,1,0:T(8,128)} %shard_map.64) | copy-start | bytes 4718596
  24.0 2.4 %collective-permute-start = (f32[2,384,256]{2,1,0:T(8,128)S(1)}, f32[2,384,256]{2,1,0:T(8,128)S(1)}, u32[]{:S(2)}, u32[]{:S(2)}) collective-permute-start(f32[2,384,256]{2,1,0:T(8,128)S(1)} %select_bitcast_fusion), channel_id=1, source_target_pairs={{0,64},{64,0},{128,192},{192,128},{1,65},{65,1},{129,193},{193,129... | collective-permute-start | bytes 2359304 | tf_op jit(solution)/shard_map/ppermute | solution.py:77
  24.4 3.3 %copy-start.1 = (s32[64]{0:T(128)S(1)}, s32[64]{0:T(128)}, u32[]{:S(2)}) copy-start(s32[64]{0:T(128)} %param.11) | copy-start | bytes 772
  26.6 11.5 %collective-permute-start.1 = (f32[384,256]{1,0:T(8,128)S(1)}, f32[384,256]{1,0:T(8,128)S(1)}, u32[]{:S(2)}, u32[]{:S(2)}) collective-permute-start(f32[384,256]{1,0:T(8,128)S(1)} %select_bitcast_fusion.1), channel_id=1, source_target_pairs={{0,128},{64,192},{128,0},{192,64},{1,129},{65,193},{129,1},{193,65... | collective-permute-start | bytes 1179656 | tf_op jit(solution)/shard_map/ppermute | solution.py:77

commit v9 on v8

--- a/solution.py
+++ b/solution.py
@@ -112,6 +112,20 @@
             device_id_type=pl.DeviceIdType.MESH,
         )
 
+    barrier = pltpu.get_barrier_semaphore()
+
+    def knock_first(d, carry):
+        pl.semaphore_signal(barrier, inc=1, device_id={"pan": my_g * inner + lax.rem(my_z + d, inner)}, device_id_type=pl.DeviceIdType.MESH)
+        return carry
+
+    def knock_second(d, carry):
+        pl.semaphore_signal(barrier, inc=1, device_id={"pan": lax.rem(my_g + d, outer) * inner + my_z}, device_id_type=pl.DeviceIdType.MESH)
+        return carry
+
+    lax.fori_loop(1, inner, knock_first, 0)
+    lax.fori_loop(1, outer, knock_second, 0)
+    pl.semaphore_wait(barrier, inner + outer - 2)
+
     def send_first(d, carry):
         first_copy(lax.rem(my_z + d, inner), my_z).start()
         return carry
@@ -166,7 +180,7 @@
             pltpu.VMEM((outer,) + data.shape[1:], data.dtype),
             pltpu.SemaphoreType.DMA((4, max(inner, outer))),
         ],
-        compiler_params=pltpu.CompilerParams(has_side_effects=True),
+        compiler_params=pltpu.CompilerParams(collective_id=0, has_side_effects=True),
     )(grouped)
 
 

time: 80.9 us -> 69.5 us (0.86)
  Pallas kernels: 50 us -> 39.1 us
    pallas_call x1, Pallas kernels: 38.6 us -> 27.8 us  [exchange_sum(): pl.pallas_call(exchange_kernel, out_shape=jax.ShapeDtypeStruct(data.shape...]
where the time goes in v9:
time: 69.5 us; the launch traced here: 68.8 us
  Pallas kernels  39.1 us (56%)
  waiting for transfers between devices  10.2 us (15%)
  blocking collectives  7.62 us (11%)
  local copies, waits for them, and re-layouts  6.31 us (9%)
  other arithmetic  3.92 us (6%)
  starting transfers between devices  1.61 us (2%)
    pallas_call x1, Pallas kernels, exchange_sum(): pl.pallas_call(exchange_kernel, out_shape=jax.ShapeDtypeStruct(data.shape...  27.8 us
    pallas_call x1, Pallas kernels, per_device(): pl.pallas_call(kernel, grid_spec=grid_spec, out_shape=jax.ShapeDtypeStruc...  11.3 us
    ppermute x2, waiting for transfers between devices, per_device(): halves = keep + lax.ppermute(send, 'obs', pairs)  10.2 us
    all_gather x1, blocking collectives, per_device(): every_obs = lax.all_gather(observer_places, 'obs', axis=1, tiled=True)  7.62 us
    unnamed x7, local copies, waits for them, and re-layouts  3.41 us
    sort x1, other arithmetic, per_device(): inverse = jnp.argsort(segment_owner)  2.03 us
    select_n x2, other arithmetic, per_device(): send = jnp.where(mine == 1, low, high)  1.65 us
    ppermute x2, starting transfers between devices, per_device(): halves = keep + lax.ppermute(send, 'obs', pairs)  1.61 us
  transfers between devices with their start and end apart: 2, of which 2 were waited for; matrix products, arithmetic and copies ran while one was open for 3% of the time, Pallas kernels for 0%

profile of v9, /device:TPU:24, one launch (start us, length us, event | category | flops | bytes accessed | tf_op | source)
XLA Modules:
  0.0 68.8 jit_solution(71391210157397563)
XLA Ops:
  0.0 0.8 %copy.13 = f32[3,256]{0,1:T(8,128)S(1)} copy(f32[3,256]{1,0:T(4,128)} %param.8) | data formatting | bytes 6144 | tf_op args[2]
  0.8 7.6 %all_gather.3 = f32[3,1024]{0,1:T(8,128)} all-gather(f32[3,256]{0,1:T(8,128)S(1)} %copy.13), channel_id=1, replica_groups=mesh['obs'=4,'pan'=64] {'obs'}, dimensions={1}, use_global_device_ids=true | all-gather | bytes 15360 | tf_op jit(solution)/shard_map/all_gather | solution.py:48
  8.4 1.3 %copy.24 = f32[1,3,512]{2,1,0:T(4,128)} copy(f32[1,3,512]{2,0,1:T(1,128)} %param.7) | data formatting | bytes 12288
  9.7 1.3 %copy.14.bins_ref = s32[8,4]{1,0:T(8,128)} copy(s32[8,4]{0,1:T(4,128)} %bitcast.42) | data formatting | bytes 256 | tf_op jit(solution)/shard_map/squeeze | solution.py:67
  11.1 11.3 %shard_map.64 = f32[4,384,256]{2,1,0:T(8,128)} custom-call(s32[8,4]{1,0:T(8,128)} %copy.14.bins_ref, f32[1024,3]{1,0:T(8,128)} %bitcast.35, f32[3,512]{1,0:T(4,128)} %bitcast.40, bf16[1024,512]{1,0:T(8,128)(2,1)} %bitcast.38, bf16[4,512,256]{2,1,0:T(8,128)(2,1)} %bitcast.39), custom_call_target="tpu_custom_call" | custom-call | tf_op jit(solution)/shard_map/pallas_call | solution.py:63
  22.4 0.0 copy-start
  22.4 1.6 %select_bitcast_fusion = f32[2,384,256]{2,1,0:T(8,128)S(1)} fusion(f32[2,2,384,256]{3,2,1,0:T(8,128)} %bitcast.33, pred[]{:T(512)S(6)} %eq.9), kind=kLoop, calls=%fused_computation.4 | loop fusion | flops 196608 | bytes 2359297 | tf_op jit(solution)/shard_map/jit(_where)/select_n | solution.py:75
  24.0 0.4 collective-permute-start
  24.4 0.0 copy-start.1
  24.4 1.9 %collective-permute-done = f32[2,384,256]{2,1,0:T(8,128)S(1)} collective-permute-done((f32[2,384,256]{2,1,0:T(8,128)S(1)}, f32[2,384,256]{2,1,0:T(8,128)S(1)}, u32[]{:S(2)}, u32[]{:S(2)}) %collective-permute-start) | collective-permute-done | bytes 786464 | tf_op jit(solution)/shard_map/ppermute | solution.py:77
  26.4 0.0 copy-done
  26.4 0.2 bitcast_add_fusion
  26.5 0.1 select_bitcast_fusion.1
  26.6 1.2 %collective-permute-start.1 = (f32[384,256]{1,0:T(8,128)S(1)}, f32[384,256]{1,0:T(8,128)S(1)}, u32[]{:S(2)}, u32[]{:S(2)}) collective-permute-start(f32[384,256]{1,0:T(8,128)S(1)} %select_bitcast_fusion.1), channel_id=1, source_target_pairs={{0,128},{64,192},{128,0},{192,64},{1,129},{65,193},{129,1},{193,65... | collective-permute-start | bytes 1179656 | tf_op jit(solution)/shard_map/ppermute | solution.py:77
  27.8 0.0 copy-done.1
  27.8 2.0 %sort.17 = (s32[64]{0:T(128)}, s32[64]{0:T(128)S(1)}) sort(s32[64]{0:T(128)S(1)} %copy-done.1, s32[64]{0:T(128)S(1)} %iota.4), dimensions={0}, to_apply=%region_0.1 | sort | flops 384 | bytes 1024 | tf_op jit(solution)/shard_map/jit(argsort)/sort | solution.py:82
  29.8 8.2 %collective-permute-done.1 = f32[384,256]{1,0:T(8,128)S(1)} collective-permute-done((f32[384,256]{1,0:T(8,128)S(1)}, f32[384,256]{1,0:T(8,128)S(1)}, u32[]{:S(2)}, u32[]{:S(2)}) %collective-permute-start.1) | collective-permute-done | bytes 393248 | tf_op jit(solution)/shard_map/ppermute | solution.py:77
  38.0 0.1 bitcast_add_fusion.1
  38.1 0.1 reshape.18
  38.2 0.6 gather_fusion
  38.9 0.8 %copy.23 = f32[8,8,8,256]{3,2,0,1:T(8,128)} copy(f32[8,8,8,256]{3,2,1,0:T(8,128)S(1)} %bitcast.36) | data formatting | bytes 1048576 | tf_op jit(solution)/shard_map/reshape | solution.py:171
  39.7 27.8 %shard_map.65 = f32[8,256]{1,0:T(8,128)} custom-call(f32[8,8,8,256]{3,2,1,0:T(8,128)} %bitcast.37), custom_call_target="tpu_custom_call" | custom-call | tf_op jit(solution)/shard_map/pallas_call | solution.py:172
  67.5 1.3 %copy.26 = f32[6,256]{1,0:T(8,128)} copy(f32[6,256]{1,0:T(8,128)} %bitcast.41) | data formatting | bytes 12288
  (4 shorter events, 0.1 us)
Async XLA Ops:
  22.4 4.0 %copy-start = (f32[4,384,256]{2,1,0:T(8,128)S(1)}, f32[4,384,256]{2,1,0:T(8,128)}, u32[]{:S(2)}) copy-start(f32[4,384,256]{2,1,0:T(8,128)} %shard_map.64) | copy-start | bytes 4718596
  24.0 2.4 %collective-permute-start = (f32[2,384,256]{2,1,0:T(8,128)S(1)}, f32[2,384,256]{2,1,0:T(8,128)S(1)}, u32[]{:S(2)}, u32[]{:S(2)}) collective-permute-start(f32[2,384,256]{2,1,0:T(8,128)S(1)} %select_bitcast_fusion), channel_id=1, source_target_pairs={{0,64},{64,0},{128,192},{192,128},{1,65},{65,1},{129,193},{193,129... | collective-permute-start | bytes 2359304 | tf_op jit(solution)/shard_map/ppermute | solution.py:77
  24.4 3.3 %copy-start.1 = (s32[64]{0:T(128)S(1)}, s32[64]{0:T(128)}, u32[]{:S(2)}) copy-start(s32[64]{0:T(128)} %param.11) | copy-start | bytes 772
  26.6 11.5 %collective-permute-start.1 = (f32[384,256]{1,0:T(8,128)S(1)}, f32[384,256]{1,0:T(8,128)S(1)}, u32[]{:S(2)}, u32[]{:S(2)}) collective-permute-start(f32[384,256]{1,0:T(8,128)S(1)} %select_bitcast_fusion.1), channel_id=1, source_target_pairs={{0,128},{64,192},{128,0},{192,64},{1,129},{65,193},{129,1},{193,65... | collective-permute-start | bytes 1179656 | tf_op jit(solution)/shard_map/ppermute | solution.py:77

commit v10 on v7

--- a/solution.py
+++ b/solution.py
@@ -102,6 +102,14 @@
         ).start()
         return carry
 
+    barrier = pltpu.get_barrier_semaphore()
+
+    def knock(d, carry):
+        pl.semaphore_signal(barrier, inc=1, device_id={"pan": lax.rem(me + d, count)}, device_id_type=pl.DeviceIdType.MESH)
+        return carry
+
+    lax.fori_loop(1, count, knock, 0)
+    pl.semaphore_wait(barrier, count - 1)
     lax.fori_loop(1, count, send, 0)
     total = x_ref[me]
 
@@ -147,7 +155,7 @@
             pltpu.SemaphoreType.DMA((count,)),
             pltpu.SemaphoreType.DMA((count,)),
         ],
-        compiler_params=pltpu.CompilerParams(has_side_effects=True),
+        compiler_params=pltpu.CompilerParams(collective_id=0, has_side_effects=True),
     )(data)
 
 

time: 77.3 us -> 68.9 us (0.89)
  Pallas kernels: 47.3 us -> 38.9 us
    pallas_call x1, Pallas kernels: 36 us -> 27.6 us  [exchange_sum(): pl.pallas_call(exchange_kernel, out_shape=jax.ShapeDtypeStruct(data.shape...]
where the time goes in v10:
time: 68.9 us; the launch traced here: 68.5 us
  Pallas kernels  38.9 us (56%)
  waiting for transfers between devices  10.2 us (15%)
  blocking collectives  7.62 us (11%)
  local copies, waits for them, and re-layouts  6.27 us (9%)
  other arithmetic  3.92 us (6%)
  starting transfers between devices  1.61 us (2%)
    pallas_call x1, Pallas kernels, exchange_sum(): pl.pallas_call(exchange_kernel, out_shape=jax.ShapeDtypeStruct(data.shape...  27.6 us
    pallas_call x1, Pallas kernels, per_device(): pl.pallas_call(kernel, grid_spec=grid_spec, out_shape=jax.ShapeDtypeStruc...  11.3 us
    ppermute x2, waiting for transfers between devices, per_device(): halves = keep + lax.ppermute(send, 'obs', pairs)  10.2 us
    all_gather x1, blocking collectives, per_device(): every_obs = lax.all_gather(observer_places, 'obs', axis=1, tiled=True)  7.62 us
    unnamed x7, local copies, waits for them, and re-layouts  3.41 us
    sort x1, other arithmetic, per_device(): inverse = jnp.argsort(segment_owner)  2.03 us
    select_n x2, other arithmetic, per_device(): send = jnp.where(mine == 1, low, high)  1.65 us
    ppermute x2, starting transfers between devices, per_device(): halves = keep + lax.ppermute(send, 'obs', pairs)  1.61 us
  transfers between devices with their start and end apart: 2, of which 2 were waited for; matrix products, arithmetic and copies ran while one was open for 3% of the time, Pallas kernels for 0%

profile of v10, /device:TPU:24, one launch (start us, length us, event | category | flops | bytes accessed | tf_op | source)
XLA Modules:
  0.0 68.5 jit_solution(4775829488218922509)
XLA Ops:
  0.0 0.8 %copy.13 = f32[3,256]{0,1:T(8,128)S(1)} copy(f32[3,256]{1,0:T(4,128)} %param.8) | data formatting | bytes 6144 | tf_op args[2]
  0.8 7.6 %all_gather.3 = f32[3,1024]{0,1:T(8,128)} all-gather(f32[3,256]{0,1:T(8,128)S(1)} %copy.13), channel_id=1, replica_groups=mesh['obs'=4,'pan'=64] {'obs'}, dimensions={1}, use_global_device_ids=true | all-gather | bytes 15360 | tf_op jit(solution)/shard_map/all_gather | solution.py:48
  8.4 1.3 %copy.21 = f32[1,3,512]{2,1,0:T(4,128)} copy(f32[1,3,512]{2,0,1:T(1,128)} %param.7) | data formatting | bytes 12288
  9.7 1.3 %copy.14.bins_ref = s32[8,4]{1,0:T(8,128)} copy(s32[8,4]{0,1:T(4,128)} %bitcast.36) | data formatting | bytes 256 | tf_op jit(solution)/shard_map/squeeze | solution.py:67
  11.1 11.3 %shard_map.64 = f32[4,384,256]{2,1,0:T(8,128)} custom-call(s32[8,4]{1,0:T(8,128)} %copy.14.bins_ref, f32[1024,3]{1,0:T(8,128)} %bitcast.31, f32[3,512]{1,0:T(4,128)} %bitcast.34, bf16[1024,512]{1,0:T(8,128)(2,1)} %bitcast.32, bf16[4,512,256]{2,1,0:T(8,128)(2,1)} %bitcast.33), custom_call_target="tpu_custom_call" | custom-call | tf_op jit(solution)/shard_map/pallas_call | solution.py:63
  22.4 0.0 copy-start
  22.4 1.6 %select_bitcast_fusion = f32[2,384,256]{2,1,0:T(8,128)S(1)} fusion(f32[2,2,384,256]{3,2,1,0:T(8,128)} %bitcast.29, pred[]{:T(512)S(6)} %eq.9), kind=kLoop, calls=%fused_computation.4 | loop fusion | flops 196608 | bytes 2359297 | tf_op jit(solution)/shard_map/jit(_where)/select_n | solution.py:75
  24.0 0.4 collective-permute-start
  24.4 0.0 copy-start.1
  24.4 1.9 %collective-permute-done = f32[2,384,256]{2,1,0:T(8,128)S(1)} collective-permute-done((f32[2,384,256]{2,1,0:T(8,128)S(1)}, f32[2,384,256]{2,1,0:T(8,128)S(1)}, u32[]{:S(2)}, u32[]{:S(2)}) %collective-permute-start) | collective-permute-done | bytes 786464 | tf_op jit(solution)/shard_map/ppermute | solution.py:77
  26.4 0.0 copy-done
  26.4 0.2 bitcast_add_fusion
  26.5 0.1 select_bitcast_fusion.1
  26.6 1.2 %collective-permute-start.1 = (f32[384,256]{1,0:T(8,128)S(1)}, f32[384,256]{1,0:T(8,128)S(1)}, u32[]{:S(2)}, u32[]{:S(2)}) collective-permute-start(f32[384,256]{1,0:T(8,128)S(1)} %select_bitcast_fusion.1), channel_id=1, source_target_pairs={{0,128},{64,192},{128,0},{192,64},{1,129},{65,193},{129,1},{193,65... | collective-permute-start | bytes 1179656 | tf_op jit(solution)/shard_map/ppermute | solution.py:77
  27.8 0.0 copy-done.1
  27.8 2.0 %sort.17 = (s32[64]{0:T(128)}, s32[64]{0:T(128)S(1)}) sort(s32[64]{0:T(128)S(1)} %copy-done.1, s32[64]{0:T(128)S(1)} %iota.4), dimensions={0}, to_apply=%region_0.1 | sort | flops 384 | bytes 1024 | tf_op jit(solution)/shard_map/jit(argsort)/sort | solution.py:82
  29.8 8.2 %collective-permute-done.1 = f32[384,256]{1,0:T(8,128)S(1)} collective-permute-done((f32[384,256]{1,0:T(8,128)S(1)}, f32[384,256]{1,0:T(8,128)S(1)}, u32[]{:S(2)}, u32[]{:S(2)}) %collective-permute-start.1) | collective-permute-done | bytes 393248 | tf_op jit(solution)/shard_map/ppermute | solution.py:77
  38.0 0.1 bitcast_add_fusion.1
  38.1 0.1 reshape.15
  38.2 0.6 gather_fusion
  38.8 0.8 %pad.4.x_ref = f32[64,8,256]{2,1,0:T(8,128)} pad(f32[64,6,256]{2,1,0:T(8,128)S(1)} %gather_fusion, f32[]{:T(128)} %constant.14.clone.1), padding=0_0x0_2x0_0 | pad | bytes 917508 | tf_op jit(solution)/shard_map/jit(_pad)/pad | solution.py:85
  39.6 27.6 %shard_map.65 = f32[8,256]{1,0:T(8,128)} custom-call(f32[64,8,256]{2,1,0:T(8,128)} %pad.4.x_ref), custom_call_target="tpu_custom_call" | custom-call | tf_op jit(solution)/shard_map/pallas_call | solution.py:148
  67.2 1.3 %copy.23 = f32[6,256]{1,0:T(8,128)} copy(f32[6,256]{1,0:T(8,128)} %bitcast.35) | data formatting | bytes 12288
  (3 shorter events, 0.0 us)
Async XLA Ops:
  22.4 4.0 %copy-start = (f32[4,384,256]{2,1,0:T(8,128)S(1)}, f32[4,384,256]{2,1,0:T(8,128)}, u32[]{:S(2)}) copy-start(f32[4,384,256]{2,1,0:T(8,128)} %shard_map.64) | copy-start | bytes 4718596
  24.0 2.4 %collective-permute-start = (f32[2,384,256]{2,1,0:T(8,128)S(1)}, f32[2,384,256]{2,1,0:T(8,128)S(1)}, u32[]{:S(2)}, u32[]{:S(2)}) collective-permute-start(f32[2,384,256]{2,1,0:T(8,128)S(1)} %select_bitcast_fusion), channel_id=1, source_target_pairs={{0,64},{64,0},{128,192},{192,128},{1,65},{65,1},{129,193},{193,129... | collective-permute-start | bytes 2359304 | tf_op jit(solution)/shard_map/ppermute | solution.py:77
  24.4 3.3 %copy-start.1 = (s32[64]{0:T(128)S(1)}, s32[64]{0:T(128)}, u32[]{:S(2)}) copy-start(s32[64]{0:T(128)} %param.11) | copy-start | bytes 772
  26.6 11.5 %collective-permute-start.1 = (f32[384,256]{1,0:T(8,128)S(1)}, f32[384,256]{1,0:T(8,128)S(1)}, u32[]{:S(2)}, u32[]{:S(2)}) collective-permute-start(f32[384,256]{1,0:T(8,128)S(1)} %select_bitcast_fusion.1), channel_id=1, source_target_pairs={{0,128},{64,192},{128,0},{192,64},{1,129},{65,193},{129,1},{193,65... | collective-permute-start | bytes 1179656 | tf_op jit(solution)/shard_map/ppermute | solution.py:77

commit v11 on v10

--- a/solution.py
+++ b/solution.py
@@ -15,11 +15,12 @@
 
 def fwh_kernel(bins_ref, obs_ref, place_ref, frac_ref, src_ref, out_ref, *, amplitude, panel_blocks, window, bins_total):
     ob = pl.program_id(0)
+    here = obs_ref[...].T
     acc = jnp.zeros((OBLK, bins_total), jnp.float32)
     pad = jnp.zeros((OBLK, bins_total - window), jnp.float32)
     for pb in range(panel_blocks):
         cols = slice(pb * PBLK, (pb + 1) * PBLK)
-        seps = [obs_ref[:, c : c + 1] - place_ref[c : c + 1, cols] for c in range(3)]
+        seps = [here[:, c : c + 1] - place_ref[c : c + 1, cols] for c in range(3)]
         dist_sq = seps[0] * seps[0] + seps[1] * seps[1] + seps[2] * seps[2]
         parts = [amplitude / jnp.sqrt(dist_sq)] + [amplitude * sep / dist_sq for sep in seps]
         weight = frac_ref[:, cols].astype(jnp.float32)
@@ -33,7 +34,7 @@
             hi_p = jnp.dot(hi_w, src, preferred_element_type=jnp.float32)
             low = lo_p if low is None else low + lo_p
             high = hi_p if high is None else high + hi_p
-        shift = bins_ref[ob, pb]
+        shift = bins_ref[ob, 0, pb]
         acc = acc + pltpu.roll(jnp.concatenate([low, pad], axis=1), shift, 1)
         acc = acc + pltpu.roll(jnp.concatenate([high, pad], axis=1), shift + 1, 1)
     out_ref[...] = acc.T
@@ -53,7 +54,7 @@
         num_scalar_prefetch=1,
         grid=(obs_blocks,),
         in_specs=[
-            pl.BlockSpec((OBLK, 3), lambda i, b: (i, 0)),
+            pl.BlockSpec((3, OBLK), lambda i, b: (0, i)),
             pl.BlockSpec((3, local_panels), lambda i, b: (0, 0)),
             pl.BlockSpec((OBLK, local_panels), lambda i, b: (i, 0)),
             pl.BlockSpec((4, local_panels, window), lambda i, b: (0, 0, 0)),
@@ -64,7 +65,7 @@
         kernel,
         grid_spec=grid_spec,
         out_shape=jax.ShapeDtypeStruct((obs_blocks // 2, bins_total, 2 * OBLK), jnp.float32),
-    )(delay_bins[:, 0, :], every_obs.T, panel_places[0], fraction[:, 0, :], sources[0])
+    )(delay_bins, every_obs, panel_places[0], fraction[:, 0, :], sources[0])
     halves = totals.reshape((2, 2) + totals.shape[1:])
     me = lax.axis_index("obs")
     for bit, dim in ((0, 1), (1, 0)):

time: 68.9 us -> 67.5 us (0.980)
  blocking collectives: 7.62 us -> 6.56 us
  local copies, waits for them, and re-layouts: 6.27 us -> 5.46 us
    squeeze x1 -> x0, local copies, waits for them, and re-layouts: 1.35 us -> none  [per_device(): delay_bins[:, 0, :]]
    all_gather x1, blocking collectives: 7.62 us -> 6.56 us  [per_device(): every_obs = lax.all_gather(observer_places, 'obs', axis=1, tiled=True)]
where the time goes in v11:
time: 67.5 us; the launch traced here: 67.2 us
  Pallas kernels  39.4 us (58%)
  waiting for transfers between devices  10.5 us (16%)
  blocking collectives  6.56 us (10%)
  local copies, waits for them, and re-layouts  5.46 us (8%)
  other arithmetic  3.92 us (6%)
  starting transfers between devices  1.26 us (2%)
    pallas_call x1, Pallas kernels, exchange_sum(): pl.pallas_call(exchange_kernel, out_shape=jax.ShapeDtypeStruct(data.shape...  27.6 us
    pallas_call x1, Pallas kernels, per_device(): pl.pallas_call(kernel, grid_spec=grid_spec, out_shape=jax.ShapeDtypeStruc...  11.9 us
    ppermute x2, waiting for transfers between devices, per_device(): halves = keep + lax.ppermute(send, 'obs', pairs)  10.5 us
    all_gather x1, blocking collectives, per_device(): every_obs = lax.all_gather(observer_places, 'obs', axis=1, tiled=True)  6.56 us
    unnamed x7, local copies, waits for them, and re-layouts  3.95 us
    sort x1, other arithmetic, per_device(): inverse = jnp.argsort(segment_owner)  2.03 us
    select_n x2, other arithmetic, per_device(): send = jnp.where(mine == 1, low, high)  1.65 us
  transfers between devices with their start and end apart: 2, of which 2 were waited for; matrix products, arithmetic and copies ran while one was open for 3% of the time, Pallas kernels for 0%

profile of v11, /device:TPU:24, one launch (start us, length us, event | category | flops | bytes accessed | tf_op | source)
XLA Modules:
  0.0 67.2 jit_solution(13828971290559622639)
XLA Ops:
  0.0 6.6 %all_gather.3.obs_ref = f32[3,1024]{1,0:T(4,128)} all-gather(f32[3,256]{1,0:T(4,128)} %param.8), channel_id=1, replica_groups=mesh['obs'=4,'pan'=64] {'obs'}, dimensions={1}, use_global_device_ids=true | all-gather | bytes 15360 | tf_op jit(solution)/shard_map/all_gather | solution.py:49
  6.6 1.3 %copy.19 = f32[1,3,512]{2,1,0:T(4,128)} copy(f32[1,3,512]{2,0,1:T(1,128)} %param.7) | data formatting | bytes 12288
  7.8 1.4 %copy.12.bins_ref = s32[8,1,4]{2,1,0:T(1,128)} copy(s32[8,1,4]{0,2,1:T(4,128)} %param.10) | data formatting | bytes 256 | tf_op args[4]
  9.2 11.9 %shard_map.64 = f32[4,384,256]{2,1,0:T(8,128)} custom-call(s32[8,1,4]{2,1,0:T(1,128)} %copy.12.bins_ref, f32[3,1024]{1,0:T(4,128)} %all_gather.3.obs_ref, f32[3,512]{1,0:T(4,128)} %bitcast.31, bf16[1024,512]{1,0:T(8,128)(2,1)} %bitcast.29, bf16[4,512,256]{2,1,0:T(8,128)(2,1)} %bitcast.30), custom_call_target="tpu_custom_call" | custom-call | tf_op jit(solution)/shard_map/pallas_call | solution.py:64
  21.1 0.0 copy-start
  21.1 1.6 %select_bitcast_fusion = f32[2,384,256]{2,1,0:T(8,128)S(1)} fusion(f32[2,2,384,256]{3,2,1,0:T(8,128)} %bitcast.27, pred[]{:T(512)S(6)} %eq.9), kind=kLoop, calls=%fused_computation.4 | loop fusion | flops 196608 | bytes 2359297 | tf_op jit(solution)/shard_map/jit(_where)/select_n | solution.py:76
  22.6 0.4 collective-permute-start
  23.1 0.0 copy-start.1
  23.1 1.9 %collective-permute-done = f32[2,384,256]{2,1,0:T(8,128)S(1)} collective-permute-done((f32[2,384,256]{2,1,0:T(8,128)S(1)}, f32[2,384,256]{2,1,0:T(8,128)S(1)}, u32[]{:S(2)}, u32[]{:S(2)}) %collective-permute-start) | collective-permute-done | bytes 786464 | tf_op jit(solution)/shard_map/ppermute | solution.py:78
  25.0 0.0 copy-done
  25.0 0.2 bitcast_add_fusion
  25.2 0.1 select_bitcast_fusion.1
  25.2 0.8 %collective-permute-start.1 = (f32[384,256]{1,0:T(8,128)S(1)}, f32[384,256]{1,0:T(8,128)S(1)}, u32[]{:S(2)}, u32[]{:S(2)}) collective-permute-start(f32[384,256]{1,0:T(8,128)S(1)} %select_bitcast_fusion.1), channel_id=1, source_target_pairs={{0,128},{64,192},{128,0},{192,64},{1,129},{65,193},{129,1},{193,65... | collective-permute-start | bytes 1179656 | tf_op jit(solution)/shard_map/ppermute | solution.py:78
  26.1 0.0 copy-done.1
  26.1 2.0 %sort.17 = (s32[64]{0:T(128)}, s32[64]{0:T(128)S(1)}) sort(s32[64]{0:T(128)S(1)} %copy-done.1, s32[64]{0:T(128)S(1)} %iota.4), dimensions={0}, to_apply=%region_0.1 | sort | flops 384 | bytes 1024 | tf_op jit(solution)/shard_map/jit(argsort)/sort | solution.py:83
  28.1 8.6 %collective-permute-done.1 = f32[384,256]{1,0:T(8,128)S(1)} collective-permute-done((f32[384,256]{1,0:T(8,128)S(1)}, f32[384,256]{1,0:T(8,128)S(1)}, u32[]{:S(2)}, u32[]{:S(2)}) %collective-permute-start.1) | collective-permute-done | bytes 393248 | tf_op jit(solution)/shard_map/ppermute | solution.py:78
  36.7 0.1 bitcast_add_fusion.1
  36.8 0.1 reshape.15
  36.8 0.6 gather_fusion
  37.5 0.8 %pad.4.x_ref = f32[64,8,256]{2,1,0:T(8,128)} pad(f32[64,6,256]{2,1,0:T(8,128)S(1)} %gather_fusion, f32[]{:T(128)} %constant.14.clone.1), padding=0_0x0_2x0_0 | pad | bytes 917508 | tf_op jit(solution)/shard_map/jit(_pad)/pad | solution.py:86
  38.3 27.6 %shard_map.65 = f32[8,256]{1,0:T(8,128)} custom-call(f32[64,8,256]{2,1,0:T(8,128)} %pad.4.x_ref), custom_call_target="tpu_custom_call" | custom-call | tf_op jit(solution)/shard_map/pallas_call | solution.py:149
  65.9 1.3 %copy.21 = f32[6,256]{1,0:T(8,128)} copy(f32[6,256]{1,0:T(8,128)} %bitcast.32) | data formatting | bytes 12288
  (3 shorter events, 0.0 us)
Async XLA Ops:
  21.1 4.0 %copy-start = (f32[4,384,256]{2,1,0:T(8,128)S(1)}, f32[4,384,256]{2,1,0:T(8,128)}, u32[]{:S(2)}) copy-start(f32[4,384,256]{2,1,0:T(8,128)} %shard_map.64) | copy-start | bytes 4718596
  22.6 2.4 %collective-permute-start = (f32[2,384,256]{2,1,0:T(8,128)S(1)}, f32[2,384,256]{2,1,0:T(8,128)S(1)}, u32[]{:S(2)}, u32[]{:S(2)}) collective-permute-start(f32[2,384,256]{2,1,0:T(8,128)S(1)} %select_bitcast_fusion), channel_id=1, source_target_pairs={{0,64},{64,0},{128,192},{192,128},{1,65},{65,1},{129,193},{193,129... | collective-permute-start | bytes 2359304 | tf_op jit(solution)/shard_map/ppermute | solution.py:78
  23.1 3.0 %copy-start.1 = (s32[64]{0:T(128)S(1)}, s32[64]{0:T(128)}, u32[]{:S(2)}) copy-start(s32[64]{0:T(128)} %param.11) | copy-start | bytes 772
  25.2 11.4 %collective-permute-start.1 = (f32[384,256]{1,0:T(8,128)S(1)}, f32[384,256]{1,0:T(8,128)S(1)}, u32[]{:S(2)}, u32[]{:S(2)}) collective-permute-start(f32[384,256]{1,0:T(8,128)S(1)} %select_bitcast_fusion.1), channel_id=1, source_target_pairs={{0,128},{64,192},{128,0},{192,64},{1,129},{65,193},{129,1},{193,65... | collective-permute-start | bytes 1179656 | tf_op jit(solution)/shard_map/ppermute | solution.py:78

commit v12 on v11

--- a/solution.py
+++ b/solution.py
@@ -46,7 +46,18 @@
     bins_total = window + MAXD + 1
     amplitude = 60.0 / math.sqrt(local_panels * lax.axis_size("obs") * lax.axis_size("pan"))
     panel_blocks = local_panels // PBLK
-    every_obs = lax.all_gather(observer_places, "obs", axis=1, tiled=True)
+    obs_count = lax.axis_size("obs")
+    obs_me = lax.axis_index("obs")
+    arrived = [observer_places] + [
+        lax.ppermute(observer_places, "obs", [(p, p ^ k) for p in range(obs_count)]) for k in range(1, obs_count)
+    ]
+    blocks = []
+    for q in range(obs_count):
+        block = arrived[0]
+        for k in range(1, obs_count):
+            block = jnp.where((obs_me ^ k) == q, arrived[k], block)
+        blocks.append(block)
+    every_obs = jnp.concatenate(blocks, axis=1)
     obs_total = every_obs.shape[1]
     obs_blocks = obs_total // OBLK
     kernel = functools.partial(fwh_kernel, amplitude=amplitude, panel_blocks=panel_blocks, window=window, bins_total=bins_total)

time: 67.5 us -> 64.1 us (0.950)
  blocking collectives: 6.56 us -> 0 us
  starting transfers between devices: 1.26 us -> 3.29 us
  other arithmetic: 3.92 us -> 5.21 us
    all_gather x1 -> x0, blocking collectives: 6.56 us -> none  [per_device(): every_obs = lax.all_gather(observer_places, 'obs', axis=1, tiled=True)]
    ppermute x0 -> x3, starting transfers between devices: none -> 1.86 us  [per_device(): lax.ppermute(observer_places, 'obs', [(p, p ^ k) for p in range(obs_count)])]
    select_n x0 -> x1, other arithmetic: none -> 0.7 us  [per_device(): block = jnp.where(obs_me ^ k == q, arrived[k], block)]
  transfers between devices with their start and end apart: 2 -> 5, of which waited for: 2 -> 3; matrix products, arithmetic and copies ran while one was open for 3% -> 7% of each run, Pallas kernels for 0% -> 0%
where the time goes in v12:
time: 64.1 us; the launch traced here: 63.8 us
  Pallas kernels  39.4 us (61%)
  waiting for transfers between devices  10.4 us (16%)
  local copies, waits for them, and re-layouts  5.45 us (9%)
  other arithmetic  5.21 us (8%)
  starting transfers between devices  3.29 us (5%)
    pallas_call x1, Pallas kernels, exchange_sum(): pl.pallas_call(exchange_kernel, out_shape=jax.ShapeDtypeStruct(data.shape...  27.5 us
    pallas_call x1, Pallas kernels, per_device(): pl.pallas_call(kernel, grid_spec=grid_spec, out_shape=jax.ShapeDtypeStruc...  11.8 us
    ppermute x2, waiting for transfers between devices, per_device(): halves = keep + lax.ppermute(send, 'obs', pairs)  10.1 us
    unnamed x7, local copies, waits for them, and re-layouts  3.94 us
    sort x1, other arithmetic, per_device(): inverse = jnp.argsort(segment_owner)  2.03 us
    ppermute x3, starting transfers between devices, per_device(): lax.ppermute(observer_places, 'obs', [(p, p ^ k) for p in range(obs_count)])  1.86 us
    select_n x2, other arithmetic, per_device(): send = jnp.where(mine == 1, low, high)  1.64 us
    ppermute x2, starting transfers between devices, per_device(): halves = keep + lax.ppermute(send, 'obs', pairs)  1.43 us
  transfers between devices with their start and end apart: 5, of which 3 were waited for; matrix products, arithmetic and copies ran while one was open for 7% of the time, Pallas kernels for 0%

profile of v12, /device:TPU:24, one launch (start us, length us, event | category | flops | bytes accessed | tf_op | source)
XLA Modules:
  0.0 63.8 jit_solution(1932889380158800582)
XLA Ops:
  0.0 0.9 %collective-permute-start = (f32[3,256]{1,0:T(4,128)}, f32[3,256]{1,0:T(4,128)S(1)}, u32[]{:S(2)}, u32[]{:S(2)}) collective-permute-start(f32[3,256]{1,0:T(4,128)} %param.8), channel_id=1, source_target_pairs={{0,192},{64,128},{128,64},{192,0},{1,193},{65,129},{129,65},{193,1... | collective-permute-start | bytes 9224 | tf_op jit(solution)/shard_map/ppermute | solution.py:52
  0.9 0.6 collective-permute-start.1
  1.5 0.4 collective-permute-start.2
  1.9 1.3 %copy.19 = f32[1,3,512]{2,1,0:T(4,128)} copy(f32[1,3,512]{2,0,1:T(1,128)} %param.7) | data formatting | bytes 12288
  3.2 1.3 %copy.12.bins_ref = s32[8,1,4]{2,1,0:T(1,128)} copy(s32[8,1,4]{0,2,1:T(4,128)} %param.10) | data formatting | bytes 256 | tf_op args[4]
  4.5 0.0 collective-permute-done
  4.5 0.2 collective-permute-done.1
  4.8 0.0 collective-permute-done.2
  4.8 0.7 %select_select_fusion.3 = (f32[3,256]{1,0:T(4,128)S(1)}, f32[3,256]{1,0:T(4,128)S(1)}, f32[3,256]{1,0:T(4,128)S(1)}, f32[3,256]{1,0:T(4,128)S(1)}) fusion(f32[3,256]{1,0:T(4,128)S(1)} %collective-permute-done, f32[3,256]{1,0:T(4,128)S(1)} %collective-permute-done.1, f32[3,256]{1,0:T(4,128)S(1)} %collective-permute-done.2, f32[3,256]{1,0:T(4,128)} %param.8, ...), kind=kLoop, calls=%fused_computation.13 | loop fusion | flops 9216 | bytes 24588 | tf_op jit(solution)/shard_map/jit(_where)/select_n | solution.py:58
  5.5 0.6 pad_maximum_fusion.obs_ref
  6.1 11.8 %shard_map.64 = f32[4,384,256]{2,1,0:T(8,128)} custom-call(s32[8,1,4]{2,1,0:T(1,128)} %copy.12.bins_ref, f32[3,1024]{1,0:T(4,128)} %pad_maximum_fusion.obs_ref, f32[3,512]{1,0:T(4,128)} %bitcast.31, bf16[1024,512]{1,0:T(8,128)(2,1)} %bitcast.29, bf16[4,512,256]{2,1,0:T(8,128)(2,1)} %bitcast.30), custom_call_target="tpu_custom_call" | custom-call | tf_op jit(solution)/shard_map/pallas_call | solution.py:75
  17.9 0.0 copy-start
  17.9 1.6 %select_bitcast_fusion = f32[2,384,256]{2,1,0:T(8,128)S(1)} fusion(f32[2,2,384,256]{3,2,1,0:T(8,128)} %bitcast.27, pred[]{:T(512)S(6)} %eq.45), kind=kLoop, calls=%fused_computation.4 | loop fusion | flops 196608 | bytes 2359297 | tf_op jit(solution)/shard_map/jit(_where)/select_n | solution.py:87
  19.5 0.1 collective-permute-start.3
  19.6 0.0 copy-start.1
  19.6 2.3 %collective-permute-done.3 = f32[2,384,256]{2,1,0:T(8,128)S(1)} collective-permute-done((f32[2,384,256]{2,1,0:T(8,128)S(1)}, f32[2,384,256]{2,1,0:T(8,128)S(1)}, u32[]{:S(2)}, u32[]{:S(2)}) %collective-permute-start.3) | collective-permute-done | bytes 786464 | tf_op jit(solution)/shard_map/ppermute | solution.py:89
  21.9 0.0 copy-done
  21.9 0.2 bitcast_add_fusion
  22.0 0.1 select_bitcast_fusion.1
  22.1 1.3 %collective-permute-start.4 = (f32[384,256]{1,0:T(8,128)S(1)}, f32[384,256]{1,0:T(8,128)S(1)}, u32[]{:S(2)}, u32[]{:S(2)}) collective-permute-start(f32[384,256]{1,0:T(8,128)S(1)} %select_bitcast_fusion.1), channel_id=1, source_target_pairs={{0,128},{64,192},{128,0},{192,64},{1,129},{65,193},{129,1},{193,65... | collective-permute-start | bytes 1179656 | tf_op jit(solution)/shard_map/ppermute | solution.py:89
  23.4 0.0 copy-done.1
  23.4 2.0 %sort.17 = (s32[64]{0:T(128)}, s32[64]{0:T(128)S(1)}) sort(s32[64]{0:T(128)S(1)} %copy-done.1, s32[64]{0:T(128)S(1)} %iota.4), dimensions={0}, to_apply=%region_0.1 | sort | flops 384 | bytes 1024 | tf_op jit(solution)/shard_map/jit(argsort)/sort | solution.py:94
  25.5 7.9 %collective-permute-done.4 = f32[384,256]{1,0:T(8,128)S(1)} collective-permute-done((f32[384,256]{1,0:T(8,128)S(1)}, f32[384,256]{1,0:T(8,128)S(1)}, u32[]{:S(2)}, u32[]{:S(2)}) %collective-permute-start.4) | collective-permute-done | bytes 393248 | tf_op jit(solution)/shard_map/ppermute | solution.py:89
  33.3 0.1 bitcast_add_fusion.1
  33.4 0.1 reshape.15
  33.5 0.6 gather_fusion
  34.1 0.8 %pad.4.x_ref = f32[64,8,256]{2,1,0:T(8,128)} pad(f32[64,6,256]{2,1,0:T(8,128)S(1)} %gather_fusion, f32[]{:T(128)} %constant.18.clone.1), padding=0_0x0_2x0_0 | pad | bytes 917508 | tf_op jit(solution)/shard_map/jit(_pad)/pad | solution.py:97
  34.9 27.5 %shard_map.65 = f32[8,256]{1,0:T(8,128)} custom-call(f32[64,8,256]{2,1,0:T(8,128)} %pad.4.x_ref), custom_call_target="tpu_custom_call" | custom-call | tf_op jit(solution)/shard_map/pallas_call | solution.py:160
  62.5 1.3 %copy.21 = f32[6,256]{1,0:T(8,128)} copy(f32[6,256]{1,0:T(8,128)} %bitcast.32) | data formatting | bytes 12288
  (3 shorter events, 0.0 us)
Async XLA Ops:
  0.0 4.5 %collective-permute-start = (f32[3,256]{1,0:T(4,128)}, f32[3,256]{1,0:T(4,128)S(1)}, u32[]{:S(2)}, u32[]{:S(2)}) collective-permute-start(f32[3,256]{1,0:T(4,128)} %param.8), channel_id=1, source_target_pairs={{0,192},{64,128},{128,64},{192,0},{1,193},{65,129},{129,65},{193,1... | collective-permute-start | bytes 9224 | tf_op jit(solution)/shard_map/ppermute | solution.py:52
  0.9 3.8 %collective-permute-start.1 = (f32[3,256]{1,0:T(4,128)}, f32[3,256]{1,0:T(4,128)S(1)}, u32[]{:S(2)}, u32[]{:S(2)}) collective-permute-start(f32[3,256]{1,0:T(4,128)} %param.8), channel_id=1, source_target_pairs={{0,128},{64,192},{128,0},{192,64},{1,129},{65,193},{129,1},{193,65... | collective-permute-start | bytes 9224 | tf_op jit(solution)/shard_map/ppermute | solution.py:52
  1.5 3.3 %collective-permute-start.2 = (f32[3,256]{1,0:T(4,128)}, f32[3,256]{1,0:T(4,128)S(1)}, u32[]{:S(2)}, u32[]{:S(2)}) collective-permute-start(f32[3,256]{1,0:T(4,128)} %param.8), channel_id=1, source_target_pairs={{0,64},{64,0},{128,192},{192,128},{1,65},{65,1},{129,193},{193,129... | collective-permute-start | bytes 9224 | tf_op jit(solution)/shard_map/ppermute | solution.py:52
  17.9 4.0 %copy-start = (f32[4,384,256]{2,1,0:T(8,128)S(1)}, f32[4,384,256]{2,1,0:T(8,128)}, u32[]{:S(2)}) copy-start(f32[4,384,256]{2,1,0:T(8,128)} %shard_map.64) | copy-start | bytes 4718596
  19.5 2.4 %collective-permute-start.3 = (f32[2,384,256]{2,1,0:T(8,128)S(1)}, f32[2,384,256]{2,1,0:T(8,128)S(1)}, u32[]{:S(2)}, u32[]{:S(2)}) collective-permute-start(f32[2,384,256]{2,1,0:T(8,128)S(1)} %select_bitcast_fusion), channel_id=1, source_target_pairs={{0,64},{64,0},{128,192},{192,128},{1,65},{65,1},{129,193},{193,129... | collective-permute-start | bytes 2359304 | tf_op jit(solution)/shard_map/ppermute | solution.py:89
  19.6 3.8 %copy-start.1 = (s32[64]{0:T(128)S(1)}, s32[64]{0:T(128)}, u32[]{:S(2)}) copy-start(s32[64]{0:T(128)} %param.11) | copy-start | bytes 772
  22.1 11.2 %collective-permute-start.4 = (f32[384,256]{1,0:T(8,128)S(1)}, f32[384,256]{1,0:T(8,128)S(1)}, u32[]{:S(2)}, u32[]{:S(2)}) collective-permute-start(f32[384,256]{1,0:T(8,128)S(1)} %select_bitcast_fusion.1), channel_id=1, source_target_pairs={{0,128},{64,192},{128,0},{192,64},{1,129},{65,193},{129,1},{193,65... | collective-permute-start | bytes 1179656 | tf_op jit(solution)/shard_map/ppermute | solution.py:89

commit v13 on v12

--- a/solution.py
+++ b/solution.py
@@ -13,8 +13,8 @@
 PBLK = 128
 
 
-def fwh_kernel(bins_ref, obs_ref, place_ref, frac_ref, src_ref, out_ref, *, amplitude, panel_blocks, window, bins_total):
-    ob = pl.program_id(0)
+def fwh_kernel(bins_ref, order_ref, obs_ref, place_ref, frac_ref, src_ref, out_ref, *, amplitude, panel_blocks, window, bins_total):
+    ob = order_ref[pl.program_id(0)]
     here = obs_ref[...].T
     acc = jnp.zeros((OBLK, bins_total), jnp.float32)
     pad = jnp.zeros((OBLK, bins_total - window), jnp.float32)
@@ -61,32 +61,40 @@
     obs_total = every_obs.shape[1]
     obs_blocks = obs_total // OBLK
     kernel = functools.partial(fwh_kernel, amplitude=amplitude, panel_blocks=panel_blocks, window=window, bins_total=bins_total)
-    grid_spec = pltpu.PrefetchScalarGridSpec(
-        num_scalar_prefetch=1,
-        grid=(obs_blocks,),
-        in_specs=[
-            pl.BlockSpec((3, OBLK), lambda i, b: (0, i)),
-            pl.BlockSpec((3, local_panels), lambda i, b: (0, 0)),
-            pl.BlockSpec((OBLK, local_panels), lambda i, b: (i, 0)),
-            pl.BlockSpec((4, local_panels, window), lambda i, b: (0, 0, 0)),
-        ],
-        out_specs=pl.BlockSpec((None, bins_total, OBLK), lambda i, b: (i // 2, 0, i % 2)),
-    )
-    totals = pl.pallas_call(
-        kernel,
-        grid_spec=grid_spec,
-        out_shape=jax.ShapeDtypeStruct((obs_blocks // 2, bins_total, 2 * OBLK), jnp.float32),
-    )(delay_bins, every_obs, panel_places[0], fraction[:, 0, :], sources[0])
-    halves = totals.reshape((2, 2) + totals.shape[1:])
-    me = lax.axis_index("obs")
-    for bit, dim in ((0, 1), (1, 0)):
-        mine = (me >> bit) & 1
-        low = lax.index_in_dim(halves, 0, dim, keepdims=False)
-        high = lax.index_in_dim(halves, 1, dim, keepdims=False)
-        keep = jnp.where(mine == 1, high, low)
-        send = jnp.where(mine == 1, low, high)
-        pairs = [(p, p ^ (1 << bit)) for p in range(4)]
-        halves = keep + lax.ppermute(send, "obs", pairs)
+
+    def blocks_of(order):
+        grid_spec = pltpu.PrefetchScalarGridSpec(
+            num_scalar_prefetch=2,
+            grid=(order.shape[0],),
+            in_specs=[
+                pl.BlockSpec((3, OBLK), lambda i, b, o: (0, o[i])),
+                pl.BlockSpec((3, local_panels), lambda i, b, o: (0, 0)),
+                pl.BlockSpec((OBLK, local_panels), lambda i, b, o: (o[i], 0)),
+                pl.BlockSpec((4, local_panels, window), lambda i, b, o: (0, 0, 0)),
+            ],
+            out_specs=pl.BlockSpec((None, bins_total, OBLK), lambda i, b, o: (i, 0, 0)),
+        )
+        return pl.pallas_call(
+            kernel,
+            grid_spec=grid_spec,
+            out_shape=jax.ShapeDtypeStruct((order.shape[0], bins_total, OBLK), jnp.float32),
+        )(delay_bins, order, every_obs, panel_places[0], fraction[:, 0, :], sources[0])
+
+    low_bit = obs_me & 1
+    high_bit = obs_me >> 1
+    pair = jnp.arange(2, dtype=jnp.int32)
+
+    def group_blocks(high, low):
+        return 2 * (2 * high + low) + pair
+
+    first = blocks_of(jnp.concatenate([group_blocks(0, 1 - low_bit), group_blocks(1, 1 - low_bit)]))
+    first_in = lax.ppermute(first, "obs", [(p, p ^ 1) for p in range(obs_count)])
+    second = blocks_of(group_blocks(1 - high_bit, low_bit))
+    second = second + jnp.where(high_bit == 1, first_in[:2], first_in[2:])
+    second_in = lax.ppermute(second, "obs", [(p, p ^ 2) for p in range(obs_count)])
+    own = blocks_of(group_blocks(high_bit, low_bit))
+    own = own + jnp.where(high_bit == 1, first_in[2:], first_in[:2]) + second_in
+    halves = jnp.concatenate([own[0], own[1]], axis=1)
     reduced = halves
     segment_count = segment_owner.shape[0]
     seg_len = bins_total // segment_count

time: 64.1 us -> 66 us (1.030)
  waiting for transfers between devices: 10.4 us -> 4.68 us
  Pallas kernels: 39.4 us -> 45.1 us
  other arithmetic: 5.21 us -> 6.71 us
    ppermute x2, waiting for transfers between devices: 10.1 us -> 4.49 us  [the longest x1 4.49 us: per_device(): lax.ppermute(second, 'obs', [(p, p ^ 2) for p in range(obs_count)])]
    pallas_call x1 -> x3, Pallas kernels: 11.8 us -> 17.3 us  [blocks_of(): pl.pallas_call(kernel, grid_spec=grid_spec, out_shape=jax.ShapeDtypeStruc...]
    add x2 -> x5, other arithmetic: 0.23 us -> 3.31 us  [the longest x3 1.19 us: group_blocks(): return 2 * (2 * high + low) + pair]
    select_n x2 -> x0, other arithmetic: 1.64 us -> none  [per_device(): send = jnp.where(mine == 1, low, high)]
    concatenate x0 -> x2, other arithmetic: none -> 0.69 us  [the longest x1 0.64 us: per_device(): jnp.concatenate([group_blocks(0, 1 - low_bit), group_blocks(1, 1 - low_bi...]
    select_n x1, other arithmetic: 0.7 us -> 0.01 us  [per_device(): block = jnp.where(obs_me ^ k == q, arrived[k], block)]
    unnamed x7 -> x11, local copies, waits for them, and re-layouts: 3.94 us -> 3.99 us
  transfers between devices with their start and end apart: 5 -> 5, of which waited for: 3 -> 2; matrix products, arithmetic and copies ran while one was open for 7% -> 8% of each run, Pallas kernels for 0% -> 15%
where the time goes in v13:
time: 66 us; the launch traced here: 65.5 us
  Pallas kernels  45.1 us (68%)
  other arithmetic  6.71 us (10%)
  local copies, waits for them, and re-layouts  5.54 us (8%)
  waiting for transfers between devices  4.68 us (7%)
  starting transfers between devices  3.38 us (5%)
    pallas_call x1, Pallas kernels, exchange_sum(): pl.pallas_call(exchange_kernel, out_shape=jax.ShapeDtypeStruct(data.shape...  27.8 us
    pallas_call x3, Pallas kernels, blocks_of(): pl.pallas_call(kernel, grid_spec=grid_spec, out_shape=jax.ShapeDtypeStruc...  17.3 us
    ppermute x1, waiting for transfers between devices, per_device(): lax.ppermute(second, 'obs', [(p, p ^ 2) for p in range(obs_count)])  4.49 us
    unnamed x11, local copies, waits for them, and re-layouts  3.99 us
    sort x1, other arithmetic, per_device(): inverse = jnp.argsort(segment_owner)  2.09 us
    ppermute x3, starting transfers between devices, per_device(): lax.ppermute(observer_places, 'obs', [(p, p ^ k) for p in range(obs_count)])  1.86 us
    ppermute x1, starting transfers between devices, per_device(): lax.ppermute(second, 'obs', [(p, p ^ 2) for p in range(obs_count)])  1.51 us
  transfers between devices with their start and end apart: 5, of which 2 were waited for; matrix products, arithmetic and copies ran while one was open for 8% of the time, Pallas kernels for 15%

profile of v13, /device:TPU:24, one launch (start us, length us, event | category | flops | bytes accessed | tf_op | source)
XLA Modules:
  0.0 65.5 jit_solution(2682059930755430904)
XLA Ops:
  0.0 0.9 %collective-permute-start = (f32[3,256]{1,0:T(4,128)}, f32[3,256]{1,0:T(4,128)S(1)}, u32[]{:S(2)}, u32[]{:S(2)}) collective-permute-start(f32[3,256]{1,0:T(4,128)} %param.8), channel_id=1, source_target_pairs={{0,192},{64,128},{128,64},{192,0},{1,193},{65,129},{129,65},{193,1... | collective-permute-start | bytes 9224 | tf_op jit(solution)/shard_map/ppermute | solution.py:52
  0.9 0.6 collective-permute-start.1
  1.5 0.4 collective-permute-start.2
  1.9 0.6 pad_add_fusion.order_ref
  2.5 0.0 copy-start
  2.5 0.7 %copy-done = f32[1,3,512]{2,0,1:T(1,128)S(1)} copy-done((f32[1,3,512]{2,0,1:T(1,128)S(1)}, f32[1,3,512]{2,0,1:T(1,128)}, u32[]{:S(2)}) %copy-start) | copy-done | bytes 6168
  3.2 0.0 copy-start.2
  3.2 0.6 copy.15
  3.8 0.1 copy-done.2
  3.9 0.0 copy-start.1
  3.9 0.7 %copy.10.bins_ref = s32[8,1,4]{2,1,0:T(1,128)} copy(s32[8,1,4]{0,2,1:T(4,128)S(1)} %copy-done.2) | data formatting | bytes 256 | tf_op args[4]
  4.6 0.0 collective-permute-done
  4.6 0.2 collective-permute-done.1
  4.8 0.0 collective-permute-done.2
  4.8 0.0 copy-done.1
  4.8 0.6 pad_maximum_fusion.1.obs_ref
  5.4 7.3 %shard_map.65 = f32[4,384,128]{2,1,0:T(8,128)} custom-call(s32[8,1,4]{2,1,0:T(1,128)} %copy.10.bins_ref, s32[4]{0:T(128)} %pad_add_fusion.order_ref, f32[3,1024]{1,0:T(4,128)} %pad_maximum_fusion.1.obs_ref, f32[3,512]{1,0:T(4,128)} %bitcast.12, bf16[1024,512]{1,0:T(8,128)(2,1)} %bitcast.6, bf16[4,512,256]{2,1,0:T(8,128)(2,1)} %bitcast.9), custom_call_target="tpu_custom_call" | custom-call | tf_op jit(solution)/shard_map/pallas_call | solution.py:77
  12.7 0.0 collective-permute-start.3
  12.7 0.0 copy-start.3
  12.7 0.6 copy-done.3
  13.3 2.1 %sort.17 = (s32[64]{0:T(128)}, s32[64]{0:T(128)S(1)}) sort(s32[64]{0:T(128)S(1)} %copy-done.3, s32[64]{0:T(128)S(1)} %iota.17), dimensions={0}, to_apply=%region_0.1 | sort | flops 384 | bytes 1024 | tf_op jit(solution)/shard_map/jit(argsort)/sort | solution.py:102
  15.4 0.6 iota_add_fusion.order_ref
  16.0 5.0 %shard_map.66 = f32[2,384,128]{2,1,0:T(8,128)} custom-call(s32[8,1,4]{2,1,0:T(1,128)} %copy.10.bins_ref, s32[2]{0:T(128)} %iota_add_fusion.order_ref, f32[3,1024]{1,0:T(4,128)} %pad_maximum_fusion.1.obs_ref, f32[3,512]{1,0:T(4,128)} %bitcast.13, bf16[1024,512]{1,0:T(8,128)(2,1)} %bitcast.7, bf16[4,512,256]{2,1,0:T(8,128)(2,1)} %bitcast.10), custom_call_target="tpu_custom_call" | custom-call | tf_op jit(solution)/shard_map/pallas_call | solution.py:77
  21.0 0.0 collective-permute-done.3
  21.0 1.1 %select_add_fusion = f32[2,384,128]{2,1,0:T(8,128)S(1)} fusion(f32[2,384,128]{2,1,0:T(8,128)} %shard_map.66, f32[4,384,128]{2,1,0:T(8,128)S(1)} %collective-permute-done.3, pred[]{:T(512)S(6)} %eq.52), kind=kLoop, calls=%fused_computation.2 | loop fusion | flops 196608 | bytes 1572865 | tf_op jit(solution)/shard_map/add | solution.py:93
  22.1 1.5 %collective-permute-start.4 = (f32[2,384,128]{2,1,0:T(8,128)S(1)}, f32[2,384,128]{2,1,0:T(8,128)S(1)}, u32[]{:S(2)}, u32[]{:S(2)}) collective-permute-start(f32[2,384,128]{2,1,0:T(8,128)S(1)} %select_add_fusion), channel_id=1, source_target_pairs={{0,128},{64,192},{128,0},{192,64},{1,129},{65,193},{129,1},{193,65... | collective-permute-start | bytes 1179656 | tf_op jit(solution)/shard_map/ppermute | solution.py:94
  23.6 0.6 iota_add_fusion.3.order_ref
  24.2 5.0 %shard_map.64 = f32[2,384,128]{2,1,0:T(8,128)} custom-call(s32[8,1,4]{2,1,0:T(1,128)} %copy.10.bins_ref, s32[2]{0:T(128)} %iota_add_fusion.3.order_ref, f32[3,1024]{1,0:T(4,128)} %pad_maximum_fusion.1.obs_ref, f32[3,512]{1,0:T(4,128)} %bitcast.14, bf16[1024,512]{1,0:T(8,128)(2,1)} %bitcast.8, bf16[4,512,256]{2,1,0:T(8,128)(2,1)} %bitcast.11), custom_call_target="tpu_custom_call" | custom-call | tf_op jit(solution)/shard_map/pallas_call | solution.py:77
  29.2 4.5 %collective-permute-done.4 = f32[2,384,128]{2,1,0:T(8,128)S(1)} collective-permute-done((f32[2,384,128]{2,1,0:T(8,128)S(1)}, f32[2,384,128]{2,1,0:T(8,128)S(1)}, u32[]{:S(2)}, u32[]{:S(2)}) %collective-permute-start.4) | collective-permute-done | bytes 393248 | tf_op jit(solution)/shard_map/ppermute | solution.py:94
  33.7 1.1 %add_add_fusion = f32[2,384,128]{2,1,0:T(8,128)S(1)} fusion(f32[2,384,128]{2,1,0:T(8,128)S(1)} %collective-permute-done.4, f32[2,384,128]{2,1,0:T(8,128)} %shard_map.64, f32[4,384,128]{2,1,0:T(8,128)S(1)} %collective-permute-done.3, pred[]{:T(512)S(6)} %eq.52), kind=kLoop, calls=%fused_computation.3 | loop fusion | flops 294912 | bytes 1966081 | tf_op jit(solution)/shard_map/add | solution.py:96
  34.9 0.6 gather_fusion
  35.6 0.8 %pad.4.x_ref = f32[64,8,256]{2,1,0:T(8,128)} pad(f32[64,6,256]{2,1,0:T(8,128)S(1)} %gather_fusion, f32[]{:T(128)} %constant.19.clone.1), padding=0_0x0_2x0_0 | pad | bytes 917508 | tf_op jit(solution)/shard_map/jit(_pad)/pad | solution.py:105
  36.4 27.8 %shard_map.67 = f32[8,256]{1,0:T(8,128)} custom-call(f32[64,8,256]{2,1,0:T(8,128)} %pad.4.x_ref), custom_call_target="tpu_custom_call" | custom-call | tf_op jit(solution)/shard_map/pallas_call | solution.py:168
  64.2 1.3 %copy.17 = f32[6,256]{1,0:T(8,128)} copy(f32[6,256]{1,0:T(8,128)} %bitcast.15) | data formatting | bytes 12288
  (9 shorter events, 0.2 us)
Async XLA Ops:
  0.0 4.6 %collective-permute-start = (f32[3,256]{1,0:T(4,128)}, f32[3,256]{1,0:T(4,128)S(1)}, u32[]{:S(2)}, u32[]{:S(2)}) collective-permute-start(f32[3,256]{1,0:T(4,128)} %param.8), channel_id=1, source_target_pairs={{0,192},{64,128},{128,64},{192,0},{1,193},{65,129},{129,65},{193,1... | collective-permute-start | bytes 9224 | tf_op jit(solution)/shard_map/ppermute | solution.py:52
  0.9 3.8 %collective-permute-start.1 = (f32[3,256]{1,0:T(4,128)}, f32[3,256]{1,0:T(4,128)S(1)}, u32[]{:S(2)}, u32[]{:S(2)}) collective-permute-start(f32[3,256]{1,0:T(4,128)} %param.8), channel_id=1, source_target_pairs={{0,128},{64,192},{128,0},{192,64},{1,129},{65,193},{129,1},{193,65... | collective-permute-start | bytes 9224 | tf_op jit(solution)/shard_map/ppermute | solution.py:52
  1.5 3.3 %collective-permute-start.2 = (f32[3,256]{1,0:T(4,128)}, f32[3,256]{1,0:T(4,128)S(1)}, u32[]{:S(2)}, u32[]{:S(2)}) collective-permute-start(f32[3,256]{1,0:T(4,128)} %param.8), channel_id=1, source_target_pairs={{0,64},{64,0},{128,192},{192,128},{1,65},{65,1},{129,193},{193,129... | collective-permute-start | bytes 9224 | tf_op jit(solution)/shard_map/ppermute | solution.py:52
  2.5 0.7 %copy-start = (f32[1,3,512]{2,0,1:T(1,128)S(1)}, f32[1,3,512]{2,0,1:T(1,128)}, u32[]{:S(2)}) copy-start(f32[1,3,512]{2,0,1:T(1,128)} %param.7) | copy-start | bytes 18436
  3.2 0.7 %copy-start.2 = (s32[8,1,4]{0,2,1:T(4,128)S(1)}, s32[8,1,4]{0,2,1:T(4,128)}, u32[]{:S(2)}) copy-start(s32[8,1,4]{0,2,1:T(4,128)} %param.10) | copy-start | bytes 388
  3.9 0.9 %copy-start.1 = (f32[3,256]{1,0:T(4,128)S(1)}, f32[3,256]{1,0:T(4,128)}, u32[]{:S(2)}) copy-start(f32[3,256]{1,0:T(4,128)} %param.8) | copy-start | bytes 9220
  12.7 8.4 %collective-permute-start.3 = (f32[4,384,128]{2,1,0:T(8,128)}, f32[4,384,128]{2,1,0:T(8,128)S(1)}, u32[]{:S(2)}, u32[]{:S(2)}) collective-permute-start(f32[4,384,128]{2,1,0:T(8,128)} %shard_map.65), channel_id=1, source_target_pairs={{0,64},{64,0},{128,192},{192,128},{1,65},{65,1},{129,193},{193,129... | collective-permute-start | bytes 2359304 | tf_op jit(solution)/shard_map/ppermute | solution.py:91
  12.7 0.7 %copy-start.3 = (s32[64]{0:T(128)S(1)}, s32[64]{0:T(128)}, u32[]{:S(2)}) copy-start(s32[64]{0:T(128)} %param.11) | copy-start | bytes 772
  22.1 11.6 %collective-permute-start.4 = (f32[2,384,128]{2,1,0:T(8,128)S(1)}, f32[2,384,128]{2,1,0:T(8,128)S(1)}, u32[]{:S(2)}, u32[]{:S(2)}) collective-permute-start(f32[2,384,128]{2,1,0:T(8,128)S(1)} %select_add_fusion), channel_id=1, source_target_pairs={{0,128},{64,192},{128,0},{192,64},{1,129},{65,193},{129,1},{193,65... | collective-permute-start | bytes 1179656 | tf_op jit(solution)/shard_map/ppermute | solution.py:94

commit v14 on v12

--- a/solution.py
+++ b/solution.py
@@ -93,9 +93,7 @@
     arranged = reduced.reshape(segment_count, seg_len, reduced.shape[1])
     inverse = jnp.argsort(segment_owner)
     arranged = arranged[inverse]
-    rows = -(-seg_len // 8) * 8
-    padded = jnp.pad(arranged, ((0, 0), (0, rows - seg_len), (0, 0)))
-    return exchange_sum(padded)[:seg_len]
+    return exchange_sum(arranged)
 
 
 def exchange_kernel(x_ref, out_ref, slots, send_sem, recv_sem):

time: 64.1 us -> 64.1 us (level)
    pad x1 -> x0, local copies, waits for them, and re-layouts: 0.82 us -> none  [per_device(): padded = jnp.pad(arranged, ((0, 0), (0, rows - seg_len), (0, 0)))]
    gather x1, local copies, waits for them, and re-layouts: 0.63 us -> 1.42 us  [per_device(): arranged = arranged[inverse]]
where the time goes in v14:
time: 64.1 us; the launch traced here: 63.7 us
  Pallas kernels  39.4 us (61%)
  waiting for transfers between devices  10.4 us (16%)
  local copies, waits for them, and re-layouts  5.41 us (8%)
  other arithmetic  5.21 us (8%)
  starting transfers between devices  3.29 us (5%)
    pallas_call x1, Pallas kernels, exchange_sum(): pl.pallas_call(exchange_kernel, out_shape=jax.ShapeDtypeStruct(data.shape...  27.5 us
    pallas_call x1, Pallas kernels, per_device(): pl.pallas_call(kernel, grid_spec=grid_spec, out_shape=jax.ShapeDtypeStruc...  11.8 us
    ppermute x2, waiting for transfers between devices, per_device(): halves = keep + lax.ppermute(send, 'obs', pairs)  10.1 us
    unnamed x7, local copies, waits for them, and re-layouts  3.94 us
    sort x1, other arithmetic, per_device(): inverse = jnp.argsort(segment_owner)  2.03 us
    ppermute x3, starting transfers between devices, per_device(): lax.ppermute(observer_places, 'obs', [(p, p ^ k) for p in range(obs_count)])  1.86 us
    select_n x2, other arithmetic, per_device(): send = jnp.where(mine == 1, low, high)  1.64 us
    ppermute x2, starting transfers between devices, per_device(): halves = keep + lax.ppermute(send, 'obs', pairs)  1.43 us
  transfers between devices with their start and end apart: 5, of which 3 were waited for; matrix products, arithmetic and copies ran while one was open for 7% of the time, Pallas kernels for 0%

profile of v14, /device:TPU:24, one launch (start us, length us, event | category | flops | bytes accessed | tf_op | source)
XLA Modules:
  0.0 63.7 jit_solution(5397559806725592060)
XLA Ops:
  0.0 0.9 %collective-permute-start = (f32[3,256]{1,0:T(4,128)}, f32[3,256]{1,0:T(4,128)S(1)}, u32[]{:S(2)}, u32[]{:S(2)}) collective-permute-start(f32[3,256]{1,0:T(4,128)} %param.8), channel_id=1, source_target_pairs={{0,192},{64,128},{128,64},{192,0},{1,193},{65,129},{129,65},{193,1... | collective-permute-start | bytes 9224 | tf_op jit(solution)/shard_map/ppermute | solution.py:52
  0.9 0.6 collective-permute-start.1
  1.5 0.4 collective-permute-start.2
  1.9 1.3 %copy.19 = f32[1,3,512]{2,1,0:T(4,128)} copy(f32[1,3,512]{2,0,1:T(1,128)} %param.7) | data formatting | bytes 12288
  3.2 1.3 %copy.12.bins_ref = s32[8,1,4]{2,1,0:T(1,128)} copy(s32[8,1,4]{0,2,1:T(4,128)} %param.10) | data formatting | bytes 256 | tf_op args[4]
  4.5 0.0 collective-permute-done
  4.5 0.2 collective-permute-done.1
  4.8 0.0 collective-permute-done.2
  4.8 0.7 %select_select_fusion.3 = (f32[3,256]{1,0:T(4,128)S(1)}, f32[3,256]{1,0:T(4,128)S(1)}, f32[3,256]{1,0:T(4,128)S(1)}, f32[3,256]{1,0:T(4,128)S(1)}) fusion(f32[3,256]{1,0:T(4,128)S(1)} %collective-permute-done, f32[3,256]{1,0:T(4,128)S(1)} %collective-permute-done.1, f32[3,256]{1,0:T(4,128)S(1)} %collective-permute-done.2, f32[3,256]{1,0:T(4,128)} %param.8, ...), kind=kLoop, calls=%fused_computation.13 | loop fusion | flops 9216 | bytes 24588 | tf_op jit(solution)/shard_map/jit(_where)/select_n | solution.py:58
  5.5 0.6 pad_maximum_fusion.obs_ref
  6.1 11.8 %shard_map.64 = f32[4,384,256]{2,1,0:T(8,128)} custom-call(s32[8,1,4]{2,1,0:T(1,128)} %copy.12.bins_ref, f32[3,1024]{1,0:T(4,128)} %pad_maximum_fusion.obs_ref, f32[3,512]{1,0:T(4,128)} %bitcast.30, bf16[1024,512]{1,0:T(8,128)(2,1)} %bitcast.28, bf16[4,512,256]{2,1,0:T(8,128)(2,1)} %bitcast.29), custom_call_target="tpu_custom_call" | custom-call | tf_op jit(solution)/shard_map/pallas_call | solution.py:75
  17.9 0.0 copy-start
  17.9 1.6 %select_bitcast_fusion = f32[2,384,256]{2,1,0:T(8,128)S(1)} fusion(f32[2,2,384,256]{3,2,1,0:T(8,128)} %bitcast.26, pred[]{:T(512)S(6)} %eq.45), kind=kLoop, calls=%fused_computation.4 | loop fusion | flops 196608 | bytes 2359297 | tf_op jit(solution)/shard_map/jit(_where)/select_n | solution.py:87
  19.5 0.1 collective-permute-start.3
  19.6 0.0 copy-start.1
  19.6 2.3 %collective-permute-done.3 = f32[2,384,256]{2,1,0:T(8,128)S(1)} collective-permute-done((f32[2,384,256]{2,1,0:T(8,128)S(1)}, f32[2,384,256]{2,1,0:T(8,128)S(1)}, u32[]{:S(2)}, u32[]{:S(2)}) %collective-permute-start.3) | collective-permute-done | bytes 786464 | tf_op jit(solution)/shard_map/ppermute | solution.py:89
  21.9 0.0 copy-done
  21.9 0.2 bitcast_add_fusion
  22.0 0.1 select_bitcast_fusion.1
  22.1 1.3 %collective-permute-start.4 = (f32[384,256]{1,0:T(8,128)S(1)}, f32[384,256]{1,0:T(8,128)S(1)}, u32[]{:S(2)}, u32[]{:S(2)}) collective-permute-start(f32[384,256]{1,0:T(8,128)S(1)} %select_bitcast_fusion.1), channel_id=1, source_target_pairs={{0,128},{64,192},{128,0},{192,64},{1,129},{65,193},{129,1},{193,65... | collective-permute-start | bytes 1179656 | tf_op jit(solution)/shard_map/ppermute | solution.py:89
  23.4 0.0 copy-done.1
  23.4 2.0 %sort.17 = (s32[64]{0:T(128)}, s32[64]{0:T(128)S(1)}) sort(s32[64]{0:T(128)S(1)} %copy-done.1, s32[64]{0:T(128)S(1)} %iota.4), dimensions={0}, to_apply=%region_0.1 | sort | flops 384 | bytes 1024 | tf_op jit(solution)/shard_map/jit(argsort)/sort | solution.py:94
  25.5 7.9 %collective-permute-done.4 = f32[384,256]{1,0:T(8,128)S(1)} collective-permute-done((f32[384,256]{1,0:T(8,128)S(1)}, f32[384,256]{1,0:T(8,128)S(1)}, u32[]{:S(2)}, u32[]{:S(2)}) %collective-permute-start.4) | collective-permute-done | bytes 393248 | tf_op jit(solution)/shard_map/ppermute | solution.py:89
  33.3 0.1 bitcast_add_fusion.1
  33.4 0.1 reshape.15
  33.5 1.4 %gather_fusion = f32[64,6,256]{2,1,0:T(8,128)} fusion(f32[64,6,256]{2,1,0:T(8,128)S(1)} %reshape.15, s32[1024]{0:T(1024)S(1)} %pad_clamp_fusion), kind=kCustom, calls=%fused_computation | custom fusion | bytes 786688 | tf_op jit(solution)/shard_map/gather | solution.py:95
  34.9 27.5 %shard_map.65 = f32[6,256]{1,0:T(8,128)} custom-call(f32[64,6,256]{2,1,0:T(8,128)} %gather_fusion), custom_call_target="tpu_custom_call" | custom-call | tf_op jit(solution)/shard_map/pallas_call | solution.py:158
  62.4 1.3 %copy.21 = f32[6,256]{1,0:T(8,128)} copy(f32[6,256]{1,0:T(8,128)} %shard_map.65) | data formatting | bytes 12288
  (3 shorter events, 0.0 us)
Async XLA Ops:
  0.0 4.5 %collective-permute-start = (f32[3,256]{1,0:T(4,128)}, f32[3,256]{1,0:T(4,128)S(1)}, u32[]{:S(2)}, u32[]{:S(2)}) collective-permute-start(f32[3,256]{1,0:T(4,128)} %param.8), channel_id=1, source_target_pairs={{0,192},{64,128},{128,64},{192,0},{1,193},{65,129},{129,65},{193,1... | collective-permute-start | bytes 9224 | tf_op jit(solution)/shard_map/ppermute | solution.py:52
  0.9 3.8 %collective-permute-start.1 = (f32[3,256]{1,0:T(4,128)}, f32[3,256]{1,0:T(4,128)S(1)}, u32[]{:S(2)}, u32[]{:S(2)}) collective-permute-start(f32[3,256]{1,0:T(4,128)} %param.8), channel_id=1, source_target_pairs={{0,128},{64,192},{128,0},{192,64},{1,129},{65,193},{129,1},{193,65... | collective-permute-start | bytes 9224 | tf_op jit(solution)/shard_map/ppermute | solution.py:52
  1.5 3.3 %collective-permute-start.2 = (f32[3,256]{1,0:T(4,128)}, f32[3,256]{1,0:T(4,128)S(1)}, u32[]{:S(2)}, u32[]{:S(2)}) collective-permute-start(f32[3,256]{1,0:T(4,128)} %param.8), channel_id=1, source_target_pairs={{0,64},{64,0},{128,192},{192,128},{1,65},{65,1},{129,193},{193,129... | collective-permute-start | bytes 9224 | tf_op jit(solution)/shard_map/ppermute | solution.py:52
  17.9 4.0 %copy-start = (f32[4,384,256]{2,1,0:T(8,128)S(1)}, f32[4,384,256]{2,1,0:T(8,128)}, u32[]{:S(2)}) copy-start(f32[4,384,256]{2,1,0:T(8,128)} %shard_map.64) | copy-start | bytes 4718596
  19.5 2.4 %collective-permute-start.3 = (f32[2,384,256]{2,1,0:T(8,128)S(1)}, f32[2,384,256]{2,1,0:T(8,128)S(1)}, u32[]{:S(2)}, u32[]{:S(2)}) collective-permute-start(f32[2,384,256]{2,1,0:T(8,128)S(1)} %select_bitcast_fusion), channel_id=1, source_target_pairs={{0,64},{64,0},{128,192},{192,128},{1,65},{65,1},{129,193},{193,129... | collective-permute-start | bytes 2359304 | tf_op jit(solution)/shard_map/ppermute | solution.py:89
  19.6 3.8 %copy-start.1 = (s32[64]{0:T(128)S(1)}, s32[64]{0:T(128)}, u32[]{:S(2)}) copy-start(s32[64]{0:T(128)} %param.11) | copy-start | bytes 772
  22.1 11.2 %collective-permute-start.4 = (f32[384,256]{1,0:T(8,128)S(1)}, f32[384,256]{1,0:T(8,128)S(1)}, u32[]{:S(2)}, u32[]{:S(2)}) collective-permute-start(f32[384,256]{1,0:T(8,128)S(1)} %select_bitcast_fusion.1), channel_id=1, source_target_pairs={{0,128},{64,192},{128,0},{192,64},{1,129},{65,193},{129,1},{193,65... | collective-permute-start | bytes 1179656 | tf_op jit(solution)/shard_map/ppermute | solution.py:89

commit v15 on v14

--- a/solution.py
+++ b/solution.py
@@ -34,7 +34,7 @@
             hi_p = jnp.dot(hi_w, src, preferred_element_type=jnp.float32)
             low = lo_p if low is None else low + lo_p
             high = hi_p if high is None else high + hi_p
-        shift = bins_ref[ob, 0, pb]
+        shift = bins_ref[0, pb, ob]
         acc = acc + pltpu.roll(jnp.concatenate([low, pad], axis=1), shift, 1)
         acc = acc + pltpu.roll(jnp.concatenate([high, pad], axis=1), shift + 1, 1)
     out_ref[...] = acc.T
@@ -76,7 +76,7 @@
         kernel,
         grid_spec=grid_spec,
         out_shape=jax.ShapeDtypeStruct((obs_blocks // 2, bins_total, 2 * OBLK), jnp.float32),
-    )(delay_bins, every_obs, panel_places[0], fraction[:, 0, :], sources[0])
+    )(jnp.transpose(delay_bins, (1, 2, 0)), every_obs, panel_places[0], fraction[:, 0, :], sources[0])
     halves = totals.reshape((2, 2) + totals.shape[1:])
     me = lax.axis_index("obs")
     for bit, dim in ((0, 1), (1, 0)):

time: 64.1 us -> 63.9 us (level)
  waiting for transfers between devices: 10.4 us -> 12.4 us
  local copies, waits for them, and re-layouts: 5.41 us -> 4.07 us
  starting transfers between devices: 3.29 us -> 2.6 us
    ppermute x3, waiting for transfers between devices: 0.25 us -> 1.6 us  [per_device(): lax.ppermute(observer_places, 'obs', [(p, p ^ k) for p in range(obs_count)])]
    unnamed x7 -> x6, local copies, waits for them, and re-layouts: 3.94 us -> 2.6 us
    ppermute x2, starting transfers between devices: 1.43 us -> 0.74 us  [per_device(): halves = keep + lax.ppermute(send, 'obs', pairs)]
    ppermute x2, waiting for transfers between devices: 10.1 us -> 10.8 us  [per_device(): halves = keep + lax.ppermute(send, 'obs', pairs)]
  transfers between devices with their start and end apart: 5 -> 5, of which waited for: 3 -> 4; matrix products, arithmetic and copies ran while one was open for 7% -> 5% of each run, Pallas kernels for 0% -> 0%
where the time goes in v15:
time: 63.9 us; the launch traced here: 63.6 us
  Pallas kernels  39.3 us (62%)
  waiting for transfers between devices  12.4 us (19%)
  other arithmetic  5.21 us (8%)
  local copies, waits for them, and re-layouts  4.07 us (6%)
  starting transfers between devices  2.6 us (4%)
    pallas_call x1, Pallas kernels, exchange_sum(): pl.pallas_call(exchange_kernel, out_shape=jax.ShapeDtypeStruct(data.shape...  27.5 us
    pallas_call x1, Pallas kernels, per_device(): pl.pallas_call(kernel, grid_spec=grid_spec, out_shape=jax.ShapeDtypeStruc...  11.8 us
    ppermute x2, waiting for transfers between devices, per_device(): halves = keep + lax.ppermute(send, 'obs', pairs)  10.8 us
    unnamed x6, local copies, waits for them, and re-layouts  2.6 us
    sort x1, other arithmetic, per_device(): inverse = jnp.argsort(segment_owner)  2.03 us
    ppermute x3, starting transfers between devices, per_device(): lax.ppermute(observer_places, 'obs', [(p, p ^ k) for p in range(obs_count)])  1.86 us
    select_n x2, other arithmetic, per_device(): send = jnp.where(mine == 1, low, high)  1.64 us
    ppermute x3, waiting for transfers between devices, per_device(): lax.ppermute(observer_places, 'obs', [(p, p ^ k) for p in range(obs_count)])  1.6 us
  transfers between devices with their start and end apart: 5, of which 4 were waited for; matrix products, arithmetic and copies ran while one was open for 5% of the time, Pallas kernels for 0%

profile of v15, /device:TPU:24, one launch (start us, length us, event | category | flops | bytes accessed | tf_op | source)
XLA Modules:
  0.0 63.6 jit_solution(1129664524155949708)
XLA Ops:
  0.0 0.9 %collective-permute-start = (f32[3,256]{1,0:T(4,128)}, f32[3,256]{1,0:T(4,128)S(1)}, u32[]{:S(2)}, u32[]{:S(2)}) collective-permute-start(f32[3,256]{1,0:T(4,128)} %param.8), channel_id=1, source_target_pairs={{0,192},{64,128},{128,64},{192,0},{1,193},{65,129},{129,65},{193,1... | collective-permute-start | bytes 9224 | tf_op jit(solution)/shard_map/ppermute | solution.py:52
  0.9 0.6 collective-permute-start.1
  1.5 0.4 collective-permute-start.2
  1.9 1.3 %copy.17 = f32[1,3,512]{2,1,0:T(4,128)} copy(f32[1,3,512]{2,0,1:T(1,128)} %param.7) | data formatting | bytes 12288
  3.2 0.1 collective-permute-done
  3.2 1.5 %collective-permute-done.1 = f32[3,256]{1,0:T(4,128)S(1)} collective-permute-done((f32[3,256]{1,0:T(4,128)}, f32[3,256]{1,0:T(4,128)S(1)}, u32[]{:S(2)}, u32[]{:S(2)}) %collective-permute-start.1) | collective-permute-done | bytes 3104 | tf_op jit(solution)/shard_map/ppermute | solution.py:52
  4.8 0.0 collective-permute-done.2
  4.8 0.7 %select_select_fusion.3 = (f32[3,256]{1,0:T(4,128)S(1)}, f32[3,256]{1,0:T(4,128)S(1)}, f32[3,256]{1,0:T(4,128)S(1)}, f32[3,256]{1,0:T(4,128)S(1)}) fusion(f32[3,256]{1,0:T(4,128)S(1)} %collective-permute-done, f32[3,256]{1,0:T(4,128)S(1)} %collective-permute-done.1, f32[3,256]{1,0:T(4,128)S(1)} %collective-permute-done.2, f32[3,256]{1,0:T(4,128)} %param.8, ...), kind=kLoop, calls=%fused_computation.13 | loop fusion | flops 9216 | bytes 24588 | tf_op jit(solution)/shard_map/jit(_where)/select_n | solution.py:58
  5.5 0.6 pad_maximum_fusion.obs_ref
  6.1 11.8 %shard_map.64 = f32[4,384,256]{2,1,0:T(8,128)} custom-call(s32[1,4,8]{2,1,0:T(4,128)} %bitcast.32, f32[3,1024]{1,0:T(4,128)} %pad_maximum_fusion.obs_ref, f32[3,512]{1,0:T(4,128)} %bitcast.31, bf16[1024,512]{1,0:T(8,128)(2,1)} %bitcast.29, bf16[4,512,256]{2,1,0:T(8,128)(2,1)} %bitcast.30), custom_call_target="tpu_custom_call" | custom-call | tf_op jit(solution)/shard_map/pallas_call | solution.py:75
  17.9 0.0 copy-start
  17.9 1.6 %select_bitcast_fusion = f32[2,384,256]{2,1,0:T(8,128)S(1)} fusion(f32[2,2,384,256]{3,2,1,0:T(8,128)} %bitcast.27, pred[]{:T(512)S(6)} %eq.45), kind=kLoop, calls=%fused_computation.4 | loop fusion | flops 196608 | bytes 2359297 | tf_op jit(solution)/shard_map/jit(_where)/select_n | solution.py:87
  19.5 0.1 collective-permute-start.3
  19.6 0.0 copy-start.1
  19.6 2.3 %collective-permute-done.3 = f32[2,384,256]{2,1,0:T(8,128)S(1)} collective-permute-done((f32[2,384,256]{2,1,0:T(8,128)S(1)}, f32[2,384,256]{2,1,0:T(8,128)S(1)}, u32[]{:S(2)}, u32[]{:S(2)}) %collective-permute-start.3) | collective-permute-done | bytes 786464 | tf_op jit(solution)/shard_map/ppermute | solution.py:89
  21.8 0.0 copy-done
  21.8 0.2 bitcast_add_fusion
  22.0 0.1 select_bitcast_fusion.1
  22.0 0.6 %collective-permute-start.4 = (f32[384,256]{1,0:T(8,128)S(1)}, f32[384,256]{1,0:T(8,128)S(1)}, u32[]{:S(2)}, u32[]{:S(2)}) collective-permute-start(f32[384,256]{1,0:T(8,128)S(1)} %select_bitcast_fusion.1), channel_id=1, source_target_pairs={{0,128},{64,192},{128,0},{192,64},{1,129},{65,193},{129,1},{193,65... | collective-permute-start | bytes 1179656 | tf_op jit(solution)/shard_map/ppermute | solution.py:89
  22.7 0.0 copy-done.1
  22.7 2.0 %sort.17 = (s32[64]{0:T(128)}, s32[64]{0:T(128)S(1)}) sort(s32[64]{0:T(128)S(1)} %copy-done.1, s32[64]{0:T(128)S(1)} %iota.4), dimensions={0}, to_apply=%region_0.1 | sort | flops 384 | bytes 1024 | tf_op jit(solution)/shard_map/jit(argsort)/sort | solution.py:94
  24.8 8.5 %collective-permute-done.4 = f32[384,256]{1,0:T(8,128)S(1)} collective-permute-done((f32[384,256]{1,0:T(8,128)S(1)}, f32[384,256]{1,0:T(8,128)S(1)}, u32[]{:S(2)}, u32[]{:S(2)}) %collective-permute-start.4) | collective-permute-done | bytes 393248 | tf_op jit(solution)/shard_map/ppermute | solution.py:89
  33.3 0.1 bitcast_add_fusion.1
  33.4 0.1 reshape.15
  33.4 1.4 %gather_fusion = f32[64,6,256]{2,1,0:T(8,128)} fusion(f32[64,6,256]{2,1,0:T(8,128)S(1)} %reshape.15, s32[1024]{0:T(1024)S(1)} %pad_clamp_fusion), kind=kCustom, calls=%fused_computation | custom fusion | bytes 786688 | tf_op jit(solution)/shard_map/gather | solution.py:95
  34.8 27.5 %shard_map.65 = f32[6,256]{1,0:T(8,128)} custom-call(f32[64,6,256]{2,1,0:T(8,128)} %gather_fusion), custom_call_target="tpu_custom_call" | custom-call | tf_op jit(solution)/shard_map/pallas_call | solution.py:158
  62.3 1.3 %copy.19 = f32[6,256]{1,0:T(8,128)} copy(f32[6,256]{1,0:T(8,128)} %shard_map.65) | data formatting | bytes 12288
  (3 shorter events, 0.0 us)
Async XLA Ops:
  0.0 3.2 %collective-permute-start = (f32[3,256]{1,0:T(4,128)}, f32[3,256]{1,0:T(4,128)S(1)}, u32[]{:S(2)}, u32[]{:S(2)}) collective-permute-start(f32[3,256]{1,0:T(4,128)} %param.8), channel_id=1, source_target_pairs={{0,192},{64,128},{128,64},{192,0},{1,193},{65,129},{129,65},{193,1... | collective-permute-start | bytes 9224 | tf_op jit(solution)/shard_map/ppermute | solution.py:52
  0.9 3.8 %collective-permute-start.1 = (f32[3,256]{1,0:T(4,128)}, f32[3,256]{1,0:T(4,128)S(1)}, u32[]{:S(2)}, u32[]{:S(2)}) collective-permute-start(f32[3,256]{1,0:T(4,128)} %param.8), channel_id=1, source_target_pairs={{0,128},{64,192},{128,0},{192,64},{1,129},{65,193},{129,1},{193,65... | collective-permute-start | bytes 9224 | tf_op jit(solution)/shard_map/ppermute | solution.py:52
  1.5 3.3 %collective-permute-start.2 = (f32[3,256]{1,0:T(4,128)}, f32[3,256]{1,0:T(4,128)S(1)}, u32[]{:S(2)}, u32[]{:S(2)}) collective-permute-start(f32[3,256]{1,0:T(4,128)} %param.8), channel_id=1, source_target_pairs={{0,64},{64,0},{128,192},{192,128},{1,65},{65,1},{129,193},{193,129... | collective-permute-start | bytes 9224 | tf_op jit(solution)/shard_map/ppermute | solution.py:52
  17.9 4.0 %copy-start = (f32[4,384,256]{2,1,0:T(8,128)S(1)}, f32[4,384,256]{2,1,0:T(8,128)}, u32[]{:S(2)}) copy-start(f32[4,384,256]{2,1,0:T(8,128)} %shard_map.64) | copy-start | bytes 4718596
  19.5 2.4 %collective-permute-start.3 = (f32[2,384,256]{2,1,0:T(8,128)S(1)}, f32[2,384,256]{2,1,0:T(8,128)S(1)}, u32[]{:S(2)}, u32[]{:S(2)}) collective-permute-start(f32[2,384,256]{2,1,0:T(8,128)S(1)} %select_bitcast_fusion), channel_id=1, source_target_pairs={{0,64},{64,0},{128,192},{192,128},{1,65},{65,1},{129,193},{193,129... | collective-permute-start | bytes 2359304 | tf_op jit(solution)/shard_map/ppermute | solution.py:89
  19.6 3.1 %copy-start.1 = (s32[64]{0:T(128)S(1)}, s32[64]{0:T(128)}, u32[]{:S(2)}) copy-start(s32[64]{0:T(128)} %param.11) | copy-start | bytes 772
  22.0 11.2 %collective-permute-start.4 = (f32[384,256]{1,0:T(8,128)S(1)}, f32[384,256]{1,0:T(8,128)S(1)}, u32[]{:S(2)}, u32[]{:S(2)}) collective-permute-start(f32[384,256]{1,0:T(8,128)S(1)} %select_bitcast_fusion.1), channel_id=1, source_target_pairs={{0,128},{64,192},{128,0},{192,64},{1,129},{65,193},{129,1},{193,65... | collective-permute-start | bytes 1179656 | tf_op jit(solution)/shard_map/ppermute | solution.py:89

commit v16 on v15

--- a/solution.py
+++ b/solution.py
@@ -20,7 +20,7 @@
     pad = jnp.zeros((OBLK, bins_total - window), jnp.float32)
     for pb in range(panel_blocks):
         cols = slice(pb * PBLK, (pb + 1) * PBLK)
-        seps = [here[:, c : c + 1] - place_ref[c : c + 1, cols] for c in range(3)]
+        seps = [here[:, c : c + 1] - place_ref[c, :, cols] for c in range(3)]
         dist_sq = seps[0] * seps[0] + seps[1] * seps[1] + seps[2] * seps[2]
         parts = [amplitude / jnp.sqrt(dist_sq)] + [amplitude * sep / dist_sq for sep in seps]
         weight = frac_ref[:, cols].astype(jnp.float32)
@@ -66,7 +66,7 @@
         grid=(obs_blocks,),
         in_specs=[
             pl.BlockSpec((3, OBLK), lambda i, b: (0, i)),
-            pl.BlockSpec((3, local_panels), lambda i, b: (0, 0)),
+            pl.BlockSpec((3, 1, local_panels), lambda i, b: (0, 0, 0)),
             pl.BlockSpec((OBLK, local_panels), lambda i, b: (i, 0)),
             pl.BlockSpec((4, local_panels, window), lambda i, b: (0, 0, 0)),
         ],
@@ -76,7 +76,7 @@
         kernel,
         grid_spec=grid_spec,
         out_shape=jax.ShapeDtypeStruct((obs_blocks // 2, bins_total, 2 * OBLK), jnp.float32),
-    )(jnp.transpose(delay_bins, (1, 2, 0)), every_obs, panel_places[0], fraction[:, 0, :], sources[0])
+    )(jnp.transpose(delay_bins, (1, 2, 0)), every_obs, jnp.transpose(panel_places, (1, 0, 2)), fraction[:, 0, :], sources[0])
     halves = totals.reshape((2, 2) + totals.shape[1:])
     me = lax.axis_index("obs")
     for bit, dim in ((0, 1), (1, 0)):

time: 63.9 us -> 63.9 us (level)
  waiting for transfers between devices: 12.4 us -> 13.7 us
  local copies, waits for them, and re-layouts: 4.07 us -> 2.78 us
    ppermute x3, waiting for transfers between devices: 1.6 us -> 2.89 us  [per_device(): lax.ppermute(observer_places, 'obs', [(p, p ^ k) for p in range(obs_count)])]
    unnamed x6 -> x5, local copies, waits for them, and re-layouts: 2.6 us -> 1.31 us
  transfers between devices with their start and end apart: 5 -> 5, of which waited for: 4 -> 4; matrix products, arithmetic and copies ran while one was open for 5% -> 3% of each run, Pallas kernels for 0% -> 0%
where the time goes in v16:
time: 63.9 us; the launch traced here: 63.6 us
  Pallas kernels  39.3 us (62%)
  waiting for transfers between devices  13.7 us (21%)
  other arithmetic  5.21 us (8%)
  local copies, waits for them, and re-layouts  2.78 us (4%)
  starting transfers between devices  2.6 us (4%)
    pallas_call x1, Pallas kernels, exchange_sum(): pl.pallas_call(exchange_kernel, out_shape=jax.ShapeDtypeStruct(data.shape...  27.5 us
    pallas_call x1, Pallas kernels, per_device(): pl.pallas_call(kernel, grid_spec=grid_spec, out_shape=jax.ShapeDtypeStruc...  11.8 us
    ppermute x2, waiting for transfers between devices, per_device(): halves = keep + lax.ppermute(send, 'obs', pairs)  10.8 us
    ppermute x3, waiting for transfers between devices, per_device(): lax.ppermute(observer_places, 'obs', [(p, p ^ k) for p in range(obs_count)])  2.89 us
    sort x1, other arithmetic, per_device(): inverse = jnp.argsort(segment_owner)  2.03 us
    ppermute x3, starting transfers between devices, per_device(): lax.ppermute(observer_places, 'obs', [(p, p ^ k) for p in range(obs_count)])  1.86 us
    select_n x2, other arithmetic, per_device(): send = jnp.where(mine == 1, low, high)  1.64 us
    gather x1, local copies, waits for them, and re-layouts, per_device(): arranged = arranged[inverse]  1.42 us
  transfers between devices with their start and end apart: 5, of which 4 were waited for; matrix products, arithmetic and copies ran while one was open for 3% of the time, Pallas kernels for 0%

profile of v16, /device:TPU:24, one launch (start us, length us, event | category | flops | bytes accessed | tf_op | source)
XLA Modules:
  0.0 63.6 jit_solution(10063069851214826235)
XLA Ops:
  0.0 0.9 %collective-permute-start = (f32[3,256]{1,0:T(4,128)}, f32[3,256]{1,0:T(4,128)S(1)}, u32[]{:S(2)}, u32[]{:S(2)}) collective-permute-start(f32[3,256]{1,0:T(4,128)} %param.8), channel_id=1, source_target_pairs={{0,192},{64,128},{128,64},{192,0},{1,193},{65,129},{129,65},{193,1... | collective-permute-start | bytes 9224 | tf_op jit(solution)/shard_map/ppermute | solution.py:52
  0.9 0.6 collective-permute-start.1
  1.5 0.4 collective-permute-start.2
  1.9 1.4 %collective-permute-done = f32[3,256]{1,0:T(4,128)S(1)} collective-permute-done((f32[3,256]{1,0:T(4,128)}, f32[3,256]{1,0:T(4,128)S(1)}, u32[]{:S(2)}, u32[]{:S(2)}) %collective-permute-start) | collective-permute-done | bytes 3104 | tf_op jit(solution)/shard_map/ppermute | solution.py:52
  3.2 1.5 %collective-permute-done.1 = f32[3,256]{1,0:T(4,128)S(1)} collective-permute-done((f32[3,256]{1,0:T(4,128)}, f32[3,256]{1,0:T(4,128)S(1)}, u32[]{:S(2)}, u32[]{:S(2)}) %collective-permute-start.1) | collective-permute-done | bytes 3104 | tf_op jit(solution)/shard_map/ppermute | solution.py:52
  4.8 0.0 collective-permute-done.2
  4.8 0.7 %select_select_fusion.3 = (f32[3,256]{1,0:T(4,128)S(1)}, f32[3,256]{1,0:T(4,128)S(1)}, f32[3,256]{1,0:T(4,128)S(1)}, f32[3,256]{1,0:T(4,128)S(1)}) fusion(f32[3,256]{1,0:T(4,128)S(1)} %collective-permute-done, f32[3,256]{1,0:T(4,128)S(1)} %collective-permute-done.1, f32[3,256]{1,0:T(4,128)S(1)} %collective-permute-done.2, f32[3,256]{1,0:T(4,128)} %param.8, ...), kind=kLoop, calls=%fused_computation.12 | loop fusion | flops 9216 | bytes 24588 | tf_op jit(solution)/shard_map/jit(_where)/select_n | solution.py:58
  5.5 0.6 pad_maximum_fusion.obs_ref
  6.1 11.8 %shard_map.64 = f32[4,384,256]{2,1,0:T(8,128)} custom-call(s32[1,4,8]{2,1,0:T(4,128)} %bitcast.30, f32[3,1024]{1,0:T(4,128)} %pad_maximum_fusion.obs_ref, f32[3,1,512]{2,1,0:T(1,128)} %bitcast.29, bf16[1024,512]{1,0:T(8,128)(2,1)} %bitcast.27, bf16[4,512,256]{2,1,0:T(8,128)(2,1)} %bitcast.28), custom_call_target="tpu_custom_call" | custom-call | tf_op jit(solution)/shard_map/pallas_call | solution.py:75
  17.9 0.0 copy-start
  17.9 1.6 %select_bitcast_fusion = f32[2,384,256]{2,1,0:T(8,128)S(1)} fusion(f32[2,2,384,256]{3,2,1,0:T(8,128)} %bitcast.25, pred[]{:T(512)S(6)} %eq.45), kind=kLoop, calls=%fused_computation.4 | loop fusion | flops 196608 | bytes 2359297 | tf_op jit(solution)/shard_map/jit(_where)/select_n | solution.py:87
  19.5 0.1 collective-permute-start.3
  19.6 0.0 copy-start.1
  19.6 2.3 %collective-permute-done.3 = f32[2,384,256]{2,1,0:T(8,128)S(1)} collective-permute-done((f32[2,384,256]{2,1,0:T(8,128)S(1)}, f32[2,384,256]{2,1,0:T(8,128)S(1)}, u32[]{:S(2)}, u32[]{:S(2)}) %collective-permute-start.3) | collective-permute-done | bytes 786464 | tf_op jit(solution)/shard_map/ppermute | solution.py:89
  21.8 0.0 copy-done
  21.8 0.2 bitcast_add_fusion
  22.0 0.1 select_bitcast_fusion.1
  22.0 0.7 %collective-permute-start.4 = (f32[384,256]{1,0:T(8,128)S(1)}, f32[384,256]{1,0:T(8,128)S(1)}, u32[]{:S(2)}, u32[]{:S(2)}) collective-permute-start(f32[384,256]{1,0:T(8,128)S(1)} %select_bitcast_fusion.1), channel_id=1, source_target_pairs={{0,128},{64,192},{128,0},{192,64},{1,129},{65,193},{129,1},{193,65... | collective-permute-start | bytes 1179656 | tf_op jit(solution)/shard_map/ppermute | solution.py:89
  22.7 0.0 copy-done.1
  22.7 2.0 %sort.17 = (s32[64]{0:T(128)}, s32[64]{0:T(128)S(1)}) sort(s32[64]{0:T(128)S(1)} %copy-done.1, s32[64]{0:T(128)S(1)} %iota.4), dimensions={0}, to_apply=%region_0.1 | sort | flops 384 | bytes 1024 | tf_op jit(solution)/shard_map/jit(argsort)/sort | solution.py:94
  24.7 8.5 %collective-permute-done.4 = f32[384,256]{1,0:T(8,128)S(1)} collective-permute-done((f32[384,256]{1,0:T(8,128)S(1)}, f32[384,256]{1,0:T(8,128)S(1)}, u32[]{:S(2)}, u32[]{:S(2)}) %collective-permute-start.4) | collective-permute-done | bytes 393248 | tf_op jit(solution)/shard_map/ppermute | solution.py:89
  33.3 0.1 bitcast_add_fusion.1
  33.4 0.1 reshape.15
  33.4 1.4 %gather_fusion = f32[64,6,256]{2,1,0:T(8,128)} fusion(f32[64,6,256]{2,1,0:T(8,128)S(1)} %reshape.15, s32[1024]{0:T(1024)S(1)} %pad_clamp_fusion), kind=kCustom, calls=%fused_computation | custom fusion | bytes 786688 | tf_op jit(solution)/shard_map/gather | solution.py:95
  34.8 27.5 %shard_map.65 = f32[6,256]{1,0:T(8,128)} custom-call(f32[64,6,256]{2,1,0:T(8,128)} %gather_fusion), custom_call_target="tpu_custom_call" | custom-call | tf_op jit(solution)/shard_map/pallas_call | solution.py:158
  62.3 1.3 %copy.16 = f32[6,256]{1,0:T(8,128)} copy(f32[6,256]{1,0:T(8,128)} %shard_map.65) | data formatting | bytes 12288
  (3 shorter events, 0.0 us)
Async XLA Ops:
  0.0 3.2 %collective-permute-start = (f32[3,256]{1,0:T(4,128)}, f32[3,256]{1,0:T(4,128)S(1)}, u32[]{:S(2)}, u32[]{:S(2)}) collective-permute-start(f32[3,256]{1,0:T(4,128)} %param.8), channel_id=1, source_target_pairs={{0,192},{64,128},{128,64},{192,0},{1,193},{65,129},{129,65},{193,1... | collective-permute-start | bytes 9224 | tf_op jit(solution)/shard_map/ppermute | solution.py:52
  0.9 3.8 %collective-permute-start.1 = (f32[3,256]{1,0:T(4,128)}, f32[3,256]{1,0:T(4,128)S(1)}, u32[]{:S(2)}, u32[]{:S(2)}) collective-permute-start(f32[3,256]{1,0:T(4,128)} %param.8), channel_id=1, source_target_pairs={{0,128},{64,192},{128,0},{192,64},{1,129},{65,193},{129,1},{193,65... | collective-permute-start | bytes 9224 | tf_op jit(solution)/shard_map/ppermute | solution.py:52
  1.5 3.3 %collective-permute-start.2 = (f32[3,256]{1,0:T(4,128)}, f32[3,256]{1,0:T(4,128)S(1)}, u32[]{:S(2)}, u32[]{:S(2)}) collective-permute-start(f32[3,256]{1,0:T(4,128)} %param.8), channel_id=1, source_target_pairs={{0,64},{64,0},{128,192},{192,128},{1,65},{65,1},{129,193},{193,129... | collective-permute-start | bytes 9224 | tf_op jit(solution)/shard_map/ppermute | solution.py:52
  17.9 4.0 %copy-start = (f32[4,384,256]{2,1,0:T(8,128)S(1)}, f32[4,384,256]{2,1,0:T(8,128)}, u32[]{:S(2)}) copy-start(f32[4,384,256]{2,1,0:T(8,128)} %shard_map.64) | copy-start | bytes 4718596
  19.5 2.4 %collective-permute-start.3 = (f32[2,384,256]{2,1,0:T(8,128)S(1)}, f32[2,384,256]{2,1,0:T(8,128)S(1)}, u32[]{:S(2)}, u32[]{:S(2)}) collective-permute-start(f32[2,384,256]{2,1,0:T(8,128)S(1)} %select_bitcast_fusion), channel_id=1, source_target_pairs={{0,64},{64,0},{128,192},{192,128},{1,65},{65,1},{129,193},{193,129... | collective-permute-start | bytes 2359304 | tf_op jit(solution)/shard_map/ppermute | solution.py:89
  19.6 3.1 %copy-start.1 = (s32[64]{0:T(128)S(1)}, s32[64]{0:T(128)}, u32[]{:S(2)}) copy-start(s32[64]{0:T(128)} %param.11) | copy-start | bytes 772
  22.0 11.2 %collective-permute-start.4 = (f32[384,256]{1,0:T(8,128)S(1)}, f32[384,256]{1,0:T(8,128)S(1)}, u32[]{:S(2)}, u32[]{:S(2)}) collective-permute-start(f32[384,256]{1,0:T(8,128)S(1)} %select_bitcast_fusion.1), channel_id=1, source_target_pairs={{0,128},{64,192},{128,0},{192,64},{1,129},{65,193},{129,1},{193,65... | collective-permute-start | bytes 1179656 | tf_op jit(solution)/shard_map/ppermute | solution.py:89

commit v17 on v15

--- a/solution.py
+++ b/solution.py
@@ -22,18 +22,15 @@
         cols = slice(pb * PBLK, (pb + 1) * PBLK)
         seps = [here[:, c : c + 1] - place_ref[c : c + 1, cols] for c in range(3)]
         dist_sq = seps[0] * seps[0] + seps[1] * seps[1] + seps[2] * seps[2]
-        parts = [amplitude / jnp.sqrt(dist_sq)] + [amplitude * sep / dist_sq for sep in seps]
+        inverse = 1.0 / dist_sq
+        parts = [amplitude / jnp.sqrt(dist_sq)] + [(amplitude * sep) * inverse for sep in seps]
         weight = frac_ref[:, cols].astype(jnp.float32)
-        low = None
-        high = None
-        for c in range(4):
-            src = src_ref[c, cols, :]
-            lo_w = (parts[c] * (1.0 - weight)).astype(jnp.bfloat16)
-            hi_w = (parts[c] * weight).astype(jnp.bfloat16)
-            lo_p = jnp.dot(lo_w, src, preferred_element_type=jnp.float32)
-            hi_p = jnp.dot(hi_w, src, preferred_element_type=jnp.float32)
-            low = lo_p if low is None else low + lo_p
-            high = hi_p if high is None else high + hi_p
+        rest = 1.0 - weight
+        lo_w = jnp.concatenate([(part * rest).astype(jnp.bfloat16) for part in parts], axis=1)
+        hi_w = jnp.concatenate([(part * weight).astype(jnp.bfloat16) for part in parts], axis=1)
+        src = src_ref[:, cols, :].reshape(4 * PBLK, src_ref.shape[2])
+        low = jnp.dot(lo_w, src, preferred_element_type=jnp.float32)
+        high = jnp.dot(hi_w, src, preferred_element_type=jnp.float32)
         shift = bins_ref[0, pb, ob]
         acc = acc + pltpu.roll(jnp.concatenate([low, pad], axis=1), shift, 1)
         acc = acc + pltpu.roll(jnp.concatenate([high, pad], axis=1), shift + 1, 1)

time: 63.9 us -> 62.4 us (0.977)
  Pallas kernels: 39.3 us -> 37.6 us
    pallas_call x1, Pallas kernels: 11.8 us -> 10.1 us  [per_device(): pl.pallas_call(kernel, grid_spec=grid_spec, out_shape=jax.ShapeDtypeStruc...]
where the time goes in v17:
time: 62.4 us; the launch traced here: 62 us
  Pallas kernels  37.6 us (60%)
  waiting for transfers between devices  12.4 us (20%)
  other arithmetic  5.21 us (8%)
  local copies, waits for them, and re-layouts  4.07 us (7%)
  starting transfers between devices  2.6 us (4%)
    pallas_call x1, Pallas kernels, exchange_sum(): pl.pallas_call(exchange_kernel, out_shape=jax.ShapeDtypeStruct(data.shape...  27.5 us
    ppermute x2, waiting for transfers between devices, per_device(): halves = keep + lax.ppermute(send, 'obs', pairs)  10.8 us
    pallas_call x1, Pallas kernels, per_device(): pl.pallas_call(kernel, grid_spec=grid_spec, out_shape=jax.ShapeDtypeStruc...  10.1 us
    unnamed x6, local copies, waits for them, and re-layouts  2.6 us
    sort x1, other arithmetic, per_device(): inverse = jnp.argsort(segment_owner)  2.03 us
    ppermute x3, starting transfers between devices, per_device(): lax.ppermute(observer_places, 'obs', [(p, p ^ k) for p in range(obs_count)])  1.86 us
    select_n x2, other arithmetic, per_device(): send = jnp.where(mine == 1, low, high)  1.64 us
    ppermute x3, waiting for transfers between devices, per_device(): lax.ppermute(observer_places, 'obs', [(p, p ^ k) for p in range(obs_count)])  1.6 us
  transfers between devices with their start and end apart: 5, of which 4 were waited for; matrix products, arithmetic and copies ran while one was open for 5% of the time, Pallas kernels for 0%

profile of v17, /device:TPU:24, one launch (start us, length us, event | category | flops | bytes accessed | tf_op | source)
XLA Modules:
  0.0 62.0 jit_solution(5177127378252849105)
XLA Ops:
  0.0 0.9 %collective-permute-start = (f32[3,256]{1,0:T(4,128)}, f32[3,256]{1,0:T(4,128)S(1)}, u32[]{:S(2)}, u32[]{:S(2)}) collective-permute-start(f32[3,256]{1,0:T(4,128)} %param.8), channel_id=1, source_target_pairs={{0,192},{64,128},{128,64},{192,0},{1,193},{65,129},{129,65},{193,1... | collective-permute-start | bytes 9224 | tf_op jit(solution)/shard_map/ppermute | solution.py:49
  0.9 0.6 collective-permute-start.1
  1.5 0.4 collective-permute-start.2
  1.9 1.3 %copy.17 = f32[1,3,512]{2,1,0:T(4,128)} copy(f32[1,3,512]{2,0,1:T(1,128)} %param.7) | data formatting | bytes 12288
  3.2 0.1 collective-permute-done
  3.2 1.5 %collective-permute-done.1 = f32[3,256]{1,0:T(4,128)S(1)} collective-permute-done((f32[3,256]{1,0:T(4,128)}, f32[3,256]{1,0:T(4,128)S(1)}, u32[]{:S(2)}, u32[]{:S(2)}) %collective-permute-start.1) | collective-permute-done | bytes 3104 | tf_op jit(solution)/shard_map/ppermute | solution.py:49
  4.8 0.0 collective-permute-done.2
  4.8 0.7 %select_select_fusion.3 = (f32[3,256]{1,0:T(4,128)S(1)}, f32[3,256]{1,0:T(4,128)S(1)}, f32[3,256]{1,0:T(4,128)S(1)}, f32[3,256]{1,0:T(4,128)S(1)}) fusion(f32[3,256]{1,0:T(4,128)S(1)} %collective-permute-done, f32[3,256]{1,0:T(4,128)S(1)} %collective-permute-done.1, f32[3,256]{1,0:T(4,128)S(1)} %collective-permute-done.2, f32[3,256]{1,0:T(4,128)} %param.8, ...), kind=kLoop, calls=%fused_computation.13 | loop fusion | flops 9216 | bytes 24588 | tf_op jit(solution)/shard_map/jit(_where)/select_n | solution.py:55
  5.5 0.6 pad_maximum_fusion.obs_ref
  6.1 10.1 %shard_map.64 = f32[4,384,256]{2,1,0:T(8,128)} custom-call(s32[1,4,8]{2,1,0:T(4,128)} %bitcast.32, f32[3,1024]{1,0:T(4,128)} %pad_maximum_fusion.obs_ref, f32[3,512]{1,0:T(4,128)} %bitcast.31, bf16[1024,512]{1,0:T(8,128)(2,1)} %bitcast.29, bf16[4,512,256]{2,1,0:T(8,128)(2,1)} %bitcast.30), custom_call_target="tpu_custom_call" | custom-call | tf_op jit(solution)/shard_map/pallas_call | solution.py:72
  16.2 0.0 copy-start
  16.2 1.6 %select_bitcast_fusion = f32[2,384,256]{2,1,0:T(8,128)S(1)} fusion(f32[2,2,384,256]{3,2,1,0:T(8,128)} %bitcast.27, pred[]{:T(512)S(6)} %eq.45), kind=kLoop, calls=%fused_computation.4 | loop fusion | flops 196608 | bytes 2359297 | tf_op jit(solution)/shard_map/jit(_where)/select_n | solution.py:84
  17.8 0.1 collective-permute-start.3
  17.9 0.0 copy-start.1
  17.9 2.3 %collective-permute-done.3 = f32[2,384,256]{2,1,0:T(8,128)S(1)} collective-permute-done((f32[2,384,256]{2,1,0:T(8,128)S(1)}, f32[2,384,256]{2,1,0:T(8,128)S(1)}, u32[]{:S(2)}, u32[]{:S(2)}) %collective-permute-start.3) | collective-permute-done | bytes 786464 | tf_op jit(solution)/shard_map/ppermute | solution.py:86
  20.2 0.0 copy-done
  20.2 0.2 bitcast_add_fusion
  20.3 0.1 select_bitcast_fusion.1
  20.4 0.6 %collective-permute-start.4 = (f32[384,256]{1,0:T(8,128)S(1)}, f32[384,256]{1,0:T(8,128)S(1)}, u32[]{:S(2)}, u32[]{:S(2)}) collective-permute-start(f32[384,256]{1,0:T(8,128)S(1)} %select_bitcast_fusion.1), channel_id=1, source_target_pairs={{0,128},{64,192},{128,0},{192,64},{1,129},{65,193},{129,1},{193,65... | collective-permute-start | bytes 1179656 | tf_op jit(solution)/shard_map/ppermute | solution.py:86
  21.0 0.0 copy-done.1
  21.0 2.0 %sort.17 = (s32[64]{0:T(128)}, s32[64]{0:T(128)S(1)}) sort(s32[64]{0:T(128)S(1)} %copy-done.1, s32[64]{0:T(128)S(1)} %iota.4), dimensions={0}, to_apply=%region_0.1 | sort | flops 384 | bytes 1024 | tf_op jit(solution)/shard_map/jit(argsort)/sort | solution.py:91
  23.1 8.5 %collective-permute-done.4 = f32[384,256]{1,0:T(8,128)S(1)} collective-permute-done((f32[384,256]{1,0:T(8,128)S(1)}, f32[384,256]{1,0:T(8,128)S(1)}, u32[]{:S(2)}, u32[]{:S(2)}) %collective-permute-start.4) | collective-permute-done | bytes 393248 | tf_op jit(solution)/shard_map/ppermute | solution.py:86
  31.6 0.1 bitcast_add_fusion.1
  31.7 0.1 reshape.15
  31.8 1.4 %gather_fusion = f32[64,6,256]{2,1,0:T(8,128)} fusion(f32[64,6,256]{2,1,0:T(8,128)S(1)} %reshape.15, s32[1024]{0:T(1024)S(1)} %pad_clamp_fusion), kind=kCustom, calls=%fused_computation | custom fusion | bytes 786688 | tf_op jit(solution)/shard_map/gather | solution.py:92
  33.2 27.5 %shard_map.65 = f32[6,256]{1,0:T(8,128)} custom-call(f32[64,6,256]{2,1,0:T(8,128)} %gather_fusion), custom_call_target="tpu_custom_call" | custom-call | tf_op jit(solution)/shard_map/pallas_call | solution.py:155
  60.7 1.3 %copy.19 = f32[6,256]{1,0:T(8,128)} copy(f32[6,256]{1,0:T(8,128)} %shard_map.65) | data formatting | bytes 12288
  (3 shorter events, 0.0 us)
Async XLA Ops:
  0.0 3.2 %collective-permute-start = (f32[3,256]{1,0:T(4,128)}, f32[3,256]{1,0:T(4,128)S(1)}, u32[]{:S(2)}, u32[]{:S(2)}) collective-permute-start(f32[3,256]{1,0:T(4,128)} %param.8), channel_id=1, source_target_pairs={{0,192},{64,128},{128,64},{192,0},{1,193},{65,129},{129,65},{193,1... | collective-permute-start | bytes 9224 | tf_op jit(solution)/shard_map/ppermute | solution.py:49
  0.9 3.8 %collective-permute-start.1 = (f32[3,256]{1,0:T(4,128)}, f32[3,256]{1,0:T(4,128)S(1)}, u32[]{:S(2)}, u32[]{:S(2)}) collective-permute-start(f32[3,256]{1,0:T(4,128)} %param.8), channel_id=1, source_target_pairs={{0,128},{64,192},{128,0},{192,64},{1,129},{65,193},{129,1},{193,65... | collective-permute-start | bytes 9224 | tf_op jit(solution)/shard_map/ppermute | solution.py:49
  1.5 3.3 %collective-permute-start.2 = (f32[3,256]{1,0:T(4,128)}, f32[3,256]{1,0:T(4,128)S(1)}, u32[]{:S(2)}, u32[]{:S(2)}) collective-permute-start(f32[3,256]{1,0:T(4,128)} %param.8), channel_id=1, source_target_pairs={{0,64},{64,0},{128,192},{192,128},{1,65},{65,1},{129,193},{193,129... | collective-permute-start | bytes 9224 | tf_op jit(solution)/shard_map/ppermute | solution.py:49
  16.2 4.0 %copy-start = (f32[4,384,256]{2,1,0:T(8,128)S(1)}, f32[4,384,256]{2,1,0:T(8,128)}, u32[]{:S(2)}) copy-start(f32[4,384,256]{2,1,0:T(8,128)} %shard_map.64) | copy-start | bytes 4718596
  17.8 2.4 %collective-permute-start.3 = (f32[2,384,256]{2,1,0:T(8,128)S(1)}, f32[2,384,256]{2,1,0:T(8,128)S(1)}, u32[]{:S(2)}, u32[]{:S(2)}) collective-permute-start(f32[2,384,256]{2,1,0:T(8,128)S(1)} %select_bitcast_fusion), channel_id=1, source_target_pairs={{0,64},{64,0},{128,192},{192,128},{1,65},{65,1},{129,193},{193,129... | collective-permute-start | bytes 2359304 | tf_op jit(solution)/shard_map/ppermute | solution.py:86
  17.9 3.1 %copy-start.1 = (s32[64]{0:T(128)S(1)}, s32[64]{0:T(128)}, u32[]{:S(2)}) copy-start(s32[64]{0:T(128)} %param.11) | copy-start | bytes 772
  20.4 11.2 %collective-permute-start.4 = (f32[384,256]{1,0:T(8,128)S(1)}, f32[384,256]{1,0:T(8,128)S(1)}, u32[]{:S(2)}, u32[]{:S(2)}) collective-permute-start(f32[384,256]{1,0:T(8,128)S(1)} %select_bitcast_fusion.1), channel_id=1, source_target_pairs={{0,128},{64,192},{128,0},{192,64},{1,129},{65,193},{129,1},{193,65... | collective-permute-start | bytes 1179656 | tf_op jit(solution)/shard_map/ppermute | solution.py:86

commit v18 on v17

--- a/solution.py
+++ b/solution.py
@@ -76,21 +76,22 @@
     )(jnp.transpose(delay_bins, (1, 2, 0)), every_obs, panel_places[0], fraction[:, 0, :], sources[0])
     halves = totals.reshape((2, 2) + totals.shape[1:])
     me = lax.axis_index("obs")
-    for bit, dim in ((0, 1), (1, 0)):
-        mine = (me >> bit) & 1
-        low = lax.index_in_dim(halves, 0, dim, keepdims=False)
-        high = lax.index_in_dim(halves, 1, dim, keepdims=False)
-        keep = jnp.where(mine == 1, high, low)
-        send = jnp.where(mine == 1, low, high)
-        pairs = [(p, p ^ (1 << bit)) for p in range(4)]
-        halves = keep + lax.ppermute(send, "obs", pairs)
-    reduced = halves
+    mine = me & 1
+    low = halves[:, 0]
+    high = halves[:, 1]
+    keep = jnp.where(mine == 1, high, low)
+    send = jnp.where(mine == 1, low, high)
+    halves = keep + lax.ppermute(send, "obs", [(p, p ^ 1) for p in range(4)])
     segment_count = segment_owner.shape[0]
     seg_len = bins_total // segment_count
-    arranged = reduced.reshape(segment_count, seg_len, reduced.shape[1])
+    arranged = halves.reshape(2, segment_count, seg_len, halves.shape[2])
     inverse = jnp.argsort(segment_owner)
-    arranged = arranged[inverse]
-    return exchange_sum(arranged)
+    arranged = jnp.swapaxes(arranged[:, inverse], 0, 1)
+    summed = exchange_sum(arranged)
+    upper = (me >> 1) & 1
+    keep = jnp.where(upper == 1, summed[1], summed[0])
+    send = jnp.where(upper == 1, summed[0], summed[1])
+    return keep + lax.ppermute(send, "obs", [(p, p ^ 2) for p in range(4)])
 
 
 def exchange_kernel(x_ref, out_ref, slots, send_sem, recv_sem):

time: 62.4 us -> 70.3 us (1.13); the launches traced: 62 us -> 68.9 us
  Pallas kernels: 37.6 us -> 48.5 us
  waiting for transfers between devices: 12.4 us -> 5.15 us
  other arithmetic: 5.21 us -> 7.6 us
  local copies, waits for them, and re-layouts: 4.07 us -> 5.31 us
    pallas_call x1, Pallas kernels: 27.5 us -> 38.4 us  [exchange_sum(): pl.pallas_call(exchange_kernel, out_shape=jax.ShapeDtypeStruct(data.shape...]
    ppermute x2, waiting for transfers between devices: 10.8 us -> 3.56 us  [the longest x1 3.36 us: per_device(): return keep + lax.ppermute(send, 'obs', [(p, p ^ 2) for p in range(4)])]
    add x2, other arithmetic: 0.23 us -> 2.52 us  [the longest x1 1.32 us: per_device(): return keep + lax.ppermute(send, 'obs', [(p, p ^ 2) for p in range(4)])]
    slice x0 -> x1, local copies, waits for them, and re-layouts: none -> 1.47 us  [per_device(): high = halves[:, 1]]
    unnamed x6 -> x3, local copies, waits for them, and re-layouts: 2.6 us -> 1.3 us
    gather x1 -> x2, local copies, waits for them, and re-layouts: 1.42 us -> 2.54 us  [per_device(): arranged = jnp.swapaxes(arranged[:, inverse], 0, 1)]
    select_n x1 -> x2, other arithmetic: 0.01 us -> 0.72 us  [the longest x1 0.72 us: per_device(): send = jnp.where(upper == 1, summed[0], summed[1])]
    select_n x2 -> x1, other arithmetic: 1.64 us -> 1.02 us  [per_device(): send = jnp.where(mine == 1, low, high)]
where the time goes in v18:
time: 70.3 us; the launch traced here: 68.9 us
  Pallas kernels  48.5 us (69%)
  other arithmetic  7.6 us (11%)
  local copies, waits for them, and re-layouts  5.31 us (8%)
  waiting for transfers between devices  5.15 us (7%)
  starting transfers between devices  2.25 us (3%)
    pallas_call x1, Pallas kernels, exchange_sum(): pl.pallas_call(exchange_kernel, out_shape=jax.ShapeDtypeStruct(data.shape...  38.4 us
    pallas_call x1, Pallas kernels, per_device(): pl.pallas_call(kernel, grid_spec=grid_spec, out_shape=jax.ShapeDtypeStruc...  10.1 us
    ppermute x1, waiting for transfers between devices, per_device(): return keep + lax.ppermute(send, 'obs', [(p, p ^ 2) for p in range(4)])  3.36 us
    gather x2, local copies, waits for them, and re-layouts, per_device(): arranged = jnp.swapaxes(arranged[:, inverse], 0, 1)  2.54 us
    sort x1, other arithmetic, per_device(): inverse = jnp.argsort(segment_owner)  2.03 us
    ppermute x3, starting transfers between devices, per_device(): lax.ppermute(observer_places, 'obs', [(p, p ^ k) for p in range(obs_count)])  1.86 us
    ppermute x3, waiting for transfers between devices, per_device(): lax.ppermute(observer_places, 'obs', [(p, p ^ k) for p in range(obs_count)])  1.6 us
    slice x1, local copies, waits for them, and re-layouts, per_device(): high = halves[:, 1]  1.47 us
  transfers between devices with their start and end apart: 5, of which 4 were waited for; matrix products, arithmetic and copies ran while one was open for 5% of the time, Pallas kernels for 0%

profile of v18, /device:TPU:24, one launch (start us, length us, event | category | flops | bytes accessed | tf_op | source)
XLA Modules:
  0.0 68.9 jit_solution(8308746229699954788)
XLA Ops:
  0.0 0.9 %collective-permute-start = (f32[3,256]{1,0:T(4,128)}, f32[3,256]{1,0:T(4,128)S(1)}, u32[]{:S(2)}, u32[]{:S(2)}) collective-permute-start(f32[3,256]{1,0:T(4,128)} %param.8), channel_id=1, source_target_pairs={{0,192},{64,128},{128,64},{192,0},{1,193},{65,129},{129,65},{193,1... | collective-permute-start | bytes 9224 | tf_op jit(solution)/shard_map/ppermute | solution.py:49
  0.9 0.6 collective-permute-start.1
  1.5 0.4 collective-permute-start.2
  1.9 1.3 %copy.24 = f32[1,3,512]{2,1,0:T(4,128)} copy(f32[1,3,512]{2,0,1:T(1,128)} %param.7) | data formatting | bytes 12288
  3.2 0.1 collective-permute-done
  3.2 1.5 %collective-permute-done.1 = f32[3,256]{1,0:T(4,128)S(1)} collective-permute-done((f32[3,256]{1,0:T(4,128)}, f32[3,256]{1,0:T(4,128)S(1)}, u32[]{:S(2)}, u32[]{:S(2)}) %collective-permute-start.1) | collective-permute-done | bytes 3104 | tf_op jit(solution)/shard_map/ppermute | solution.py:49
  4.8 0.0 collective-permute-done.2
  4.8 0.7 %select_select_fusion.3 = (f32[3,256]{1,0:T(4,128)S(1)}, f32[3,256]{1,0:T(4,128)S(1)}, f32[3,256]{1,0:T(4,128)S(1)}, f32[3,256]{1,0:T(4,128)S(1)}) fusion(f32[3,256]{1,0:T(4,128)S(1)} %collective-permute-done, f32[3,256]{1,0:T(4,128)S(1)} %collective-permute-done.1, f32[3,256]{1,0:T(4,128)S(1)} %collective-permute-done.2, f32[3,256]{1,0:T(4,128)} %param.8, ...), kind=kLoop, calls=%fused_computation.11 | loop fusion | flops 9216 | bytes 24588 | tf_op jit(solution)/shard_map/jit(_where)/select_n | solution.py:55
  5.5 0.6 pad_maximum_fusion.obs_ref
  6.1 10.1 %shard_map.64 = f32[4,384,256]{2,1,0:T(8,128)} custom-call(s32[1,4,8]{2,1,0:T(4,128)} %bitcast.21, f32[3,1024]{1,0:T(4,128)} %pad_maximum_fusion.obs_ref, f32[3,512]{1,0:T(4,128)} %bitcast.20, bf16[1024,512]{1,0:T(8,128)(2,1)} %bitcast.18, bf16[4,512,256]{2,1,0:T(8,128)(2,1)} %bitcast.19), custom_call_target="tpu_custom_call" | custom-call | tf_op jit(solution)/shard_map/pallas_call | solution.py:72
  16.2 1.5 %fusion = (f32[2,1,384,256]{3,2,1,0:T(8,128)S(1)}, f32[2,1,384,256]{3,2,1,0:T(8,128)S(1)}) fusion(f32[2,2,384,256]{3,2,1,0:T(8,128)} %bitcast.16), kind=kLoop, calls=%fused_computation.13 | loop fusion | bytes 3145728 | tf_op jit(solution)/shard_map/slice | solution.py:81
  17.7 0.0 copy-start
  17.7 1.0 %select_bitcast_fusion = f32[2,384,256]{2,0,1:T(2,128)S(1)} fusion(pred[]{:T(512)S(6)} %eq.45, f32[2,1,384,256]{3,2,1,0:T(8,128)S(1)} %get-tuple-element.8, f32[2,1,384,256]{3,2,1,0:T(8,128)S(1)} %get-tuple-element.7), kind=kLoop, calls=%fused_computation.2 | loop fusion | flops 196608 | bytes 2359297 | tf_op jit(solution)/shard_map/jit(_where)/select_n | solution.py:83
  18.7 0.1 collective-permute-start.3
  18.8 0.0 copy-done
  18.8 2.0 %sort.17 = (s32[64]{0:T(128)}, s32[64]{0:T(128)S(1)}) sort(s32[64]{0:T(128)S(1)} %copy-done, s32[64]{0:T(128)S(1)} %iota.4), dimensions={0}, to_apply=%region_0.1 | sort | flops 384 | bytes 1024 | tf_op jit(solution)/shard_map/jit(argsort)/sort | solution.py:88
  20.9 0.2 collective-permute-done.3
  21.1 1.2 %bitcast_add_fusion = f32[2,384,256]{2,0,1:T(2,128)S(1)} fusion(f32[2,384,256]{2,0,1:T(2,128)S(1)} %collective-permute-done.3, pred[]{:T(512)S(6)} %eq.45, f32[2,1,384,256]{3,2,1,0:T(8,128)S(1)} %get-tuple-element.8, f32[2,1,384,256]{3,2,1,0:T(8,128)S(1)} %get-tuple-element.7), kind=kLoop, calls=%fused_computation.1 | loop fusion | flops 393216 | bytes 3145729 | tf_op jit(solution)/shard_map/add | solution.py:84
  22.3 1.4 %gather_fusion = f32[64,2,6,256]{3,1,2,0:T(2,128)S(1)} fusion(f32[2,64,6,256]{3,0,2,1:T(2,128)S(1)} %bitcast.17, s32[1024]{0:T(1024)S(1)} %pad_clamp_fusion), kind=kCustom, calls=%fused_computation | custom fusion | bytes 1573120 | tf_op jit(solution)/shard_map/gather | solution.py:89
  23.7 1.1 %copy.15.x_ref = f32[64,2,6,256]{3,2,1,0:T(8,128)} copy(f32[64,2,6,256]{3,1,2,0:T(2,128)S(1)} %gather_fusion) | data formatting | bytes 1572864 | tf_op jit(solution)/shard_map/gather | solution.py:89
  24.8 38.4 %shard_map.65 = f32[2,6,256]{2,1,0:T(8,128)} custom-call(f32[64,2,6,256]{3,2,1,0:T(8,128)} %copy.15.x_ref), custom_call_target="tpu_custom_call" | custom-call | tf_op jit(solution)/shard_map/pallas_call | solution.py:156
  63.2 0.7 %select_bitcast_fusion.1 = f32[6,256]{1,0:T(8,128)S(1)} fusion(f32[2,6,256]{2,1,0:T(8,128)} %shard_map.65, pred[]{:T(512)S(6)} %eq.44), kind=kLoop, calls=%fused_computation.6 | loop fusion | flops 1536 | bytes 18433 | tf_op jit(solution)/shard_map/jit(_where)/select_n | solution.py:93
  63.9 0.3 collective-permute-start.4
  64.2 3.4 %collective-permute-done.4 = f32[6,256]{1,0:T(8,128)S(1)} collective-permute-done((f32[6,256]{1,0:T(8,128)S(1)}, f32[6,256]{1,0:T(8,128)S(1)}, u32[]{:S(2)}, u32[]{:S(2)}) %collective-permute-start.4) | collective-permute-done | bytes 6176 | tf_op jit(solution)/shard_map/ppermute | solution.py:94
  67.6 1.3 %bitcast_add_fusion.1 = f32[6,256]{1,0:T(8,128)} fusion(f32[6,256]{1,0:T(8,128)S(1)} %collective-permute-done.4, f32[2,6,256]{2,1,0:T(8,128)} %shard_map.65, pred[]{:T(512)S(6)} %eq.44), kind=kLoop, calls=%fused_computation.5 | loop fusion | flops 3072 | bytes 24577 | tf_op jit(solution)/shard_map/add | solution.py:94
  (3 shorter events, 0.0 us)
Async XLA Ops:
  0.0 3.2 %collective-permute-start = (f32[3,256]{1,0:T(4,128)}, f32[3,256]{1,0:T(4,128)S(1)}, u32[]{:S(2)}, u32[]{:S(2)}) collective-permute-start(f32[3,256]{1,0:T(4,128)} %param.8), channel_id=1, source_target_pairs={{0,192},{64,128},{128,64},{192,0},{1,193},{65,129},{129,65},{193,1... | collective-permute-start | bytes 9224 | tf_op jit(solution)/shard_map/ppermute | solution.py:49
  0.9 3.8 %collective-permute-start.1 = (f32[3,256]{1,0:T(4,128)}, f32[3,256]{1,0:T(4,128)S(1)}, u32[]{:S(2)}, u32[]{:S(2)}) collective-permute-start(f32[3,256]{1,0:T(4,128)} %param.8), channel_id=1, source_target_pairs={{0,128},{64,192},{128,0},{192,64},{1,129},{65,193},{129,1},{193,65... | collective-permute-start | bytes 9224 | tf_op jit(solution)/shard_map/ppermute | solution.py:49
  1.5 3.3 %collective-permute-start.2 = (f32[3,256]{1,0:T(4,128)}, f32[3,256]{1,0:T(4,128)S(1)}, u32[]{:S(2)}, u32[]{:S(2)}) collective-permute-start(f32[3,256]{1,0:T(4,128)} %param.8), channel_id=1, source_target_pairs={{0,64},{64,0},{128,192},{192,128},{1,65},{65,1},{129,193},{193,129... | collective-permute-start | bytes 9224 | tf_op jit(solution)/shard_map/ppermute | solution.py:49
  17.7 1.2 %copy-start = (s32[64]{0:T(128)S(1)}, s32[64]{0:T(128)}, u32[]{:S(2)}) copy-start(s32[64]{0:T(128)} %param.11) | copy-start | bytes 772
  18.7 2.4 %collective-permute-start.3 = (f32[2,384,256]{2,0,1:T(2,128)S(1)}, f32[2,384,256]{2,0,1:T(2,128)S(1)}, u32[]{:S(2)}, u32[]{:S(2)}) collective-permute-start(f32[2,384,256]{2,0,1:T(2,128)S(1)} %select_bitcast_fusion), channel_id=1, source_target_pairs={{0,64},{64,0},{128,192},{192,128},{1,65},{65,1},{129,193},{193,129... | collective-permute-start | bytes 2359304 | tf_op jit(solution)/shard_map/ppermute | solution.py:84
  63.9 3.7 %collective-permute-start.4 = (f32[6,256]{1,0:T(8,128)S(1)}, f32[6,256]{1,0:T(8,128)S(1)}, u32[]{:S(2)}, u32[]{:S(2)}) collective-permute-start(f32[6,256]{1,0:T(8,128)S(1)} %select_bitcast_fusion.1), channel_id=1, source_target_pairs={{0,128},{64,192},{128,0},{192,64},{1,129},{65,193},{129,1},{193,65... | collective-permute-start | bytes 18440 | tf_op jit(solution)/shard_map/ppermute | solution.py:94

commit v19 on v17

--- a/solution.py
+++ b/solution.py
@@ -90,7 +90,8 @@
     arranged = reduced.reshape(segment_count, seg_len, reduced.shape[1])
     inverse = jnp.argsort(segment_owner)
     arranged = arranged[inverse]
-    return exchange_sum(arranged)
+    flat = arranged.reshape(segment_count, 1, seg_len * arranged.shape[2])
+    return exchange_sum(flat).reshape(seg_len, arranged.shape[2])
 
 
 def exchange_kernel(x_ref, out_ref, slots, send_sem, recv_sem):

time: 62.4 us -> 60.2 us (0.965)
  Pallas kernels: 37.6 us -> 35.1 us
  other arithmetic: 5.21 us -> 5.93 us
    pallas_call x1, Pallas kernels: 27.5 us -> 24.9 us  [exchange_sum(): pl.pallas_call(exchange_kernel, out_shape=jax.ShapeDtypeStruct(data.shape...]
    reshape x0 -> x2, local copies, waits for them, and re-layouts: none -> 1.74 us  [the longest x1 1.14 us: per_device(): flat = arranged.reshape(segment_count, 1, seg_len * arranged.shape[2])]
    unnamed x6 -> x5, local copies, waits for them, and re-layouts: 2.6 us -> 1.3 us
    gather x1, local copies, waits for them, and re-layouts: 1.42 us -> 0.63 us  [per_device(): arranged = arranged[inverse]]
    pallas_call x0 -> x1, other arithmetic: none -> 0.71 us  [exchange_sum(): pl.pallas_call(exchange_kernel, out_shape=jax.ShapeDtypeStruct(data.shape...]
  transfers between devices with their start and end apart: 5 -> 5, of which waited for: 4 -> 4; matrix products, arithmetic and copies ran while one was open for 5% -> 6% of each run, Pallas kernels for 0% -> 0%
where the time goes in v19:
time: 60.2 us; the launch traced here: 59.8 us
  Pallas kernels  35.1 us (58%)
  waiting for transfers between devices  12.4 us (21%)
  other arithmetic  5.93 us (10%)
  local copies, waits for them, and re-layouts  3.73 us (6%)
  starting transfers between devices  2.6 us (4%)
    pallas_call x1, Pallas kernels, exchange_sum(): pl.pallas_call(exchange_kernel, out_shape=jax.ShapeDtypeStruct(data.shape...  24.9 us
    ppermute x2, waiting for transfers between devices, per_device(): halves = keep + lax.ppermute(send, 'obs', pairs)  10.8 us
    pallas_call x1, Pallas kernels, per_device(): pl.pallas_call(kernel, grid_spec=grid_spec, out_shape=jax.ShapeDtypeStruc...  10.2 us
    sort x1, other arithmetic, per_device(): inverse = jnp.argsort(segment_owner)  2.03 us
    ppermute x3, starting transfers between devices, per_device(): lax.ppermute(observer_places, 'obs', [(p, p ^ k) for p in range(obs_count)])  1.86 us
    select_n x2, other arithmetic, per_device(): send = jnp.where(mine == 1, low, high)  1.64 us
    ppermute x3, waiting for transfers between devices, per_device(): lax.ppermute(observer_places, 'obs', [(p, p ^ k) for p in range(obs_count)])  1.6 us
    unnamed x5, local copies, waits for them, and re-layouts  1.3 us
  transfers between devices with their start and end apart: 5, of which 4 were waited for; matrix products, arithmetic and copies ran while one was open for 6% of the time, Pallas kernels for 0%

profile of v19, /device:TPU:24, one launch (start us, length us, event | category | flops | bytes accessed | tf_op | source)
XLA Modules:
  0.0 59.8 jit_solution(8444130377220335177)
XLA Ops:
  0.0 0.9 %collective-permute-start = (f32[3,256]{1,0:T(4,128)}, f32[3,256]{1,0:T(4,128)S(1)}, u32[]{:S(2)}, u32[]{:S(2)}) collective-permute-start(f32[3,256]{1,0:T(4,128)} %param.8), channel_id=1, source_target_pairs={{0,192},{64,128},{128,64},{192,0},{1,193},{65,129},{129,65},{193,1... | collective-permute-start | bytes 9224 | tf_op jit(solution)/shard_map/ppermute | solution.py:49
  0.9 0.6 collective-permute-start.1
  1.5 0.4 collective-permute-start.2
  1.9 1.3 %copy.18 = f32[1,3,512]{2,1,0:T(4,128)} copy(f32[1,3,512]{2,0,1:T(1,128)} %param.7) | data formatting | bytes 12288
  3.2 0.1 collective-permute-done
  3.2 1.5 %collective-permute-done.1 = f32[3,256]{1,0:T(4,128)S(1)} collective-permute-done((f32[3,256]{1,0:T(4,128)}, f32[3,256]{1,0:T(4,128)S(1)}, u32[]{:S(2)}, u32[]{:S(2)}) %collective-permute-start.1) | collective-permute-done | bytes 3104 | tf_op jit(solution)/shard_map/ppermute | solution.py:49
  4.8 0.0 collective-permute-done.2
  4.8 0.7 %select_select_fusion.3 = (f32[3,256]{1,0:T(4,128)S(1)}, f32[3,256]{1,0:T(4,128)S(1)}, f32[3,256]{1,0:T(4,128)S(1)}, f32[3,256]{1,0:T(4,128)S(1)}) fusion(f32[3,256]{1,0:T(4,128)S(1)} %collective-permute-done, f32[3,256]{1,0:T(4,128)S(1)} %collective-permute-done.1, f32[3,256]{1,0:T(4,128)S(1)} %collective-permute-done.2, f32[3,256]{1,0:T(4,128)} %param.8, ...), kind=kLoop, calls=%fused_computation.13 | loop fusion | flops 9216 | bytes 24588 | tf_op jit(solution)/shard_map/jit(_where)/select_n | solution.py:55
  5.5 0.6 %pad_maximum_fusion.obs_ref = f32[3,1024]{1,0:T(4,128)} fusion(f32[3,256]{1,0:T(4,128)S(1)} %get-tuple-element.8, f32[3,256]{1,0:T(4,128)S(1)} %get-tuple-element.9, f32[3,256]{1,0:T(4,128)S(1)} %get-tuple-element.10, f32[3,256]{1,0:T(4,128)S(1)} %get-tuple-element.7), kind=kLoop, calls=%fused_computation.7 | loop fusion | flops 9216 | bytes 24576 | tf_op jit(solution)/shard_map/concatenate | solution.py:57
  6.1 10.2 %shard_map.64 = f32[4,384,256]{2,1,0:T(8,128)} custom-call(s32[1,4,8]{2,1,0:T(4,128)} %bitcast.32, f32[3,1024]{1,0:T(4,128)} %pad_maximum_fusion.obs_ref, f32[3,512]{1,0:T(4,128)} %bitcast.31, bf16[1024,512]{1,0:T(8,128)(2,1)} %bitcast.29, bf16[4,512,256]{2,1,0:T(8,128)(2,1)} %bitcast.30), custom_call_target="tpu_custom_call" | custom-call | tf_op jit(solution)/shard_map/pallas_call | solution.py:72
  16.2 0.0 copy-start
  16.2 1.6 %select_bitcast_fusion = f32[2,384,256]{2,1,0:T(8,128)S(1)} fusion(f32[2,2,384,256]{3,2,1,0:T(8,128)} %bitcast.27, pred[]{:T(512)S(6)} %eq.45), kind=kLoop, calls=%fused_computation.4 | loop fusion | flops 196608 | bytes 2359297 | tf_op jit(solution)/shard_map/jit(_where)/select_n | solution.py:84
  17.8 0.1 collective-permute-start.3
  17.9 0.0 copy-start.1
  17.9 2.3 %collective-permute-done.3 = f32[2,384,256]{2,1,0:T(8,128)S(1)} collective-permute-done((f32[2,384,256]{2,1,0:T(8,128)S(1)}, f32[2,384,256]{2,1,0:T(8,128)S(1)}, u32[]{:S(2)}, u32[]{:S(2)}) %collective-permute-start.3) | collective-permute-done | bytes 786464 | tf_op jit(solution)/shard_map/ppermute | solution.py:86
  20.2 0.0 copy-done
  20.2 0.2 bitcast_add_fusion
  20.3 0.1 select_bitcast_fusion.1
  20.4 0.6 %collective-permute-start.4 = (f32[384,256]{1,0:T(8,128)S(1)}, f32[384,256]{1,0:T(8,128)S(1)}, u32[]{:S(2)}, u32[]{:S(2)}) collective-permute-start(f32[384,256]{1,0:T(8,128)S(1)} %select_bitcast_fusion.1), channel_id=1, source_target_pairs={{0,128},{64,192},{128,0},{192,64},{1,129},{65,193},{129,1},{193,65... | collective-permute-start | bytes 1179656 | tf_op jit(solution)/shard_map/ppermute | solution.py:86
  21.0 0.0 copy-done.1
  21.0 2.0 %sort.17 = (s32[64]{0:T(128)}, s32[64]{0:T(128)S(1)}) sort(s32[64]{0:T(128)S(1)} %copy-done.1, s32[64]{0:T(128)S(1)} %iota.4), dimensions={0}, to_apply=%region_0.1 | sort | flops 384 | bytes 1024 | tf_op jit(solution)/shard_map/jit(argsort)/sort | solution.py:91
  23.1 8.5 %collective-permute-done.4 = f32[384,256]{1,0:T(8,128)S(1)} collective-permute-done((f32[384,256]{1,0:T(8,128)S(1)}, f32[384,256]{1,0:T(8,128)S(1)}, u32[]{:S(2)}, u32[]{:S(2)}) %collective-permute-start.4) | collective-permute-done | bytes 393248 | tf_op jit(solution)/shard_map/ppermute | solution.py:86
  31.6 0.1 bitcast_add_fusion.1
  31.7 0.1 reshape.21
  31.8 0.6 %gather_fusion = f32[64,6,256]{2,1,0:T(8,128)S(1)} fusion(f32[64,6,256]{2,1,0:T(8,128)S(1)} %reshape.21, s32[1024]{0:T(1024)S(1)} %pad_clamp_fusion), kind=kCustom, calls=%fused_computation | custom fusion | bytes 786688 | tf_op jit(solution)/shard_map/gather | solution.py:92
  32.4 1.1 %reshape.33.x_ref = f32[64,1,1536]{2,1,0:T(1,128)} reshape(f32[64,6,256]{2,1,0:T(8,128)S(1)} %gather_fusion) | data formatting | bytes 786432 | tf_op jit(solution)/shard_map/reshape | solution.py:93
  33.6 24.9 %shard_map.65 = f32[1,1536]{1,0:T(1,128)} custom-call(f32[64,1,1536]{2,1,0:T(1,128)} %reshape.33.x_ref), custom_call_target="tpu_custom_call" | custom-call | tf_op jit(solution)/shard_map/pallas_call | solution.py:156
  58.5 0.7 %reduce = f32[1536]{0:T(1024)S(1)} reduce(f32[1,1536]{1,0:T(1,128)} %shard_map.65, f32[]{:T(128)} %constant.21), dimensions={0}, to_apply=%pallas_call.7.reduce_sub_computation | reduce | bytes 12292 | tf_op jit(solution)/shard_map/pallas_call | solution.py:156
  59.2 0.6 %reshape.23 = f32[6,256]{1,0:T(8,128)} reshape(f32[1536]{0:T(1024)S(1)} %reduce) | data formatting | bytes 12288 | tf_op jit(solution)/shard_map/reshape | solution.py:94
  (3 shorter events, 0.0 us)
Async XLA Ops:
  0.0 3.2 %collective-permute-start = (f32[3,256]{1,0:T(4,128)}, f32[3,256]{1,0:T(4,128)S(1)}, u32[]{:S(2)}, u32[]{:S(2)}) collective-permute-start(f32[3,256]{1,0:T(4,128)} %param.8), channel_id=1, source_target_pairs={{0,192},{64,128},{128,64},{192,0},{1,193},{65,129},{129,65},{193,1... | collective-permute-start | bytes 9224 | tf_op jit(solution)/shard_map/ppermute | solution.py:49
  0.9 3.8 %collective-permute-start.1 = (f32[3,256]{1,0:T(4,128)}, f32[3,256]{1,0:T(4,128)S(1)}, u32[]{:S(2)}, u32[]{:S(2)}) collective-permute-start(f32[3,256]{1,0:T(4,128)} %param.8), channel_id=1, source_target_pairs={{0,128},{64,192},{128,0},{192,64},{1,129},{65,193},{129,1},{193,65... | collective-permute-start | bytes 9224 | tf_op jit(solution)/shard_map/ppermute | solution.py:49
  1.5 3.3 %collective-permute-start.2 = (f32[3,256]{1,0:T(4,128)}, f32[3,256]{1,0:T(4,128)S(1)}, u32[]{:S(2)}, u32[]{:S(2)}) collective-permute-start(f32[3,256]{1,0:T(4,128)} %param.8), channel_id=1, source_target_pairs={{0,64},{64,0},{128,192},{192,128},{1,65},{65,1},{129,193},{193,129... | collective-permute-start | bytes 9224 | tf_op jit(solution)/shard_map/ppermute | solution.py:49
  16.2 4.0 %copy-start = (f32[4,384,256]{2,1,0:T(8,128)S(1)}, f32[4,384,256]{2,1,0:T(8,128)}, u32[]{:S(2)}) copy-start(f32[4,384,256]{2,1,0:T(8,128)} %shard_map.64) | copy-start | bytes 4718596
  17.8 2.4 %collective-permute-start.3 = (f32[2,384,256]{2,1,0:T(8,128)S(1)}, f32[2,384,256]{2,1,0:T(8,128)S(1)}, u32[]{:S(2)}, u32[]{:S(2)}) collective-permute-start(f32[2,384,256]{2,1,0:T(8,128)S(1)} %select_bitcast_fusion), channel_id=1, source_target_pairs={{0,64},{64,0},{128,192},{192,128},{1,65},{65,1},{129,193},{193,129... | collective-permute-start | bytes 2359304 | tf_op jit(solution)/shard_map/ppermute | solution.py:86
  17.9 3.1 %copy-start.1 = (s32[64]{0:T(128)S(1)}, s32[64]{0:T(128)}, u32[]{:S(2)}) copy-start(s32[64]{0:T(128)} %param.11) | copy-start | bytes 772
  20.4 11.2 %collective-permute-start.4 = (f32[384,256]{1,0:T(8,128)S(1)}, f32[384,256]{1,0:T(8,128)S(1)}, u32[]{:S(2)}, u32[]{:S(2)}) collective-permute-start(f32[384,256]{1,0:T(8,128)S(1)} %select_bitcast_fusion.1), channel_id=1, source_target_pairs={{0,128},{64,192},{128,0},{192,64},{1,129},{65,193},{129,1},{193,65... | collective-permute-start | bytes 1179656 | tf_op jit(solution)/shard_map/ppermute | solution.py:86

commit v20 on v19

--- a/solution.py
+++ b/solution.py
@@ -13,7 +13,7 @@
 PBLK = 128
 
 
-def fwh_kernel(bins_ref, obs_ref, place_ref, frac_ref, src_ref, out_ref, *, amplitude, panel_blocks, window, bins_total):
+def fwh_kernel(bins_ref, me_ref, obs_ref, place_ref, frac_ref, src_ref, out_ref, *, amplitude, panel_blocks, window, bins_total):
     ob = pl.program_id(0)
     here = obs_ref[...].T
     acc = jnp.zeros((OBLK, bins_total), jnp.float32)
@@ -59,31 +59,25 @@
     obs_blocks = obs_total // OBLK
     kernel = functools.partial(fwh_kernel, amplitude=amplitude, panel_blocks=panel_blocks, window=window, bins_total=bins_total)
     grid_spec = pltpu.PrefetchScalarGridSpec(
-        num_scalar_prefetch=1,
+        num_scalar_prefetch=2,
         grid=(obs_blocks,),
         in_specs=[
-            pl.BlockSpec((3, OBLK), lambda i, b: (0, i)),
-            pl.BlockSpec((3, local_panels), lambda i, b: (0, 0)),
-            pl.BlockSpec((OBLK, local_panels), lambda i, b: (i, 0)),
-            pl.BlockSpec((4, local_panels, window), lambda i, b: (0, 0, 0)),
+            pl.BlockSpec((3, OBLK), lambda i, b, m: (0, i)),
+            pl.BlockSpec((3, local_panels), lambda i, b, m: (0, 0)),
+            pl.BlockSpec((OBLK, local_panels), lambda i, b, m: (i, 0)),
+            pl.BlockSpec((4, local_panels, window), lambda i, b, m: (0, 0, 0)),
         ],
-        out_specs=pl.BlockSpec((None, bins_total, OBLK), lambda i, b: (i // 2, 0, i % 2)),
+        out_specs=pl.BlockSpec((None, bins_total, OBLK), lambda i, b, m: (((i // 2) % 2 + m[0]) % 2 * 2 + ((i // 4) + m[0] // 2) % 2, 0, i % 2)),
     )
     totals = pl.pallas_call(
         kernel,
         grid_spec=grid_spec,
         out_shape=jax.ShapeDtypeStruct((obs_blocks // 2, bins_total, 2 * OBLK), jnp.float32),
-    )(jnp.transpose(delay_bins, (1, 2, 0)), every_obs, panel_places[0], fraction[:, 0, :], sources[0])
+    )(jnp.transpose(delay_bins, (1, 2, 0)), jnp.reshape(obs_me, (1,)).astype(jnp.int32), every_obs, panel_places[0], fraction[:, 0, :], sources[0])
     halves = totals.reshape((2, 2) + totals.shape[1:])
-    me = lax.axis_index("obs")
-    for bit, dim in ((0, 1), (1, 0)):
-        mine = (me >> bit) & 1
-        low = lax.index_in_dim(halves, 0, dim, keepdims=False)
-        high = lax.index_in_dim(halves, 1, dim, keepdims=False)
-        keep = jnp.where(mine == 1, high, low)
-        send = jnp.where(mine == 1, low, high)
+    for bit in (0, 1):
         pairs = [(p, p ^ (1 << bit)) for p in range(4)]
-        halves = keep + lax.ppermute(send, "obs", pairs)
+        halves = halves[0] + lax.ppermute(halves[1], "obs", pairs)
     reduced = halves
     segment_count = segment_owner.shape[0]
     seg_len = bins_total // segment_count

time: 60.2 us -> 59.9 us (level)
  other arithmetic: 5.93 us -> 4.21 us
  local copies, waits for them, and re-layouts: 3.73 us -> 5.06 us
    select_n x2 -> x0, other arithmetic: 1.64 us -> none  [per_device(): send = jnp.where(mine == 1, low, high)]
    slice x0 -> x1, local copies, waits for them, and re-layouts: none -> 1.3 us  [per_device(): halves = halves[0] + lax.ppermute(halves[1], 'obs', pairs)]
where the time goes in v20:
time: 59.9 us; the launch traced here: 59.4 us
  Pallas kernels  35.1 us (59%)
  waiting for transfers between devices  12.4 us (21%)
  local copies, waits for them, and re-layouts  5.06 us (8%)
  other arithmetic  4.21 us (7%)
  starting transfers between devices  2.64 us (4%)
    pallas_call x1, Pallas kernels, exchange_sum(): pl.pallas_call(exchange_kernel, out_shape=jax.ShapeDtypeStruct(data.shape...  24.9 us
    ppermute x2, waiting for transfers between devices, per_device(): halves = halves[0] + lax.ppermute(halves[1], 'obs', pairs)  10.8 us
    pallas_call x1, Pallas kernels, per_device(): pl.pallas_call(kernel, grid_spec=grid_spec, out_shape=jax.ShapeDtypeStruc...  10.1 us
    sort x1, other arithmetic, per_device(): inverse = jnp.argsort(segment_owner)  2.03 us
    ppermute x3, starting transfers between devices, per_device(): lax.ppermute(observer_places, 'obs', [(p, p ^ k) for p in range(obs_count)])  1.86 us
    ppermute x3, waiting for transfers between devices, per_device(): lax.ppermute(observer_places, 'obs', [(p, p ^ k) for p in range(obs_count)])  1.6 us
    slice x1, local copies, waits for them, and re-layouts, per_device(): halves = halves[0] + lax.ppermute(halves[1], 'obs', pairs)  1.3 us
    unnamed x5, local copies, waits for them, and re-layouts  1.3 us
  transfers between devices with their start and end apart: 5, of which 4 were waited for; matrix products, arithmetic and copies ran while one was open for 6% of the time, Pallas kernels for 0%

profile of v20, /device:TPU:24, one launch (start us, length us, event | category | flops | bytes accessed | tf_op | source)
XLA Modules:
  0.0 59.4 jit_solution(12744920258637332640)
XLA Ops:
  0.0 0.9 %collective-permute-start = (f32[3,256]{1,0:T(4,128)}, f32[3,256]{1,0:T(4,128)S(1)}, u32[]{:S(2)}, u32[]{:S(2)}) collective-permute-start(f32[3,256]{1,0:T(4,128)} %param.8), channel_id=1, source_target_pairs={{0,192},{64,128},{128,64},{192,0},{1,193},{65,129},{129,65},{193,1... | collective-permute-start | bytes 9224 | tf_op jit(solution)/shard_map/ppermute | solution.py:49
  0.9 0.6 collective-permute-start.1
  1.5 0.4 collective-permute-start.2
  1.9 1.3 %copy.10 = f32[1,3,512]{2,1,0:T(4,128)} copy(f32[1,3,512]{2,0,1:T(1,128)} %param.7) | data formatting | bytes 12288
  3.2 0.1 collective-permute-done
  3.2 1.5 %collective-permute-done.1 = f32[3,256]{1,0:T(4,128)S(1)} collective-permute-done((f32[3,256]{1,0:T(4,128)}, f32[3,256]{1,0:T(4,128)S(1)}, u32[]{:S(2)}, u32[]{:S(2)}) %collective-permute-start.1) | collective-permute-done | bytes 3104 | tf_op jit(solution)/shard_map/ppermute | solution.py:49
  4.8 0.0 collective-permute-done.2
  4.8 0.7 %select_select_fusion.3 = (f32[3,256]{1,0:T(4,128)S(1)}, f32[3,256]{1,0:T(4,128)S(1)}, f32[3,256]{1,0:T(4,128)S(1)}, f32[3,256]{1,0:T(4,128)S(1)}) fusion(f32[3,256]{1,0:T(4,128)S(1)} %collective-permute-done, f32[3,256]{1,0:T(4,128)S(1)} %collective-permute-done.1, f32[3,256]{1,0:T(4,128)S(1)} %collective-permute-done.2, f32[3,256]{1,0:T(4,128)} %param.8, ...), kind=kLoop, calls=%fused_computation.11 | loop fusion | flops 9216 | bytes 24588 | tf_op jit(solution)/shard_map/jit(_where)/select_n | solution.py:55
  5.5 0.6 %pad_maximum_fusion.obs_ref = f32[3,1024]{1,0:T(4,128)} fusion(f32[3,256]{1,0:T(4,128)S(1)} %get-tuple-element.8, f32[3,256]{1,0:T(4,128)S(1)} %get-tuple-element.9, f32[3,256]{1,0:T(4,128)S(1)} %get-tuple-element.10, f32[3,256]{1,0:T(4,128)S(1)} %get-tuple-element.7), kind=kLoop, calls=%fused_computation.5 | loop fusion | flops 9216 | bytes 24576 | tf_op jit(solution)/shard_map/concatenate | solution.py:57
  6.1 10.1 %shard_map.64 = f32[4,384,256]{2,1,0:T(8,128)} custom-call(s32[1,4,8]{2,1,0:T(4,128)} %bitcast.16, s32[1]{0:T(128)} %bitcast.1.me_ref, f32[3,1024]{1,0:T(4,128)} %pad_maximum_fusion.obs_ref, f32[3,512]{1,0:T(4,128)} %bitcast.15, bf16[1024,512]{1,0:T(8,128)(2,1)} %bitcast.13, bf16[4,512,256]{2,1,0:T(8,128)(2,1)} %bitcast.14), custom_call_target="tpu_custom_call" | custom-call | tf_op jit(solution)/shard_map/pallas_call | solution.py:72
  16.2 0.0 copy-start
  16.2 1.3 %slice.21 = f32[2,384,256]{2,1,0:T(8,128)S(1)} slice(f32[4,384,256]{2,1,0:T(8,128)} %shard_map.64), slice={[2:4], [0:384], [0:256]} | slice | bytes 1572864 | tf_op jit(solution)/shard_map/slice | solution.py:80
  17.5 0.0 copy-start.1
  17.5 0.1 collective-permute-start.3
  17.6 2.3 %collective-permute-done.3 = f32[2,384,256]{2,1,0:T(8,128)S(1)} collective-permute-done((f32[2,384,256]{2,1,0:T(8,128)S(1)}, f32[2,384,256]{2,1,0:T(8,128)S(1)}, u32[]{:S(2)}, u32[]{:S(2)}) %collective-permute-start.3) | collective-permute-done | bytes 786464 | tf_op jit(solution)/shard_map/ppermute | solution.py:80
  19.9 0.0 copy-done
  19.9 0.1 slice_add_fusion
  20.0 0.7 %collective-permute-start.4 = (f32[384,256]{1,0:T(8,128)S(1)}, f32[384,256]{1,0:T(8,128)S(1)}, u32[]{:S(2)}, u32[]{:S(2)}) collective-permute-start(f32[384,256]{1,0:T(8,128)S(1)} %slice_bitcast_fusion), channel_id=1, source_target_pairs={{0,128},{64,192},{128,0},{192,64},{1,129},{65,193},{129,1},{193,65... | collective-permute-start | bytes 1179656 | tf_op jit(solution)/shard_map/ppermute | solution.py:80
  20.7 0.0 copy-done.1
  20.7 2.0 %sort.17 = (s32[64]{0:T(128)}, s32[64]{0:T(128)S(1)}) sort(s32[64]{0:T(128)S(1)} %copy-done.1, s32[64]{0:T(128)S(1)} %iota.4), dimensions={0}, to_apply=%region_0.1 | sort | flops 384 | bytes 1024 | tf_op jit(solution)/shard_map/jit(argsort)/sort | solution.py:85
  22.8 8.5 %collective-permute-done.4 = f32[384,256]{1,0:T(8,128)S(1)} collective-permute-done((f32[384,256]{1,0:T(8,128)S(1)}, f32[384,256]{1,0:T(8,128)S(1)}, u32[]{:S(2)}, u32[]{:S(2)}) %collective-permute-start.4) | collective-permute-done | bytes 393248 | tf_op jit(solution)/shard_map/ppermute | solution.py:80
  31.3 0.1 fusion
  31.3 0.1 reshape.18
  31.4 0.6 %gather_fusion = f32[64,6,256]{2,1,0:T(8,128)S(1)} fusion(f32[64,6,256]{2,1,0:T(8,128)S(1)} %reshape.18, s32[1024]{0:T(1024)S(1)} %pad_clamp_fusion), kind=kCustom, calls=%fused_computation | custom fusion | bytes 786688 | tf_op jit(solution)/shard_map/gather | solution.py:86
  32.0 1.1 %reshape.30.x_ref = f32[64,1,1536]{2,1,0:T(1,128)} reshape(f32[64,6,256]{2,1,0:T(8,128)S(1)} %gather_fusion) | data formatting | bytes 786432 | tf_op jit(solution)/shard_map/reshape | solution.py:87
  33.2 24.9 %shard_map.65 = f32[1,1536]{1,0:T(1,128)} custom-call(f32[64,1,1536]{2,1,0:T(1,128)} %reshape.30.x_ref), custom_call_target="tpu_custom_call" | custom-call | tf_op jit(solution)/shard_map/pallas_call | solution.py:150
  58.1 0.7 %reduce = f32[1536]{0:T(1024)S(1)} reduce(f32[1,1536]{1,0:T(1,128)} %shard_map.65, f32[]{:T(128)} %constant.21), dimensions={0}, to_apply=%pallas_call.7.reduce_sub_computation | reduce | bytes 12292 | tf_op jit(solution)/shard_map/pallas_call | solution.py:150
  58.8 0.6 %reshape.20 = f32[6,256]{1,0:T(8,128)} reshape(f32[1536]{0:T(1024)S(1)} %reduce) | data formatting | bytes 12288 | tf_op jit(solution)/shard_map/reshape | solution.py:88
  (4 shorter events, 0.0 us)
Async XLA Ops:
  0.0 3.2 %collective-permute-start = (f32[3,256]{1,0:T(4,128)}, f32[3,256]{1,0:T(4,128)S(1)}, u32[]{:S(2)}, u32[]{:S(2)}) collective-permute-start(f32[3,256]{1,0:T(4,128)} %param.8), channel_id=1, source_target_pairs={{0,192},{64,128},{128,64},{192,0},{1,193},{65,129},{129,65},{193,1... | collective-permute-start | bytes 9224 | tf_op jit(solution)/shard_map/ppermute | solution.py:49
  0.9 3.8 %collective-permute-start.1 = (f32[3,256]{1,0:T(4,128)}, f32[3,256]{1,0:T(4,128)S(1)}, u32[]{:S(2)}, u32[]{:S(2)}) collective-permute-start(f32[3,256]{1,0:T(4,128)} %param.8), channel_id=1, source_target_pairs={{0,128},{64,192},{128,0},{192,64},{1,129},{65,193},{129,1},{193,65... | collective-permute-start | bytes 9224 | tf_op jit(solution)/shard_map/ppermute | solution.py:49
  1.5 3.3 %collective-permute-start.2 = (f32[3,256]{1,0:T(4,128)}, f32[3,256]{1,0:T(4,128)S(1)}, u32[]{:S(2)}, u32[]{:S(2)}) collective-permute-start(f32[3,256]{1,0:T(4,128)} %param.8), channel_id=1, source_target_pairs={{0,64},{64,0},{128,192},{192,128},{1,65},{65,1},{129,193},{193,129... | collective-permute-start | bytes 9224 | tf_op jit(solution)/shard_map/ppermute | solution.py:49
  16.2 3.7 %copy-start = (f32[4,384,256]{2,1,0:T(8,128)S(1)}, f32[4,384,256]{2,1,0:T(8,128)}, u32[]{:S(2)}) copy-start(f32[4,384,256]{2,1,0:T(8,128)} %shard_map.64) | copy-start | bytes 4718596
  17.5 3.2 %copy-start.1 = (s32[64]{0:T(128)S(1)}, s32[64]{0:T(128)}, u32[]{:S(2)}) copy-start(s32[64]{0:T(128)} %param.11) | copy-start | bytes 772
  17.5 2.4 %collective-permute-start.3 = (f32[2,384,256]{2,1,0:T(8,128)S(1)}, f32[2,384,256]{2,1,0:T(8,128)S(1)}, u32[]{:S(2)}, u32[]{:S(2)}) collective-permute-start(f32[2,384,256]{2,1,0:T(8,128)S(1)} %slice.21), channel_id=1, source_target_pairs={{0,64},{64,0},{128,192},{192,128},{1,65},{65,1},{129,193},{193,129... | collective-permute-start | bytes 2359304 | tf_op jit(solution)/shard_map/ppermute | solution.py:80
  20.0 11.2 %collective-permute-start.4 = (f32[384,256]{1,0:T(8,128)S(1)}, f32[384,256]{1,0:T(8,128)S(1)}, u32[]{:S(2)}, u32[]{:S(2)}) collective-permute-start(f32[384,256]{1,0:T(8,128)S(1)} %slice_bitcast_fusion), channel_id=1, source_target_pairs={{0,128},{64,192},{128,0},{192,64},{1,129},{65,193},{129,1},{193,65... | collective-permute-start | bytes 1179656 | tf_op jit(solution)/shard_map/ppermute | solution.py:80

commit v21 on v20

--- a/solution.py
+++ b/solution.py
@@ -85,7 +85,7 @@
     inverse = jnp.argsort(segment_owner)
     arranged = arranged[inverse]
     flat = arranged.reshape(segment_count, 1, seg_len * arranged.shape[2])
-    return exchange_sum(flat).reshape(seg_len, arranged.shape[2])
+    return exchange_sum(flat, seg_len)
 
 
 def exchange_kernel(x_ref, out_ref, slots, send_sem, recv_sem):
@@ -142,14 +142,16 @@
         return carry
 
     lax.fori_loop(1, count, drain, 0)
-    out_ref[...] = total
+    width = out_ref.shape[1]
+    for r in range(out_ref.shape[0]):
+        out_ref[r : r + 1, :] = total[:, r * width : (r + 1) * width]
 
 
-def exchange_sum(data):
+def exchange_sum(data, rows):
     count = data.shape[0]
     return pl.pallas_call(
         exchange_kernel,
-        out_shape=jax.ShapeDtypeStruct(data.shape[1:], data.dtype),
+        out_shape=jax.ShapeDtypeStruct((rows, data.shape[2] // rows), data.dtype),
         in_specs=[pl.BlockSpec(memory_space=pltpu.VMEM)],
         out_specs=pl.BlockSpec(memory_space=pltpu.VMEM),
         scratch_shapes=[

time: 59.9 us -> 59.8 us (level)
  other arithmetic: 4.21 us -> 3.5 us
  local copies, waits for them, and re-layouts: 5.06 us -> 5.75 us
    unnamed x5 -> x6, local copies, waits for them, and re-layouts: 1.3 us -> 2.6 us
    pallas_call x1 -> x0, other arithmetic: 0.71 us -> none  [exchange_sum(): pl.pallas_call(exchange_kernel, out_shape=jax.ShapeDtypeStruct(data.shape...]
    reshape x1 -> x0, local copies, waits for them, and re-layouts: 0.6 us -> none  [per_device(): return exchange_sum(flat).reshape(seg_len, arranged.shape[2])]
where the time goes in v21:
time: 59.8 us; the launch traced here: 59.4 us
  Pallas kernels  35.1 us (59%)
  waiting for transfers between devices  12.4 us (21%)
  local copies, waits for them, and re-layouts  5.75 us (10%)
  other arithmetic  3.5 us (6%)
  starting transfers between devices  2.64 us (4%)
    pallas_call x1, Pallas kernels, exchange_sum(): pl.pallas_call(exchange_kernel, out_shape=jax.ShapeDtypeStruct((rows, dat...  24.9 us
    ppermute x2, waiting for transfers between devices, per_device(): halves = halves[0] + lax.ppermute(halves[1], 'obs', pairs)  10.8 us
    pallas_call x1, Pallas kernels, per_device(): pl.pallas_call(kernel, grid_spec=grid_spec, out_shape=jax.ShapeDtypeStruc...  10.2 us
    unnamed x6, local copies, waits for them, and re-layouts  2.6 us
    sort x1, other arithmetic, per_device(): inverse = jnp.argsort(segment_owner)  2.03 us
    ppermute x3, starting transfers between devices, per_device(): lax.ppermute(observer_places, 'obs', [(p, p ^ k) for p in range(obs_count)])  1.86 us
    ppermute x3, waiting for transfers between devices, per_device(): lax.ppermute(observer_places, 'obs', [(p, p ^ k) for p in range(obs_count)])  1.6 us
    slice x1, local copies, waits for them, and re-layouts, per_device(): halves = halves[0] + lax.ppermute(halves[1], 'obs', pairs)  1.3 us
  transfers between devices with their start and end apart: 5, of which 4 were waited for; matrix products, arithmetic and copies ran while one was open for 6% of the time, Pallas kernels for 0%

profile of v21, /device:TPU:24, one launch (start us, length us, event | category | flops | bytes accessed | tf_op | source)
XLA Modules:
  0.0 59.4 jit_solution(14577714583145703450)
XLA Ops:
  0.0 0.9 %collective-permute-start = (f32[3,256]{1,0:T(4,128)}, f32[3,256]{1,0:T(4,128)S(1)}, u32[]{:S(2)}, u32[]{:S(2)}) collective-permute-start(f32[3,256]{1,0:T(4,128)} %param.8), channel_id=1, source_target_pairs={{0,192},{64,128},{128,64},{192,0},{1,193},{65,129},{129,65},{193,1... | collective-permute-start | bytes 9224 | tf_op jit(solution)/shard_map/ppermute | solution.py:49
  0.9 0.6 collective-permute-start.1
  1.5 0.4 collective-permute-start.2
  1.9 1.3 %copy.10 = f32[1,3,512]{2,1,0:T(4,128)} copy(f32[1,3,512]{2,0,1:T(1,128)} %param.7) | data formatting | bytes 12288
  3.2 0.1 collective-permute-done
  3.2 1.5 %collective-permute-done.1 = f32[3,256]{1,0:T(4,128)S(1)} collective-permute-done((f32[3,256]{1,0:T(4,128)}, f32[3,256]{1,0:T(4,128)S(1)}, u32[]{:S(2)}, u32[]{:S(2)}) %collective-permute-start.1) | collective-permute-done | bytes 3104 | tf_op jit(solution)/shard_map/ppermute | solution.py:49
  4.8 0.0 collective-permute-done.2
  4.8 0.7 %select_select_fusion.3 = (f32[3,256]{1,0:T(4,128)S(1)}, f32[3,256]{1,0:T(4,128)S(1)}, f32[3,256]{1,0:T(4,128)S(1)}, f32[3,256]{1,0:T(4,128)S(1)}) fusion(f32[3,256]{1,0:T(4,128)S(1)} %collective-permute-done, f32[3,256]{1,0:T(4,128)S(1)} %collective-permute-done.1, f32[3,256]{1,0:T(4,128)S(1)} %collective-permute-done.2, f32[3,256]{1,0:T(4,128)} %param.8, ...), kind=kLoop, calls=%fused_computation.11 | loop fusion | flops 9216 | bytes 24588 | tf_op jit(solution)/shard_map/jit(_where)/select_n | solution.py:55
  5.5 0.6 %pad_maximum_fusion.obs_ref = f32[3,1024]{1,0:T(4,128)} fusion(f32[3,256]{1,0:T(4,128)S(1)} %get-tuple-element.8, f32[3,256]{1,0:T(4,128)S(1)} %get-tuple-element.9, f32[3,256]{1,0:T(4,128)S(1)} %get-tuple-element.10, f32[3,256]{1,0:T(4,128)S(1)} %get-tuple-element.7), kind=kLoop, calls=%fused_computation.5 | loop fusion | flops 9216 | bytes 24576 | tf_op jit(solution)/shard_map/concatenate | solution.py:57
  6.1 10.2 %shard_map.64 = f32[4,384,256]{2,1,0:T(8,128)} custom-call(s32[1,4,8]{2,1,0:T(4,128)} %bitcast.16, s32[1]{0:T(128)} %bitcast.1.me_ref, f32[3,1024]{1,0:T(4,128)} %pad_maximum_fusion.obs_ref, f32[3,512]{1,0:T(4,128)} %bitcast.15, bf16[1024,512]{1,0:T(8,128)(2,1)} %bitcast.13, bf16[4,512,256]{2,1,0:T(8,128)(2,1)} %bitcast.14), custom_call_target="tpu_custom_call" | custom-call | tf_op jit(solution)/shard_map/pallas_call | solution.py:72
  16.2 0.0 copy-start
  16.2 1.3 %slice.21 = f32[2,384,256]{2,1,0:T(8,128)S(1)} slice(f32[4,384,256]{2,1,0:T(8,128)} %shard_map.64), slice={[2:4], [0:384], [0:256]} | slice | bytes 1572864 | tf_op jit(solution)/shard_map/slice | solution.py:80
  17.5 0.0 copy-start.1
  17.5 0.1 collective-permute-start.3
  17.6 2.3 %collective-permute-done.3 = f32[2,384,256]{2,1,0:T(8,128)S(1)} collective-permute-done((f32[2,384,256]{2,1,0:T(8,128)S(1)}, f32[2,384,256]{2,1,0:T(8,128)S(1)}, u32[]{:S(2)}, u32[]{:S(2)}) %collective-permute-start.3) | collective-permute-done | bytes 786464 | tf_op jit(solution)/shard_map/ppermute | solution.py:80
  19.9 0.0 copy-done
  19.9 0.1 slice_add_fusion
  20.0 0.7 %collective-permute-start.4 = (f32[384,256]{1,0:T(8,128)S(1)}, f32[384,256]{1,0:T(8,128)S(1)}, u32[]{:S(2)}, u32[]{:S(2)}) collective-permute-start(f32[384,256]{1,0:T(8,128)S(1)} %slice_bitcast_fusion), channel_id=1, source_target_pairs={{0,128},{64,192},{128,0},{192,64},{1,129},{65,193},{129,1},{193,65... | collective-permute-start | bytes 1179656 | tf_op jit(solution)/shard_map/ppermute | solution.py:80
  20.7 0.0 copy-done.1
  20.7 2.0 %sort.17 = (s32[64]{0:T(128)}, s32[64]{0:T(128)S(1)}) sort(s32[64]{0:T(128)S(1)} %copy-done.1, s32[64]{0:T(128)S(1)} %iota.4), dimensions={0}, to_apply=%region_0.1 | sort | flops 384 | bytes 1024 | tf_op jit(solution)/shard_map/jit(argsort)/sort | solution.py:85
  22.8 8.5 %collective-permute-done.4 = f32[384,256]{1,0:T(8,128)S(1)} collective-permute-done((f32[384,256]{1,0:T(8,128)S(1)}, f32[384,256]{1,0:T(8,128)S(1)}, u32[]{:S(2)}, u32[]{:S(2)}) %collective-permute-start.4) | collective-permute-done | bytes 393248 | tf_op jit(solution)/shard_map/ppermute | solution.py:80
  31.3 0.1 fusion
  31.3 0.1 reshape.15
  31.4 0.6 %gather_fusion = f32[64,6,256]{2,1,0:T(8,128)S(1)} fusion(f32[64,6,256]{2,1,0:T(8,128)S(1)} %reshape.15, s32[1024]{0:T(1024)S(1)} %pad_clamp_fusion), kind=kCustom, calls=%fused_computation | custom fusion | bytes 786688 | tf_op jit(solution)/shard_map/gather | solution.py:86
  32.0 1.1 %reshape.26.x_ref = f32[64,1,1536]{2,1,0:T(1,128)} reshape(f32[64,6,256]{2,1,0:T(8,128)S(1)} %gather_fusion) | data formatting | bytes 786432 | tf_op jit(solution)/shard_map/reshape | solution.py:87
  33.2 24.9 %shard_map.65 = f32[6,256]{1,0:T(8,128)} custom-call(f32[64,1,1536]{2,1,0:T(1,128)} %reshape.26.x_ref), custom_call_target="tpu_custom_call" | custom-call | tf_op jit(solution)/shard_map/pallas_call | solution.py:152
  58.1 1.3 %copy.12 = f32[6,256]{1,0:T(8,128)} copy(f32[6,256]{1,0:T(8,128)} %shard_map.65) | data formatting | bytes 12288
  (4 shorter events, 0.0 us)
Async XLA Ops:
  0.0 3.2 %collective-permute-start = (f32[3,256]{1,0:T(4,128)}, f32[3,256]{1,0:T(4,128)S(1)}, u32[]{:S(2)}, u32[]{:S(2)}) collective-permute-start(f32[3,256]{1,0:T(4,128)} %param.8), channel_id=1, source_target_pairs={{0,192},{64,128},{128,64},{192,0},{1,193},{65,129},{129,65},{193,1... | collective-permute-start | bytes 9224 | tf_op jit(solution)/shard_map/ppermute | solution.py:49
  0.9 3.8 %collective-permute-start.1 = (f32[3,256]{1,0:T(4,128)}, f32[3,256]{1,0:T(4,128)S(1)}, u32[]{:S(2)}, u32[]{:S(2)}) collective-permute-start(f32[3,256]{1,0:T(4,128)} %param.8), channel_id=1, source_target_pairs={{0,128},{64,192},{128,0},{192,64},{1,129},{65,193},{129,1},{193,65... | collective-permute-start | bytes 9224 | tf_op jit(solution)/shard_map/ppermute | solution.py:49
  1.5 3.3 %collective-permute-start.2 = (f32[3,256]{1,0:T(4,128)}, f32[3,256]{1,0:T(4,128)S(1)}, u32[]{:S(2)}, u32[]{:S(2)}) collective-permute-start(f32[3,256]{1,0:T(4,128)} %param.8), channel_id=1, source_target_pairs={{0,64},{64,0},{128,192},{192,128},{1,65},{65,1},{129,193},{193,129... | collective-permute-start | bytes 9224 | tf_op jit(solution)/shard_map/ppermute | solution.py:49
  16.2 3.7 %copy-start = (f32[4,384,256]{2,1,0:T(8,128)S(1)}, f32[4,384,256]{2,1,0:T(8,128)}, u32[]{:S(2)}) copy-start(f32[4,384,256]{2,1,0:T(8,128)} %shard_map.64) | copy-start | bytes 4718596
  17.5 3.2 %copy-start.1 = (s32[64]{0:T(128)S(1)}, s32[64]{0:T(128)}, u32[]{:S(2)}) copy-start(s32[64]{0:T(128)} %param.11) | copy-start | bytes 772
  17.5 2.4 %collective-permute-start.3 = (f32[2,384,256]{2,1,0:T(8,128)S(1)}, f32[2,384,256]{2,1,0:T(8,128)S(1)}, u32[]{:S(2)}, u32[]{:S(2)}) collective-permute-start(f32[2,384,256]{2,1,0:T(8,128)S(1)} %slice.21), channel_id=1, source_target_pairs={{0,64},{64,0},{128,192},{192,128},{1,65},{65,1},{129,193},{193,129... | collective-permute-start | bytes 2359304 | tf_op jit(solution)/shard_map/ppermute | solution.py:80
  20.0 11.2 %collective-permute-start.4 = (f32[384,256]{1,0:T(8,128)S(1)}, f32[384,256]{1,0:T(8,128)S(1)}, u32[]{:S(2)}, u32[]{:S(2)}) collective-permute-start(f32[384,256]{1,0:T(8,128)S(1)} %slice_bitcast_fusion), channel_id=1, source_target_pairs={{0,128},{64,192},{128,0},{192,64},{1,129},{65,193},{129,1},{193,65... | collective-permute-start | bytes 1179656 | tf_op jit(solution)/shard_map/ppermute | solution.py:80

commit v22 on v20

--- a/solution.py
+++ b/solution.py
@@ -92,8 +92,11 @@
     count = x_ref.shape[0]
     me = lax.axis_index("pan")
 
+    def offset(d):
+        return (d % 2 * 2 - 1) * ((d + 1) // 2)
+
     def send(d, carry):
-        target = lax.rem(me + d, count)
+        target = lax.rem(me + offset(d) + count, count)
         pltpu.make_async_remote_copy(
             src_ref=x_ref.at[target],
             dst_ref=slots.at[me],
@@ -116,7 +119,7 @@
     total = x_ref[me]
 
     def gather(d, total):
-        source = lax.rem(me + count - d, count)
+        source = lax.rem(me + count - offset(d), count)
         pltpu.make_async_remote_copy(
             src_ref=x_ref.at[source],
             dst_ref=slots.at[source],

time: 59.9 us -> 60.1 us (level); the launches traced: 59.4 us -> 59 us
  no operation moved by 1% of the time
where the time goes in v22:
time: 60.1 us; the launch traced here: 59 us
  Pallas kernels  34.6 us (58%)
  waiting for transfers between devices  12.4 us (21%)
  local copies, waits for them, and re-layouts  5.06 us (8%)
  other arithmetic  4.21 us (7%)
  starting transfers between devices  2.64 us (4%)
    pallas_call x1, Pallas kernels, exchange_sum(): pl.pallas_call(exchange_kernel, out_shape=jax.ShapeDtypeStruct(data.shape...  24.4 us
    ppermute x2, waiting for transfers between devices, per_device(): halves = halves[0] + lax.ppermute(halves[1], 'obs', pairs)  10.8 us
    pallas_call x1, Pallas kernels, per_device(): pl.pallas_call(kernel, grid_spec=grid_spec, out_shape=jax.ShapeDtypeStruc...  10.1 us
    sort x1, other arithmetic, per_device(): inverse = jnp.argsort(segment_owner)  2.03 us
    ppermute x3, starting transfers between devices, per_device(): lax.ppermute(observer_places, 'obs', [(p, p ^ k) for p in range(obs_count)])  1.86 us
    ppermute x3, waiting for transfers between devices, per_device(): lax.ppermute(observer_places, 'obs', [(p, p ^ k) for p in range(obs_count)])  1.6 us
    slice x1, local copies, waits for them, and re-layouts, per_device(): halves = halves[0] + lax.ppermute(halves[1], 'obs', pairs)  1.3 us
    unnamed x5, local copies, waits for them, and re-layouts  1.3 us
  transfers between devices with their start and end apart: 5, of which 4 were waited for; matrix products, arithmetic and copies ran while one was open for 6% of the time, Pallas kernels for 0%

profile of v22, /device:TPU:24, one launch (start us, length us, event | category | flops | bytes accessed | tf_op | source)
XLA Modules:
  0.0 59.0 jit_solution(7345158313794513844)
XLA Ops:
  0.0 0.9 %collective-permute-start = (f32[3,256]{1,0:T(4,128)}, f32[3,256]{1,0:T(4,128)S(1)}, u32[]{:S(2)}, u32[]{:S(2)}) collective-permute-start(f32[3,256]{1,0:T(4,128)} %param.8), channel_id=1, source_target_pairs={{0,192},{64,128},{128,64},{192,0},{1,193},{65,129},{129,65},{193,1... | collective-permute-start | bytes 9224 | tf_op jit(solution)/shard_map/ppermute | solution.py:49
  0.9 0.6 collective-permute-start.1
  1.5 0.4 collective-permute-start.2
  1.9 1.3 %copy.10 = f32[1,3,512]{2,1,0:T(4,128)} copy(f32[1,3,512]{2,0,1:T(1,128)} %param.7) | data formatting | bytes 12288
  3.2 0.1 collective-permute-done
  3.2 1.5 %collective-permute-done.1 = f32[3,256]{1,0:T(4,128)S(1)} collective-permute-done((f32[3,256]{1,0:T(4,128)}, f32[3,256]{1,0:T(4,128)S(1)}, u32[]{:S(2)}, u32[]{:S(2)}) %collective-permute-start.1) | collective-permute-done | bytes 3104 | tf_op jit(solution)/shard_map/ppermute | solution.py:49
  4.8 0.0 collective-permute-done.2
  4.8 0.7 %select_select_fusion.3 = (f32[3,256]{1,0:T(4,128)S(1)}, f32[3,256]{1,0:T(4,128)S(1)}, f32[3,256]{1,0:T(4,128)S(1)}, f32[3,256]{1,0:T(4,128)S(1)}) fusion(f32[3,256]{1,0:T(4,128)S(1)} %collective-permute-done, f32[3,256]{1,0:T(4,128)S(1)} %collective-permute-done.1, f32[3,256]{1,0:T(4,128)S(1)} %collective-permute-done.2, f32[3,256]{1,0:T(4,128)} %param.8, ...), kind=kLoop, calls=%fused_computation.11 | loop fusion | flops 9216 | bytes 24588 | tf_op jit(solution)/shard_map/jit(_where)/select_n | solution.py:55
  5.5 0.6 %pad_maximum_fusion.obs_ref = f32[3,1024]{1,0:T(4,128)} fusion(f32[3,256]{1,0:T(4,128)S(1)} %get-tuple-element.8, f32[3,256]{1,0:T(4,128)S(1)} %get-tuple-element.9, f32[3,256]{1,0:T(4,128)S(1)} %get-tuple-element.10, f32[3,256]{1,0:T(4,128)S(1)} %get-tuple-element.7), kind=kLoop, calls=%fused_computation.5 | loop fusion | flops 9216 | bytes 24576 | tf_op jit(solution)/shard_map/concatenate | solution.py:57
  6.1 10.1 %shard_map.64 = f32[4,384,256]{2,1,0:T(8,128)} custom-call(s32[1,4,8]{2,1,0:T(4,128)} %bitcast.16, s32[1]{0:T(128)} %bitcast.1.me_ref, f32[3,1024]{1,0:T(4,128)} %pad_maximum_fusion.obs_ref, f32[3,512]{1,0:T(4,128)} %bitcast.15, bf16[1024,512]{1,0:T(8,128)(2,1)} %bitcast.13, bf16[4,512,256]{2,1,0:T(8,128)(2,1)} %bitcast.14), custom_call_target="tpu_custom_call" | custom-call | tf_op jit(solution)/shard_map/pallas_call | solution.py:72
  16.2 0.0 copy-start
  16.2 1.3 %slice.21 = f32[2,384,256]{2,1,0:T(8,128)S(1)} slice(f32[4,384,256]{2,1,0:T(8,128)} %shard_map.64), slice={[2:4], [0:384], [0:256]} | slice | bytes 1572864 | tf_op jit(solution)/shard_map/slice | solution.py:80
  17.5 0.0 copy-start.1
  17.5 0.1 collective-permute-start.3
  17.6 2.3 %collective-permute-done.3 = f32[2,384,256]{2,1,0:T(8,128)S(1)} collective-permute-done((f32[2,384,256]{2,1,0:T(8,128)S(1)}, f32[2,384,256]{2,1,0:T(8,128)S(1)}, u32[]{:S(2)}, u32[]{:S(2)}) %collective-permute-start.3) | collective-permute-done | bytes 786464 | tf_op jit(solution)/shard_map/ppermute | solution.py:80
  19.9 0.0 copy-done
  19.9 0.1 slice_add_fusion
  20.0 0.7 %collective-permute-start.4 = (f32[384,256]{1,0:T(8,128)S(1)}, f32[384,256]{1,0:T(8,128)S(1)}, u32[]{:S(2)}, u32[]{:S(2)}) collective-permute-start(f32[384,256]{1,0:T(8,128)S(1)} %slice_bitcast_fusion), channel_id=1, source_target_pairs={{0,128},{64,192},{128,0},{192,64},{1,129},{65,193},{129,1},{193,65... | collective-permute-start | bytes 1179656 | tf_op jit(solution)/shard_map/ppermute | solution.py:80
  20.7 0.0 copy-done.1
  20.7 2.0 %sort.17 = (s32[64]{0:T(128)}, s32[64]{0:T(128)S(1)}) sort(s32[64]{0:T(128)S(1)} %copy-done.1, s32[64]{0:T(128)S(1)} %iota.4), dimensions={0}, to_apply=%region_0.1 | sort | flops 384 | bytes 1024 | tf_op jit(solution)/shard_map/jit(argsort)/sort | solution.py:85
  22.8 8.5 %collective-permute-done.4 = f32[384,256]{1,0:T(8,128)S(1)} collective-permute-done((f32[384,256]{1,0:T(8,128)S(1)}, f32[384,256]{1,0:T(8,128)S(1)}, u32[]{:S(2)}, u32[]{:S(2)}) %collective-permute-start.4) | collective-permute-done | bytes 393248 | tf_op jit(solution)/shard_map/ppermute | solution.py:80
  31.3 0.1 fusion
  31.3 0.1 reshape.18
  31.4 0.6 %gather_fusion = f32[64,6,256]{2,1,0:T(8,128)S(1)} fusion(f32[64,6,256]{2,1,0:T(8,128)S(1)} %reshape.18, s32[1024]{0:T(1024)S(1)} %pad_clamp_fusion), kind=kCustom, calls=%fused_computation | custom fusion | bytes 786688 | tf_op jit(solution)/shard_map/gather | solution.py:86
  32.0 1.1 %reshape.30.x_ref = f32[64,1,1536]{2,1,0:T(1,128)} reshape(f32[64,6,256]{2,1,0:T(8,128)S(1)} %gather_fusion) | data formatting | bytes 786432 | tf_op jit(solution)/shard_map/reshape | solution.py:87
  33.2 24.4 %shard_map.65 = f32[1,1536]{1,0:T(1,128)} custom-call(f32[64,1,1536]{2,1,0:T(1,128)} %reshape.30.x_ref), custom_call_target="tpu_custom_call" | custom-call | tf_op jit(solution)/shard_map/pallas_call | solution.py:153
  57.6 0.7 %reduce = f32[1536]{0:T(1024)S(1)} reduce(f32[1,1536]{1,0:T(1,128)} %shard_map.65, f32[]{:T(128)} %constant.21), dimensions={0}, to_apply=%pallas_call.7.reduce_sub_computation | reduce | bytes 12292 | tf_op jit(solution)/shard_map/pallas_call | solution.py:153
  58.4 0.6 %reshape.20 = f32[6,256]{1,0:T(8,128)} reshape(f32[1536]{0:T(1024)S(1)} %reduce) | data formatting | bytes 12288 | tf_op jit(solution)/shard_map/reshape | solution.py:88
  (4 shorter events, 0.0 us)
Async XLA Ops:
  0.0 3.2 %collective-permute-start = (f32[3,256]{1,0:T(4,128)}, f32[3,256]{1,0:T(4,128)S(1)}, u32[]{:S(2)}, u32[]{:S(2)}) collective-permute-start(f32[3,256]{1,0:T(4,128)} %param.8), channel_id=1, source_target_pairs={{0,192},{64,128},{128,64},{192,0},{1,193},{65,129},{129,65},{193,1... | collective-permute-start | bytes 9224 | tf_op jit(solution)/shard_map/ppermute | solution.py:49
  0.9 3.8 %collective-permute-start.1 = (f32[3,256]{1,0:T(4,128)}, f32[3,256]{1,0:T(4,128)S(1)}, u32[]{:S(2)}, u32[]{:S(2)}) collective-permute-start(f32[3,256]{1,0:T(4,128)} %param.8), channel_id=1, source_target_pairs={{0,128},{64,192},{128,0},{192,64},{1,129},{65,193},{129,1},{193,65... | collective-permute-start | bytes 9224 | tf_op jit(solution)/shard_map/ppermute | solution.py:49
  1.5 3.3 %collective-permute-start.2 = (f32[3,256]{1,0:T(4,128)}, f32[3,256]{1,0:T(4,128)S(1)}, u32[]{:S(2)}, u32[]{:S(2)}) collective-permute-start(f32[3,256]{1,0:T(4,128)} %param.8), channel_id=1, source_target_pairs={{0,64},{64,0},{128,192},{192,128},{1,65},{65,1},{129,193},{193,129... | collective-permute-start | bytes 9224 | tf_op jit(solution)/shard_map/ppermute | solution.py:49
  16.2 3.7 %copy-start = (f32[4,384,256]{2,1,0:T(8,128)S(1)}, f32[4,384,256]{2,1,0:T(8,128)}, u32[]{:S(2)}) copy-start(f32[4,384,256]{2,1,0:T(8,128)} %shard_map.64) | copy-start | bytes 4718596
  17.5 3.2 %copy-start.1 = (s32[64]{0:T(128)S(1)}, s32[64]{0:T(128)}, u32[]{:S(2)}) copy-start(s32[64]{0:T(128)} %param.11) | copy-start | bytes 772
  17.5 2.4 %collective-permute-start.3 = (f32[2,384,256]{2,1,0:T(8,128)S(1)}, f32[2,384,256]{2,1,0:T(8,128)S(1)}, u32[]{:S(2)}, u32[]{:S(2)}) collective-permute-start(f32[2,384,256]{2,1,0:T(8,128)S(1)} %slice.21), channel_id=1, source_target_pairs={{0,64},{64,0},{128,192},{192,128},{1,65},{65,1},{129,193},{193,129... | collective-permute-start | bytes 2359304 | tf_op jit(solution)/shard_map/ppermute | solution.py:80
  20.0 11.2 %collective-permute-start.4 = (f32[384,256]{1,0:T(8,128)S(1)}, f32[384,256]{1,0:T(8,128)S(1)}, u32[]{:S(2)}, u32[]{:S(2)}) collective-permute-start(f32[384,256]{1,0:T(8,128)S(1)} %slice_bitcast_fusion), channel_id=1, source_target_pairs={{0,128},{64,192},{128,0},{192,64},{1,129},{65,193},{129,1},{193,65... | collective-permute-start | bytes 1179656 | tf_op jit(solution)/shard_map/ppermute | solution.py:80
